TPU v7x, 32 devices: a whole 2x2x4 slice. The times are simulated.
32 devices in a mesh: tm: 2 (over y), rows: 4 (over z), dp: 4 (over x, core).
Axes of the slice: x: 2, y: 2, z: 4, core: 2. Of those that a mesh axis runs over, the one named last changes fastest.
Arguments:
- video: bfloat16 [4, 32, 16, 32, 128], P('dp', 'tm', 'rows'), may hold values from -6 to 6
- cotangent: bfloat16 [4, 32, 16, 32, 128], P('dp', 'tm', 'rows'), may hold values from -6 to 6
- in_kernel: bfloat16 [3, 3, 128, 128], replicated, may hold values from -0.03125 to 0.03125
- out_kernel: bfloat16 [3, 3, 128, 128], replicated, may hold values from -0.1875 to 0.1875
- skip_gain: float32 [128], replicated, may hold values from 0.5 to 1.5
- log_decay: float32 [32, 128], P('tm'), may hold values from -3 to 0, as said below
Outputs:
- layer_out: bfloat16 [4, 32, 16, 32, 128], P('dp', 'tm', 'rows')
- video_grad: bfloat16 [4, 32, 16, 32, 128], P('dp', 'tm', 'rows')
- in_kernel_grad: float32 [3, 3, 128, 128], replicated
- out_kernel_grad: float32 [3, 3, 128, 128], replicated
- skip_gain_grad: float32 [128], replicated
- decay_grad: float32 [32, 128], P('tm')
Inputs may be any that keep to these rules, and one draw needn't show every extreme that they name: log_decay is negative.
All inputs are finite; a program needn't handle non-finite values.
Results may differ from a plain program's by a relative error of at most 0.0085.
Values may be sent and summed in bfloat16 or wider, within the bound.
No kernel may reach another device: no remote copies, remote signals or barrier semaphores. Data moves between devices by JAX's collectives and lax.ppermute only.
A program may use at most 64 MiB of HBM per device.

v0:
```python
import math

import jax
import jax.numpy as jnp
from jax import lax
from jax.sharding import PartitionSpec as P


def padded_2(cells, sides, width):
    for axis, dim in sides:
        count = lax.axis_size(axis)
        ends = count - 1
        head = lax.slice_in_dim(cells, 0, width, axis=dim)
        tail = lax.slice_in_dim(cells, cells.shape[dim] - width, cells.shape[dim], axis=dim)
        cells = jnp.concatenate(
            [
                lax.ppermute(tail, axis, [(i, (i + 1) % count) for i in range(ends)]),
                cells,
                lax.ppermute(head, axis, [((i + 1) % count, i) for i in range(ends)]),
            ],
            axis=dim,
        )
    return cells


def pad_columns(field):
    return jnp.pad(field, ((0, 0), (0, 0), (0, 0), (1, 1), (0, 0)))


def forward_conv(padded, kernel):
    seqs, frames, rows_two, cols_two, chans = padded.shape
    rows, cols = (rows_two - 2, cols_two - 2)
    total = None
    for i in range(3):
        for j in range(3):
            piece = padded[:, :, i : i + rows, j : j + cols, :].reshape(-1, chans)
            term = jnp.dot(piece, kernel[i, j], preferred_element_type=jnp.float32)
            total = term if total is None else total + term
    return total.reshape(seqs, frames, rows, cols, kernel.shape[3])


def adjoint_conv(padded, kernel):
    seqs, frames, rows_two, cols_two, chans = padded.shape
    rows, cols = (rows_two - 2, cols_two - 2)
    total = None
    for i in range(3):
        for j in range(3):
            piece = padded[:, :, 2 - i : 2 - i + rows, 2 - j : 2 - j + cols, :].reshape(-1, chans)
            term = lax.dot_general(
                piece, kernel[i, j], (((1,), (1,)), ((), ())), preferred_element_type=jnp.float32
            )
            total = term if total is None else total + term
    return total.reshape(seqs, frames, rows, cols, kernel.shape[2])


def kernel_grad(padded, grad):
    seqs, frames, rows_two, cols_two, chans = padded.shape
    rows, cols = (rows_two - 2, cols_two - 2)
    flat_grad = grad.reshape(-1, grad.shape[-1])
    outer_list = []
    for i in range(3):
        inner_list = []
        for j in range(3):
            piece = padded[:, :, i : i + rows, j : j + cols, :].reshape(-1, chans)
            inner_list.append(
                lax.dot_general(
                    piece, flat_grad, (((0,), (0,)), ((), ())), preferred_element_type=jnp.float32
                )
            )
        outer_list.append(jnp.stack(inner_list))
    return jnp.stack(outer_list)


def on_device(video, cotangent, in_kernel, out_kernel, skip_gain, log_decay):
    seqs, frames, rows, cols, chans = video.shape
    padded_x = pad_columns(padded_2(video, (("rows", 2),), 1))
    drive = forward_conv(padded_x, in_kernel)
    cum = jnp.cumsum(log_decay, axis=0)
    later_mask = (
        lax.broadcasted_iota(jnp.int32, (frames, frames), 0)
        >= lax.broadcasted_iota(jnp.int32, (frames, frames), 1)
    )[:, :, None]
    gaps = cum[:, None, :] - cum[None, :, :]
    within = jnp.where(later_mask, jnp.exp(jnp.where(later_mask, gaps, 0.0)), 0.0)
    local_states = jnp.einsum("tkp,skrcp->strcp", within, drive, precision=lax.Precision.HIGHEST)
    group_total = cum[-1]
    empty = jnp.zeros_like(local_states[:, -1])
    group_logs = lax.all_gather(group_total[None, :], "tm", axis=0, tiled=True)
    running = jnp.cumsum(group_logs, axis=0)
    own = lax.axis_index("tm")
    own_running = lax.dynamic_index_in_dim(running, own, 0, keepdims=False)
    piece = lax.all_gather(
        local_states[:, -1][None].astype(jnp.bfloat16), "tm", axis=0, tiled=True
    ).astype(jnp.float32)
    count = piece.shape[0]
    upto = running
    index = jnp.arange(count, dtype=jnp.int32)
    reach = own_running[None, :] - group_total[None, :] - upto
    weight = jnp.where((index < own)[:, None], jnp.exp(jnp.minimum(reach, 0.0)), 0.0)
    carry_in = empty + jnp.einsum("np,nsrcp->srcp", weight, piece, precision=lax.Precision.HIGHEST)
    states = local_states + jnp.exp(cum)[None, :, None, None, :] * carry_in[:, None]
    states_bf = states.astype(jnp.bfloat16)
    padded_s = pad_columns(padded_2(states_bf, (("rows", 2),), 1))
    pre = forward_conv(padded_s, out_kernel) + skip_gain * video.astype(jnp.float32)
    activated, pullback = jax.vjp(jax.nn.gelu, pre)
    grad_pre = pullback(cotangent.astype(jnp.float32))[0]
    grad_bf = grad_pre.astype(jnp.bfloat16)
    out_grad = kernel_grad(padded_s, grad_bf)
    gain_grad = jnp.sum(grad_pre * video.astype(jnp.float32), axis=(0, 1, 2, 3))
    padded_g = pad_columns(padded_2(grad_bf, (("rows", 2),), 1))
    state_grad = adjoint_conv(padded_g, out_kernel)
    local_adjoint = jnp.einsum(
        "tkp,strcp->skrcp", within, state_grad, precision=lax.Precision.HIGHEST
    )
    leading = jnp.exp(cum[0])[None, None, None, :] * local_adjoint[:, 0]
    piece = lax.all_gather(leading[None].astype(jnp.bfloat16), "tm", axis=0, tiled=True).astype(
        jnp.float32
    )
    count = piece.shape[0]
    upto = running
    index = jnp.arange(count, dtype=jnp.int32)
    reach = upto - group_logs - own_running[None, :]
    weight = jnp.where((index > own)[:, None], jnp.exp(jnp.minimum(reach, 0.0)), 0.0)
    back_in = empty + jnp.einsum("np,nsrcp->srcp", weight, piece, precision=lax.Precision.HIGHEST)
    adjoint = (
        local_adjoint
        + jnp.exp(group_total[None, :] - cum)[None, :, None, None, :] * back_in[:, None]
    )
    previous = jnp.concatenate([carry_in[:, None], states[:, :-1]], axis=1)
    decay_part = jnp.sum(
        adjoint * jnp.exp(log_decay)[None, :, None, None, :] * previous, axis=(0, 2, 3)
    )
    decay_scale = 1.0 / math.sqrt(seqs * rows * cols * lax.axis_size("rows") * lax.axis_size("dp"))
    decay_grad = lax.psum(decay_part, ("rows", "dp")) * decay_scale
    adjoint_bf = adjoint.astype(jnp.bfloat16)
    in_grad = kernel_grad(padded_x, adjoint_bf)
    padded_a = pad_columns(padded_2(adjoint_bf, (("rows", 2),), 1))
    video_grad = (adjoint_conv(padded_a, in_kernel) + skip_gain * grad_pre).astype(jnp.bfloat16)
    in_sum, out_sum, gain_sum = lax.psum((in_grad, out_grad, gain_grad), ("tm", "rows", "dp"))
    weight_scale = 1.0 / math.sqrt(
        seqs
        * frames
        * rows
        * cols
        * lax.axis_size("tm")
        * lax.axis_size("rows")
        * lax.axis_size("dp")
    )
    return (
        activated.astype(jnp.bfloat16),
        video_grad,
        in_sum * weight_scale,
        out_sum * weight_scale,
        gain_sum * weight_scale,
        decay_grad,
    )


def solution(mesh):
    placed = (
        P("dp", "tm", "rows", None, None),
        P("dp", "tm", "rows", None, None),
        P(),
        P(),
        P(),
        P("tm", None),
    )
    return jax.shard_map(
        on_device,
        mesh=mesh,
        in_specs=placed,
        out_specs=(
            P("dp", "tm", "rows", None, None),
            P("dp", "tm", "rows", None, None),
            P(),
            P(),
            P(),
            P("tm", None),
        ),
        check_vma=False,
    )
```

profile of v0, /device:TPU:0, one launch (start us, length us, event | category | flops | bytes accessed | tf_op | source)
XLA Modules:
  0.0 367.8 jit_solution(14901978521855251328)
XLA Ops:
  7.2 1.0 fusion.177
  8.2 5.0 %collective-permute-start = (bf16[1,16,1,32,128]{4,3,2,1,0:T(8,128)(2,1)S(1)}, bf16[1,16,1,32,128]{4,3,2,1,0:T(8,128)(2,1)S(1)}, u32[]{:S(2)}, u32[]{:S(2)}) collective-permute-start(bf16[1,16,1,32,128]{4,3,2,1,0:T(8,128)(2,1)S(1)} %get-tuple-element.71), channel_id=1, source_target_pairs={{0,4},{4,8},{8,12},{1,5},{5,9},{9,13},{2,6},{6,10},{10,14},{3,7},{... | collective-permute-start | bytes 393224 | tf_op jit(solution)/shard_map/ppermute | solution.py:17
  13.2 1.3 collective-permute-start.1
  15.2 4.2 %all-gather = f32[2,1,128]{2,1,0:T(1,128)S(1)} all-gather(f32[1,1,128]{2,1,0:T(1,128)S(1)} %slice_bitcast_fusion.1), channel_id=1, replica_groups=mesh['tm'=2,'rows'=4,'dp'=4] {'tm'}, dimensions={0}, use_global_device_ids=true | all-gather | bytes 1536 | tf_op jit(solution)/shard_map/all_gather | solution.py:88
  20.0 1.6 fusion.25
  25.6 4.5 %copy.169 = f32[16,4,32,128]{2,0,1,3:T(8,128)} copy(f32[16,4,32,128]{3,2,1,0:T(8,128)S(1)} %bitcast.443) | data formatting | bytes 2097152 | tf_op jit(solution)/shard_map/reshape
  30.1 8.3 %fusion.19 = f32[128,4,32,16]{2,3,1,0:T(8,128)} fusion(f32[16,4,32,128]{2,0,1,3:T(8,128)} %copy.169, f32[16,128]{0,1:T(8,128)S(1)} %copy.167, pred[16,16]{0,1:T(8,128)(4,1)S(1)} %iota_compare_fusion.2), kind=kOutput, calls=%fused_computation.74 | convolution fusion | flops 50429952 | bytes 2105600 | tf_op jit(solution)/shard_map/tkp,skrcp->strcp/dot_general | solution.py:85
  38.4 3.7 %copy.171 = f32[128,4,32,16]{0,2,1,3:T(8,128)S(1)} copy(f32[128,4,32,16]{2,3,1,0:T(8,128)} %fusion.19) | data formatting | bytes 2097152 | tf_op jit(solution)/shard_map/tkp,skrcp->strcp/dot_general | solution.py:85
  42.1 4.6 %all_gather.9 = bf16[2,1,4,32,128]{4,3,2,1,0:T(8,128)(2,1)S(1)} all-gather(bf16[1,1,4,32,128]{4,3,2,1,0:T(8,128)(2,1)S(1)} %slice.550), channel_id=1, replica_groups=mesh['tm'=2,'rows'=4,'dp'=4] {'tm'}, dimensions={0}, use_global_device_ids=true | all-gather | bytes 98304 | tf_op jit(solution)/shard_map/all_gather | solution.py:92
  47.0 4.2 %collective-permute-start.2 = (bf16[1,16,1,32,128]{4,3,2,1,0:T(8,128)(2,1)S(1)}, bf16[1,16,1,32,128]{4,3,2,1,0:T(8,128)(2,1)S(1)}, u32[]{:S(2)}, u32[]{:S(2)}) collective-permute-start(bf16[1,16,1,32,128]{4,3,2,1,0:T(8,128)(2,1)S(1)} %get-tuple-element.67), channel_id=1, source_target_pairs={{0,4},{4,8},{8,12},{1,5},{5,9},{9,13},{2,6},{6,10},{10,14},{3,7},{... | collective-permute-start | bytes 393224 | tf_op jit(solution)/shard_map/ppermute | solution.py:17
  51.2 1.5 collective-permute-start.3
  52.7 1.1 slice.347
  53.9 4.2 %collective-permute-done.3 = bf16[1,16,1,32,128]{4,3,2,1,0:T(8,128)(2,1)S(1)} collective-permute-done((bf16[1,16,1,32,128]{4,3,2,1,0:T(8,128)(2,1)S(1)}, bf16[1,16,1,32,128]{4,3,2,1,0:T(8,128)(2,1)S(1)}, u32[]{:S(2)}, u32[]{:S(2)}) %collective-permute-start.3) | collective-permute-done | bytes 131104 | tf_op jit(solution)/shard_map/ppermute | solution.py:19
  62.9 1.8 fusion.6
  74.2 40.4 %psum.30 = f32[128]{0:T(128)S(1)} all-reduce(f32[128]{0:T(128)S(1)} %get-tuple-element.26), channel_id=1, replica_groups=mesh['tm'=2,'rows'=4,'dp'=4] {'tm','rows','dp'}, use_global_device_ids=true, to_apply=%region_5.6 | all-reduce | flops 128 | bytes 1024 | tf_op jit(solution)/shard_map/psum | solution.py:139
  115.1 2.2 collective-permute-start.4
  117.3 1.5 collective-permute-start.5
  122.4 1.9 collective-permute-done.5
  127.9 1.3 fusion.1
  129.2 5.4 %copy.172 = f32[16,4,32,128]{2,0,1,3:T(8,128)} copy(f32[16,4,32,128]{3,2,1,0:T(8,128)} %bitcast.442) | data formatting | bytes 2097152 | tf_op jit(solution)/shard_map/reshape.7
  134.6 8.1 %fusion.17 = f32[128,4,32,16]{2,3,1,0:T(8,128)} fusion(f32[16,4,32,128]{2,0,1,3:T(8,128)} %copy.172, f32[16,128]{0,1:T(8,128)S(1)} %copy.167, pred[16,16]{0,1:T(8,128)(4,1)S(1)} %iota_compare_fusion.2), kind=kOutput, calls=%fused_computation.72 | convolution fusion | flops 50429952 | bytes 2105600 | tf_op jit(solution)/shard_map/tkp,strcp->skrcp/dot_general | solution.py:112
  142.8 4.5 %copy.173 = f32[128,4,32,16]{0,2,1,3:T(8,128)} copy(f32[128,4,32,16]{2,3,1,0:T(8,128)} %fusion.17) | data formatting | bytes 2097152 | tf_op jit(solution)/shard_map/tkp,strcp->skrcp/dot_general | solution.py:112
  148.2 5.1 %all_gather.11 = bf16[2,1,4,32,128]{4,3,2,1,0:T(8,128)(2,1)S(1)} all-gather(bf16[1,1,4,32,128]{4,3,2,1,0:T(8,128)(2,1)S(1)} %fusion.71), channel_id=1, replica_groups=mesh['tm'=2,'rows'=4,'dp'=4] {'tm'}, dimensions={0}, use_global_device_ids=true | all-gather | bytes 98304 | tf_op jit(solution)/shard_map/all_gather | solution.py:116
  153.3 1.9 fusion.16
  161.6 57.8 %psum.31 = f32[16,128]{0,1:T(8,128)S(1)} all-reduce(f32[16,128]{0,1:T(8,128)S(1)} %copy.212), channel_id=1, replica_groups=mesh['tm'=2,'rows'=4,'dp'=4] {'rows','dp'}, use_global_device_ids=true, to_apply=%region_7.8 | all-reduce | flops 2048 | bytes 16384 | tf_op jit(solution)/shard_map/psum | solution.py:134
  219.4 1.3 collective-permute-start.6
  220.7 1.3 collective-permute-start.7
  225.4 2.2 collective-permute-done.7
  231.8 1.0 add_convert_fusion
  232.8 124.3 %all-reduce.7.cloned.1.call-done = (f32[3,3,128,128]{3,2,1,0:T(8,128)}, f32[3,3,128,128]{3,2,1,0:T(8,128)}) async-done(((f32[3,3,128,128]{3,2,1,0:T(8,128)}, f32[3,3,128,128]{3,2,1,0:T(8,128)}), (f32[3,3,128,128]{3,2,1,0:T(8,128)}, f32[3,3,128,128]{3,2,1,0:T(8,128)})) %all-reduce.7.cloned.1.call-update) | async-done | bytes 1179664 | tf_op jit(solution)/shard_map/psum | solution.py:139
  357.2 1.9 broadcast_multiply_fusion.1
  359.1 1.9 broadcast_multiply_fusion
  (126 shorter events, 42.2 us)
Async XLA Ops:
  7.2 350.0 %all-reduce.7.cloned.1.call-start = ((), (), s32[]{:S(2)}) async-start(), calls=%async_computation | async-start | bytes 2359296 | tf_op jit(solution)/shard_map/psum | solution.py:139
  8.2 11.5 %collective-permute-start = (bf16[1,16,1,32,128]{4,3,2,1,0:T(8,128)(2,1)S(1)}, bf16[1,16,1,32,128]{4,3,2,1,0:T(8,128)(2,1)S(1)}, u32[]{:S(2)}, u32[]{:S(2)}) collective-permute-start(bf16[1,16,1,32,128]{4,3,2,1,0:T(8,128)(2,1)S(1)} %get-tuple-element.71), channel_id=1, source_target_pairs={{0,4},{4,8},{8,12},{1,5},{5,9},{9,13},{2,6},{6,10},{10,14},{3,7},{... | collective-permute-start | bytes 393224 | tf_op jit(solution)/shard_map/ppermute | solution.py:17
  13.2 6.9 %collective-permute-start.1 = (bf16[1,16,1,32,128]{4,3,2,1,0:T(8,128)(2,1)S(1)}, bf16[1,16,1,32,128]{4,3,2,1,0:T(8,128)(2,1)S(1)}, u32[]{:S(2)}, u32[]{:S(2)}) collective-permute-start(bf16[1,16,1,32,128]{4,3,2,1,0:T(8,128)(2,1)S(1)} %get-tuple-element.72), channel_id=1, source_target_pairs={{4,0},{8,4},{12,8},{5,1},{9,5},{13,9},{6,2},{10,6},{14,10},{7,3},{... | collective-permute-start | bytes 393224 | tf_op jit(solution)/shard_map/ppermute | solution.py:19
  21.7 1.0 copy-start.6
  22.3 1.1 copy-start
  23.4 0.8 copy-start.3
  23.4 1.9 copy-start.1
  42.1 10.6 %copy-start.10 = (f32[16,128]{1,0:T(8,128)S(1)}, f32[16,128]{1,0:T(8,128)}, u32[]{:S(2)}) copy-start(f32[16,128]{1,0:T(8,128)} %param.11) | copy-start | bytes 24580
  47.0 6.9 %collective-permute-start.2 = (bf16[1,16,1,32,128]{4,3,2,1,0:T(8,128)(2,1)S(1)}, bf16[1,16,1,32,128]{4,3,2,1,0:T(8,128)(2,1)S(1)}, u32[]{:S(2)}, u32[]{:S(2)}) collective-permute-start(bf16[1,16,1,32,128]{4,3,2,1,0:T(8,128)(2,1)S(1)} %get-tuple-element.67), channel_id=1, source_target_pairs={{0,4},{4,8},{8,12},{1,5},{5,9},{9,13},{2,6},{6,10},{10,14},{3,7},{... | collective-permute-start | bytes 393224 | tf_op jit(solution)/shard_map/ppermute | solution.py:17
  51.2 6.9 %collective-permute-start.3 = (bf16[1,16,1,32,128]{4,3,2,1,0:T(8,128)(2,1)S(1)}, bf16[1,16,1,32,128]{4,3,2,1,0:T(8,128)(2,1)S(1)}, u32[]{:S(2)}, u32[]{:S(2)}) collective-permute-start(bf16[1,16,1,32,128]{4,3,2,1,0:T(8,128)(2,1)S(1)} %get-tuple-element.68), channel_id=1, source_target_pairs={{4,0},{8,4},{12,8},{5,1},{9,5},{13,9},{6,2},{10,6},{14,10},{7,3},{... | collective-permute-start | bytes 393224 | tf_op jit(solution)/shard_map/ppermute | solution.py:19
  58.6 1.0 copy-start.5
  61.9 1.0 copy-start.8
  61.9 1.0 copy-start.11
  115.1 7.3 %collective-permute-start.4 = (bf16[1,16,1,32,128]{4,3,2,1,0:T(8,128)(2,1)}, bf16[1,16,1,32,128]{4,3,2,1,0:T(8,128)(2,1)S(1)}, u32[]{:S(2)}, u32[]{:S(2)}) collective-permute-start(bf16[1,16,1,32,128]{4,3,2,1,0:T(8,128)(2,1)} %get-tuple-element.63), channel_id=1, source_target_pairs={{0,4},{4,8},{8,12},{1,5},{5,9},{9,13},{2,6},{6,10},{10,14},{3,7},{... | collective-permute-start | bytes 393224 | tf_op jit(solution)/shard_map/ppermute | solution.py:17
  117.3 7.1 %collective-permute-start.5 = (bf16[1,16,1,32,128]{4,3,2,1,0:T(8,128)(2,1)}, bf16[1,16,1,32,128]{4,3,2,1,0:T(8,128)(2,1)S(1)}, u32[]{:S(2)}, u32[]{:S(2)}) collective-permute-start(bf16[1,16,1,32,128]{4,3,2,1,0:T(8,128)(2,1)} %get-tuple-element.64), channel_id=1, source_target_pairs={{4,0},{8,4},{12,8},{5,1},{9,5},{13,9},{6,2},{10,6},{14,10},{7,3},{... | collective-permute-start | bytes 393224 | tf_op jit(solution)/shard_map/ppermute | solution.py:19
  147.3 7.9 %copy-start.2 = (bf16[1,16,4,32,128]{4,3,2,1,0:T(8,128)(2,1)S(1)}, bf16[1,16,4,32,128]{4,3,2,1,0:T(8,128)(2,1)}, u32[]{:S(2)}) copy-start(bf16[1,16,4,32,128]{4,3,2,1,0:T(8,128)(2,1)} %copy-done.1) | copy-start | bytes 1572868
  153.3 2.3 copy-start.4
  160.5 61.5 %copy-start.9 = (f32[1,128,128]{2,1,0:T(8,128)S(1)}, f32[1,128,128]{2,1,0:T(8,128)}, u32[]{:S(2)}) copy-start(f32[1,128,128]{2,1,0:T(8,128)} %convolution_bitcast_fusion.14) | copy-start | bytes 196612
  219.4 6.0 %collective-permute-start.6 = (bf16[1,16,1,32,128]{4,3,2,1,0:T(8,128)(2,1)S(1)}, bf16[1,16,1,32,128]{4,3,2,1,0:T(8,128)(2,1)S(1)}, u32[]{:S(2)}, u32[]{:S(2)}) collective-permute-start(bf16[1,16,1,32,128]{4,3,2,1,0:T(8,128)(2,1)S(1)} %get-tuple-element.59), channel_id=1, source_target_pairs={{0,4},{4,8},{8,12},{1,5},{5,9},{9,13},{2,6},{6,10},{10,14},{3,7},{... | collective-permute-start | bytes 393224 | tf_op jit(solution)/shard_map/ppermute | solution.py:17
  220.7 6.9 %collective-permute-start.7 = (bf16[1,16,1,32,128]{4,3,2,1,0:T(8,128)(2,1)S(1)}, bf16[1,16,1,32,128]{4,3,2,1,0:T(8,128)(2,1)S(1)}, u32[]{:S(2)}, u32[]{:S(2)}) collective-permute-start(bf16[1,16,1,32,128]{4,3,2,1,0:T(8,128)(2,1)S(1)} %get-tuple-element.60), channel_id=1, source_target_pairs={{4,0},{8,4},{12,8},{5,1},{9,5},{13,9},{6,2},{10,6},{14,10},{7,3},{... | collective-permute-start | bytes 393224 | tf_op jit(solution)/shard_map/ppermute | solution.py:19
  228.0 1.0 copy-start.7
Sparse Core Ops, SparseCore 0:
  225.5 131.6 all-reduce.6
where the time goes:
time: 369 us; the launch traced here: 368 us
  waiting for transfers between devices  133 us (36%)
  blocking collectives  112 us (30%)
  matrix products  42.6 us (12%)
  local copies, waits for them, and re-layouts  26.5 us (7%)
  other arithmetic  20.8 us (6%)
  starting transfers between devices  18.3 us (5%)
  between operations  14.6 us (4%)
    psum x1, waiting for transfers between devices, on_device(): lax.psum((in_grad, out_grad, gain_grad), ('tm', 'rows', 'dp'))  124 us
    psum x1, blocking collectives, on_device(): decay_grad = lax.psum(decay_part, ('rows', 'dp')) * decay_scale  57.8 us
    psum x1, blocking collectives, on_device(): lax.psum((in_grad, out_grad, gain_grad), ('tm', 'rows', 'dp'))  40.4 us
    dot_general x18, matrix products, kernel_grad(): lax.dot_general(piece, flat_grad, (((0,), (0,)), ((), ())), preferred_ele...  14.9 us
    ppermute x4, starting transfers between devices, padded_2(): lax.ppermute(tail, axis, [(i, (i + 1) % count) for i in range(ends)])  12.7 us
    ppermute x4, waiting for transfers between devices, padded_2(): lax.ppermute(head, axis, [((i + 1) % count, i) for i in range(ends)])  8.64 us
    dot_general x1, matrix products, on_device(): jnp.einsum('tkp,skrcp->strcp', within, drive, precision=lax.Precision.HIG...  8.27 us
    dot_general x1, matrix products, on_device(): jnp.einsum('tkp,strcp->skrcp', within, state_grad, precision=lax.Precisio...  8.14 us
  transfers between devices with their start and end apart: 9, of which 5 were waited for; matrix products, arithmetic and copies ran while one was open for 4% of the time, Pallas kernels for 0%

commit v1 on v0

v1 whole, which is shorter than its diff:
```python
import functools
import math

import jax
import jax.numpy as jnp
from jax import lax
from jax.experimental import pallas as pl
from jax.experimental.pallas import tpu as pltpu
from jax.sharding import PartitionSpec as P

BF = jnp.bfloat16
F32 = jnp.float32
VMEM_LIMIT = 24 * 1024 * 1024
GELU_A = math.sqrt(2.0 / math.pi)
GELU_B = 0.044715


def vmem():
    return pl.BlockSpec(memory_space=pltpu.VMEM)


def smem():
    return pl.BlockSpec(memory_space=pltpu.SMEM)


def call(body, outs, ins, scalars, scratch=(), flops=0):
    moved = sum(math.prod(a.shape) * a.dtype.itemsize for a in list(ins) + list(outs))
    return pl.pallas_call(
        body,
        out_shape=outs,
        in_specs=[smem() if n < scalars else vmem() for n in range(len(ins))],
        out_specs=[vmem() for _ in outs],
        scratch_shapes=list(scratch),
        compiler_params=pltpu.CompilerParams(vmem_limit_bytes=VMEM_LIMIT),
        cost_estimate=pl.CostEstimate(flops=flops, bytes_accessed=moved, transcendentals=0),
    )(*ins)


def shape(dims, dtype):
    return jax.ShapeDtypeStruct(tuple(dims), dtype)


def columns(count, width, lanes):
    return lax.rem(lax.broadcasted_iota(jnp.int32, (count, lanes), 0), width)


def from_left(field, column):
    return jnp.where(column == 0, 0.0, pltpu.roll(field, 1, 0))


def from_right(field, column, width):
    return jnp.where(column == width - 1, 0.0, pltpu.roll(field, field.shape[0] - 1, 0))


def taps(field, first, rows):
    frames, _, cols, chans = field.shape
    return jnp.concatenate(
        [field[:, first + i : first + i + rows].reshape(frames * rows * cols, chans) for i in range(3)],
        axis=1,
    )


def conv(field, first, rows, weights):
    frames, _, cols, _ = field.shape
    out = weights.shape[1] // 3
    wide = jnp.dot(taps(field, first, rows), weights, preferred_element_type=F32)
    column = columns(wide.shape[0], cols, out)
    return (
        wide[:, out : 2 * out]
        + from_left(wide[:, :out], column)
        + from_right(wide[:, 2 * out :], column, cols)
    )


def spread(grad, cols):
    column = columns(grad.shape[0], cols, grad.shape[1])
    return jnp.concatenate(
        [
            from_right(grad, column, cols).astype(BF),
            grad.astype(BF),
            from_left(grad, column).astype(BF),
        ],
        axis=1,
    )


def outer(left, right):
    return lax.dot_general(left, right, (((0,), (0,)), ((), ())), preferred_element_type=F32)


def group_of(frames, most):
    size = most
    while frames % size:
        size -= 1
    return size


def fill_halo(edge_ref, wide_ref, own_ref, first_ref, second_ref):
    rows, deep = own_ref.shape[1], first_ref.shape[1]
    odd = edge_ref[2] == 1
    wide_ref[:, deep : deep + rows] = own_ref[...]
    wide_ref[:, pl.ds(jnp.where(odd, 0, rows + deep), deep)] = first_ref[...]
    wide_ref[:, pl.ds(jnp.where(odd, rows + deep, 0), deep)] = second_ref[...]


def inside(edge_ref, field, width):
    count = field.shape[0]
    upper = jnp.where(edge_ref[0] == 1, field[:width], 0.0)
    lower = jnp.where(edge_ref[1] == 1, field[count - width :], 0.0)
    return jnp.concatenate([upper, field[width : count - width], lower], axis=0)


def drive_kernel(edge_ref, own_ref, first_ref, second_ref, kernel_ref, lam_ref, wide_ref, local_ref, end_ref):
    frames, rows, cols, _ = own_ref.shape
    state_chans = kernel_ref.shape[1] // 3
    fill_halo(edge_ref, wide_ref, own_ref, first_ref, second_ref)
    group = group_of(frames, 2)
    many = (rows + 2) * cols

    def step(n, state):
        base = n * group
        drive = conv(wide_ref[pl.ds(base, group)], 0, rows + 2, kernel_ref[...])
        for k in range(group):
            now = inside(edge_ref, drive[k * many : (k + 1) * many], cols)
            state = lam_ref[base + k] * state + now
            local_ref[base + k] = state.reshape(rows + 2, cols, state_chans)
        return state

    last = lax.fori_loop(0, frames // group, step, jnp.zeros((many, state_chans), F32))
    end_ref[...] = last.reshape(rows + 2, cols, state_chans).astype(BF)


def layer_kernel(
    local_ref, carry_ref, reach_ref, own_ref, cot_ref, kernel_ref, gain_ref,
    state_ref, act_ref, grad_ref, gain_grad_ref,
):
    frames, rows, cols, chans = own_ref.shape
    group = group_of(frames, 2)
    many = group * rows * cols
    carry = carry_ref[...].astype(F32)

    def step(n, total):
        base = n * group
        state = jnp.stack(
            [(local_ref[base + k] + reach_ref[base + k] * carry).astype(BF) for k in range(group)]
        )
        state_ref[pl.ds(base, group)] = state
        own = own_ref[pl.ds(base, group)].reshape(many, chans).astype(F32)
        pre = conv(state, 0, rows, kernel_ref[...]) + gain_ref[...] * own
        square = pre * pre
        bend = jnp.tanh(GELU_A * (pre + GELU_B * square * pre))
        half = 0.5 * (1.0 + bend)
        slope = half + 0.5 * pre * (1.0 - bend * bend) * (GELU_A * (1.0 + 3.0 * GELU_B * square))
        grad = cot_ref[pl.ds(base, group)].reshape(many, chans).astype(F32) * slope
        act_ref[pl.ds(base, group)] = (pre * half).astype(BF).reshape(group, rows, cols, chans)
        grad_ref[pl.ds(base, group)] = grad.astype(BF).reshape(group, rows, cols, chans)
        return total + jnp.sum((grad * own).reshape(many // 8, 8, chans), axis=0)

    total = lax.fori_loop(0, frames // group, step, jnp.zeros((8, chans), F32))
    gain_grad_ref[...] = jnp.sum(total, axis=0, keepdims=True)


def put_blocks(total, out_ref, scale):
    left, right = out_ref.shape[2:]
    for i in range(3):
        for j in range(3):
            out_ref[i, j] = (
                total[i * left : (i + 1) * left, j * right : (j + 1) * right] * scale
            ).astype(out_ref.dtype)


def out_grad_kernel(scale, state_ref, grad_ref, out_ref, total_ref):
    frames, rows, cols, chans = grad_ref.shape
    group = group_of(frames, 4)
    total_ref[...] = jnp.zeros_like(total_ref)

    def step(n, _):
        base = n * group
        grad = grad_ref[pl.ds(base, group)].reshape(group * rows * cols, chans).astype(F32)
        left = taps(state_ref[pl.ds(base, group)], 0, rows)
        total_ref[...] += outer(left, spread(grad, cols))
        return 0

    lax.fori_loop(0, frames // group, step, 0)
    put_blocks(total_ref[...], out_ref, scale)


def back_kernel(edge_ref, own_ref, first_ref, second_ref, kernel_ref, lam_ref, local_ref, lead_ref, wide_ref):
    frames, rows, cols, _ = own_ref.shape
    state_chans = kernel_ref.shape[1] // 3
    fill_halo(edge_ref, wide_ref, own_ref, first_ref, second_ref)
    group = group_of(frames, 2)
    many = (rows + 2) * cols

    def step(n, carry):
        base = frames - (n + 1) * group
        flow = conv(wide_ref[pl.ds(base, group)], 0, rows + 2, kernel_ref[...])
        for k in reversed(range(group)):
            adjoint = inside(edge_ref, flow[k * many : (k + 1) * many], cols) + carry
            local_ref[base + k] = adjoint.reshape(rows + 2, cols, state_chans)
            carry = lam_ref[base + k] * adjoint
        return carry

    lead = lax.fori_loop(0, frames // group, step, jnp.zeros((many, state_chans), F32))
    lead_ref[...] = lead.reshape(rows + 2, cols, state_chans).astype(BF)


def in_grad_kernel(
    scale, decay_scale, local_ref, back_ref, reach_ref, lam_ref, wide_ref, state_ref, carry_ref,
    adjoint_ref, out_ref, decay_ref, total_ref,
):
    frames, rows_two, cols, chans = local_ref.shape
    rows = rows_two - 2
    group = group_of(frames, 4)
    many = rows * cols
    back = back_ref[...].astype(F32)
    total_ref[...] = jnp.zeros_like(total_ref)

    def step(n, previous):
        base = n * group
        kept = []
        for k in range(group):
            adjoint = local_ref[base + k] + reach_ref[base + k] * back
            adjoint_ref[base + k] = adjoint.astype(BF)
            mine = adjoint[1 : 1 + rows].reshape(many, chans)
            kept.append(mine)
            part = jnp.sum((mine * previous).reshape(many // 8, 8, chans), axis=0)
            decay_ref[base + k] = jnp.sum(part, axis=0, keepdims=True) * lam_ref[base + k] * decay_scale
            previous = state_ref[base + k, 1 : 1 + rows].reshape(many, chans).astype(F32)
        left = taps(wide_ref[pl.ds(base, group)], 1, rows)
        total_ref[...] += outer(left, spread(jnp.concatenate(kept, axis=0), cols))
        return previous

    before = carry_ref[1 : 1 + rows].reshape(many, chans).astype(F32)
    lax.fori_loop(0, frames // group, step, before)
    put_blocks(total_ref[...], out_ref, scale)


def video_grad_kernel(adjoint_ref, grad_ref, kernel_ref, gain_ref, out_ref):
    frames, rows, cols, chans = grad_ref.shape
    group = group_of(frames, 2)

    def step(n, _):
        base = n * group
        grad = grad_ref[pl.ds(base, group)].reshape(group * rows * cols, chans).astype(F32)
        flow = conv(adjoint_ref[pl.ds(base, group)], 0, rows, kernel_ref[...])
        out_ref[pl.ds(base, group)] = (
            (flow + gain_ref[...] * grad).astype(BF).reshape(group, rows, cols, chans)
        )
        return 0

    lax.fori_loop(0, frames // group, step, 0)


def halo_pair(field, deep):
    count = lax.axis_size("rows")
    odd = lax.rem(lax.axis_index("rows"), 2)
    rows = field.shape[1]
    swap = lambda low: [p for i in range(low, count - 1, 2) for p in ((i, i + 1), (i + 1, i))]
    pick = lambda flag: lax.dynamic_slice_in_dim(field, flag * (rows - deep), deep, axis=1)
    first, second = pick(1 - odd), pick(odd)
    return lax.ppermute(first, "rows", swap(0)), lax.ppermute(second, "rows", swap(1))


def from_earlier(end, totals):
    count = lax.axis_size("tm")
    found, between = None, None
    for k in range(1, count):
        pairs = [(i, i + k) for i in range(count - k)]
        piece = lax.ppermute(end, "tm", pairs)
        if k == 1:
            found = piece.astype(F32)
        else:
            step = lax.ppermute(totals, "tm", [(i, i + k - 1) for i in range(count - k + 1)])
            between = step if between is None else between + step
            found = found + jnp.exp(between) * piece.astype(F32)
    if found is None:
        return jnp.zeros(end.shape, BF)
    return found.astype(BF)


def from_later(lead, totals):
    count = lax.axis_size("tm")
    found, between = None, None
    for k in range(1, count):
        pairs = [(i + k, i) for i in range(count - k)]
        piece = lax.ppermute(lead, "tm", pairs)
        if k == 1:
            found = piece.astype(F32)
        else:
            step = lax.ppermute(totals, "tm", [(i + k - 1, i) for i in range(count - k + 1)])
            between = step if between is None else between + step
            found = found + jnp.exp(between) * piece.astype(F32)
    if found is None:
        return jnp.zeros(lead.shape, BF)
    return found.astype(BF)


def tree_sum(part):
    stages = []
    for axis in ("dp", "tm", "rows"):
        size, mask = lax.axis_size(axis), 1
        while mask < size:
            stages.append((axis, mask))
            mask *= 2
    split = 2 if part.shape[0] % 64 == 0 else 0
    swap = lambda value, axis, mask: lax.ppermute(
        value, axis, [(i, i ^ mask) for i in range(lax.axis_size(axis))]
    )
    bit = lambda axis, mask: jnp.where((lax.axis_index(axis) & mask) != 0, 1, 0)
    done = []
    for axis, mask in stages[:split]:
        half = part.shape[0] // 2
        mine = bit(axis, mask)
        sent = lax.dynamic_slice_in_dim(part, (1 - mine) * half, half, axis=0).astype(BF)
        kept = lax.dynamic_slice_in_dim(part, mine * half, half, axis=0)
        part = kept.astype(F32) + swap(sent, axis, mask).astype(F32)
        done.append((axis, mask))
    whole = part.astype(BF)
    for axis, mask in stages[split:]:
        whole = (whole.astype(F32) + swap(whole, axis, mask).astype(F32)).astype(BF)
    for axis, mask in reversed(done):
        other = swap(whole, axis, mask)
        mine = bit(axis, mask) == 1
        whole = jnp.where(
            mine, jnp.concatenate([other, whole], axis=0), jnp.concatenate([whole, other], axis=0)
        )
    return whole


def on_device(video, cotangent, in_kernel, out_kernel, skip_gain, log_decay):
    seqs, frames, rows, cols, chans = video.shape
    state_chans = in_kernel.shape[3]
    sizes = {axis: lax.axis_size(axis) for axis in ("tm", "rows", "dp")}
    devices = sizes["tm"] * sizes["rows"] * sizes["dp"]
    for size in sizes.values():
        assert size & (size - 1) == 0
    assert seqs == 1 and rows >= 2
    video, cotangent = video[0], cotangent[0]
    band = lax.axis_index("rows")
    edge = jnp.stack(
        [jnp.where(band > 0, 1, 0), jnp.where(band < sizes["rows"] - 1, 1, 0), lax.rem(band, 2)]
    ).astype(jnp.int32)
    cum = jnp.cumsum(log_decay, axis=0)
    totals = cum[-1:]
    lam = jnp.exp(log_decay)[:, None, :]
    reach = jnp.exp(cum)[:, None, :]
    back_reach = jnp.exp(totals - cum)[:, None, :]
    gain = skip_gain[None, :]
    flat = lambda k: k.transpose(0, 2, 1, 3).reshape(3 * k.shape[2], 3 * k.shape[3])
    flip = lambda k: k[::-1, ::-1].transpose(0, 3, 1, 2).reshape(3 * k.shape[3], 3 * k.shape[2])
    wide_rows = frames * (rows + 2) * cols
    narrow_rows = frames * rows * cols
    each = 2 * 9 * chans * state_chans
    weight_scale = 1.0 / math.sqrt(devices * narrow_rows * seqs)
    decay_scale = 1.0 / math.sqrt(seqs * rows * cols * sizes["rows"] * sizes["dp"])

    first, second = halo_pair(video, 2)
    wide, local, end = call(
        drive_kernel,
        [
            shape((frames, rows + 4, cols, chans), BF),
            shape((frames, rows + 2, cols, state_chans), F32),
            shape((rows + 2, cols, state_chans), BF),
        ],
        [edge, video, first, second, flat(in_kernel), lam],
        1,
        flops=each * wide_rows,
    )
    carry = from_earlier(end, totals)
    state, act, grad, gain_part = call(
        layer_kernel,
        [
            shape((frames, rows + 2, cols, state_chans), BF),
            shape(video.shape, BF),
            shape(video.shape, BF),
            shape((1, chans), F32),
        ],
        [local, carry, reach, video, cotangent, flat(out_kernel), gain],
        0,
        flops=each * narrow_rows,
    )
    first, second = halo_pair(grad, 2)
    (out_part,) = call(
        functools.partial(out_grad_kernel, weight_scale),
        [shape((3, 3, state_chans, chans), F32)],
        [state, grad],
        0,
        scratch=[pltpu.VMEM((3 * state_chans, 3 * chans), F32)],
        flops=each * narrow_rows,
    )
    local, lead = call(
        back_kernel,
        [
            shape((frames, rows + 2, cols, state_chans), F32),
            shape((rows + 2, cols, state_chans), BF),
        ],
        [edge, grad, first, second, flip(out_kernel), lam],
        1,
        scratch=[pltpu.VMEM((frames, rows + 4, cols, chans), BF)],
        flops=each * wide_rows,
    )
    back = from_later(lead, totals)
    adjoint, in_part, decay_part = call(
        functools.partial(in_grad_kernel, weight_scale, decay_scale),
        [
            shape((frames, rows + 2, cols, state_chans), BF),
            shape((3, 3, chans, state_chans), F32),
            shape((frames, 1, state_chans), F32),
        ],
        [local, back, back_reach, lam, wide, state, carry],
        0,
        scratch=[pltpu.VMEM((3 * chans, 3 * state_chans), F32)],
        flops=each * narrow_rows,
    )
    (video_grad,) = call(
        video_grad_kernel,
        [shape(video.shape, BF)],
        [adjoint, grad, flip(in_kernel), gain],
        0,
        flops=each * narrow_rows,
    )
    block = lax.axis_index("tm")
    slots = jnp.where(
        jnp.arange(sizes["tm"])[:, None, None] == block, decay_part[:, 0][None], 0.0
    ).reshape(-1, state_chans)
    pieces = [
        in_part.reshape(-1, state_chans),
        out_part.reshape(-1, chans),
        slots,
        gain_part * weight_scale,
    ]
    used = sum(p.shape[0] for p in pieces)
    pieces.append(jnp.zeros((-used % 64, chans), F32))
    total = tree_sum(jnp.concatenate(pieces, axis=0)).astype(F32)
    at = 0
    sums = []
    for piece in pieces[:4]:
        sums.append(lax.slice_in_dim(total, at, at + piece.shape[0], axis=0))
        at += piece.shape[0]
    return (
        act[None],
        video_grad[None],
        sums[0].reshape(3, 3, chans, state_chans),
        sums[1].reshape(3, 3, state_chans, chans),
        sums[3][0],
        lax.dynamic_slice_in_dim(sums[2], block * frames, frames, axis=0),
    )


def solution(mesh):
    placed = (
        P("dp", "tm", "rows", None, None),
        P("dp", "tm", "rows", None, None),
        P(),
        P(),
        P(),
        P("tm", None),
    )
    return jax.shard_map(
        on_device,
        mesh=mesh,
        in_specs=placed,
        out_specs=(
            P("dp", "tm", "rows", None, None),
            P("dp", "tm", "rows", None, None),
            P(),
            P(),
            P(),
            P("tm", None),
        ),
        check_vma=False,
    )
```

time: 369 us -> 91.7 us (0.25)
  blocking collectives: 112 us -> 0 us
  waiting for transfers between devices: 133 us -> 34 us
  matrix products: 42.6 us -> 0 us
  other arithmetic: 20.8 us -> 1.33 us
  Pallas kernels: 0 us -> 17.9 us
  local copies, waits for them, and re-layouts: 26.5 us -> 12.1 us
  between operations: 14.6 us -> 1 us
  starting transfers between devices: 18.3 us -> 25.1 us
    psum x1 -> x0, waiting for transfers between devices: 124 us -> none  [on_device(): lax.psum((in_grad, out_grad, gain_grad), ('tm', 'rows', 'dp'))]
    psum x2 -> x0, blocking collectives: 98.2 us -> none  [the longest x1 57.8 us: on_device(): decay_grad = lax.psum(decay_part, ('rows', 'dp')) * decay_scale]
    dot_general x56 -> x0, matrix products: 42.6 us -> none  [the longest x18 14.9 us: kernel_grad(): lax.dot_general(piece, flat_grad, (((0,), (0,)), ((), ())), preferred_ele...]
    ppermute x8 -> x13, waiting for transfers between devices: 8.65 us -> 34 us  [the longest x7 22.9 us: tree_sum(): lax.ppermute(value, axis, [(i, i ^ mask) for i in range(lax.axis_size(axi...]
    pallas_call x0 -> x6, Pallas kernels: none -> 17.9 us  [call(): pl.pallas_call(body, out_shape=outs, in_specs=[smem() if n < scalars else...]
    all_gather x3 -> x0, blocking collectives: 13.9 us -> none  [the longest x1 5.05 us: on_device(): lax.all_gather(leading[None].astype(jnp.bfloat16), 'tm', axis=0, tiled=True)]
    dot_general x2 -> x0, local copies, waits for them, and re-layouts: 8.26 us -> none  [the longest x1 4.54 us: on_device(): jnp.einsum('tkp,strcp->skrcp', within, state_grad, precision=lax.Precisio...]
    ppermute x8 -> x13, starting transfers between devices: 18.2 us -> 25.1 us  [the longest x7 11 us: tree_sum(): lax.ppermute(value, axis, [(i, i ^ mask) for i in range(lax.axis_size(axi...]
  transfers between devices with their start and end apart: 9 -> 13, of which waited for: 5 -> 10; matrix products, arithmetic and copies ran while one was open for 4% -> 4% of each run, Pallas kernels for 0% -> 5%
where the time goes in v1:
time: 91.7 us; the launch traced here: 91.4 us
  waiting for transfers between devices  34 us (37%)
  starting transfers between devices  25.1 us (27%)
  Pallas kernels  17.9 us (20%)
  local copies, waits for them, and re-layouts  12.1 us (13%)
  other arithmetic  1.33 us (1%)
  between operations  1 us (1%)
    ppermute x7, waiting for transfers between devices, tree_sum(): lax.ppermute(value, axis, [(i, i ^ mask) for i in range(lax.axis_size(axi...  22.9 us
    pallas_call x6, Pallas kernels, call(): pl.pallas_call(body, out_shape=outs, in_specs=[smem() if n < scalars else...  17.9 us
    ppermute x7, starting transfers between devices, tree_sum(): lax.ppermute(value, axis, [(i, i ^ mask) for i in range(lax.axis_size(axi...  11 us
    ppermute x2, starting transfers between devices, halo_pair(): lax.ppermute(first, 'rows', swap(0))  7.71 us
    ppermute x2, waiting for transfers between devices, halo_pair(): lax.ppermute(first, 'rows', swap(0))  7.17 us
    unnamed x34, local copies, waits for them, and re-layouts  5.51 us
    ppermute x1, starting transfers between devices, from_earlier(): piece = lax.ppermute(end, 'tm', pairs)  3.71 us
    ppermute x1, waiting for transfers between devices, from_later(): piece = lax.ppermute(lead, 'tm', pairs)  2.98 us
  transfers between devices with their start and end apart: 13, of which 10 were waited for; matrix products, arithmetic and copies ran while one was open for 4% of the time, Pallas kernels for 5%

profile of v1, /device:TPU:0, one launch (start us, length us, event | category | flops | bytes accessed | tf_op | source)
XLA Modules:
  0.0 91.4 jit_solution(11807442595170716360)
XLA Ops:
  0.7 1.1 %dynamic-slice_bitcast_fusion = (bf16[16,2,32,128]{3,2,1,0:T(8,128)(2,1)S(1)}, bf16[16,2,32,128]{3,2,1,0:T(8,128)(2,1)S(1)}) fusion(bf16[1,16,4,32,128]{4,3,2,1,0:T(8,128)(2,1)} %param.6, s32[]{:T(128)S(6)} %select_n.62, s32[]{:T(128)S(6)} %select_n.61), kind=kLoop, calls=%fused_computation.16 | loop fusion | bytes 1048584 | tf_op jit(solution)/shard_map/dynamic_slice | solution.py:260
  1.8 3.1 %collective-permute-start = (bf16[16,2,32,128]{3,2,1,0:T(8,128)(2,1)S(1)}, bf16[16,2,32,128]{3,2,1,0:T(8,128)(2,1)S(1)}, u32[]{:S(2)}, u32[]{:S(2)}) collective-permute-start(bf16[16,2,32,128]{3,2,1,0:T(8,128)(2,1)S(1)} %get-tuple-element.35), channel_id=1, source_target_pairs={{0,4},{4,0},{8,12},{12,8},{1,5},{5,1},{9,13},{13,9},{2,6},{6,2},{1... | collective-permute-start | bytes 786440 | tf_op jit(solution)/shard_map/ppermute | solution.py:262
  7.5 3.7 %collective-permute-done.first_ref = bf16[16,2,32,128]{3,2,1,0:T(8,128)(2,1)S(1)} collective-permute-done((bf16[16,2,32,128]{3,2,1,0:T(8,128)(2,1)S(1)}, bf16[16,2,32,128]{3,2,1,0:T(8,128)(2,1)S(1)}, u32[]{:S(2)}, u32[]{:S(2)}) %collective-permute-start) | collective-permute-done | bytes 262176 | tf_op jit(solution)/shard_map/ppermute | solution.py:262
  11.9 0.9 %copy-done.10 = bf16[16,2,32,128]{3,2,1,0:T(8,128)(2,1)S(1)} copy-done((bf16[16,2,32,128]{3,2,1,0:T(8,128)(2,1)S(1)}, bf16[16,2,32,128]{3,2,1,0:T(8,128)(2,1)}, u32[]{:S(2)}) %copy-start.10) | copy-done | bytes 262168
  12.9 4.0 %shard_map.109 = (bf16[16,8,32,128]{3,2,1,0:T(8,128)(2,1)S(1)}, f32[16,6,32,128]{3,2,1,0:T(8,128)S(1)}, bf16[6,32,128]{2,1,0:T(8,128)(2,1)}) custom-call(s32[3]{0:T(128)S(1)} %pad_add_fusion.edge_ref, bf16[16,4,32,128]{3,2,1,0:T(8,128)(2,1)S(1)} %bitcast.51, bf16[16,2,32,128]{3,2,1,0:T(8,128)(2,1)S(1)} %collective-permute-done.first_ref, ...), custom_call_target="tpu_custom_call" | custom-call | flops 905969664 | bytes 4022284 | tf_op jit(solution)/shard_map/pallas_call | solution.py:28
  16.9 3.7 %collective-permute-start.2 = (bf16[6,32,128]{2,1,0:T(8,128)(2,1)}, bf16[6,32,128]{2,1,0:T(8,128)(2,1)S(1)}, u32[]{:S(2)}, u32[]{:S(2)}) collective-permute-start(bf16[6,32,128]{2,1,0:T(8,128)(2,1)} %get-tuple-element.19), channel_id=1, source_target_pairs={{0,16},{1,17},{2,18},{3,19},{4,20},{5,21},{6,22},{7,23},{8,24},{9,... | collective-permute-start | bytes 147464 | tf_op jit(solution)/shard_map/ppermute | solution.py:270
  20.6 0.7 reverse_bitcast_fusion.1
  21.7 1.0 %collective-permute-done.2.carry_ref = bf16[6,32,128]{2,1,0:T(8,128)(2,1)S(1)} collective-permute-done((bf16[6,32,128]{2,1,0:T(8,128)(2,1)}, bf16[6,32,128]{2,1,0:T(8,128)(2,1)S(1)}, u32[]{:S(2)}, u32[]{:S(2)}) %collective-permute-start.2) | collective-permute-done | bytes 49184 | tf_op jit(solution)/shard_map/ppermute | solution.py:270
  22.7 1.0 %copy-done.3 = bf16[1,16,4,32,128]{4,3,2,1,0:T(8,128)(2,1)S(1)} copy-done((bf16[1,16,4,32,128]{4,3,2,1,0:T(8,128)(2,1)S(1)}, bf16[1,16,4,32,128]{4,3,2,1,0:T(8,128)(2,1)}, u32[]{:S(2)}) %copy-start.3) | copy-done | bytes 524312
  23.7 4.0 %shard_map.110 = (bf16[16,6,32,128]{3,2,1,0:T(8,128)(2,1)S(1)}, bf16[16,4,32,128]{3,2,1,0:T(8,128)(2,1)}, bf16[16,4,32,128]{3,2,1,0:T(8,128)(2,1)S(1)}, f32[1,128]{1,0:T(1,128)S(1)}) custom-call(f32[16,6,32,128]{3,2,1,0:T(8,128)S(1)} %get-tuple-element.18.local_ref, bf16[6,32,128]{2,1,0:T(8,128)(2,1)S(1)} %collective-permute-done.2.carry_ref, ...), custom_call_target="tpu_custom_call" | custom-call | flops 603979776 | bytes 4809728 | tf_op jit(solution)/shard_map/pallas_call | solution.py:28
  27.7 0.9 copy-done.1
  28.6 0.8 copy-done.4
  29.4 4.6 %collective-permute-start.3 = (bf16[16,2,32,128]{3,2,1,0:T(8,128)(2,1)S(1)}, bf16[16,2,32,128]{3,2,1,0:T(8,128)(2,1)S(1)}, u32[]{:S(2)}, u32[]{:S(2)}) collective-permute-start(bf16[16,2,32,128]{3,2,1,0:T(8,128)(2,1)S(1)} %get-tuple-element.33), channel_id=1, source_target_pairs={{0,4},{4,0},{8,12},{12,8},{1,5},{5,1},{9,13},{13,9},{2,6},{6,2},{1... | collective-permute-start | bytes 786440 | tf_op jit(solution)/shard_map/ppermute | solution.py:262
  35.2 3.4 %collective-permute-done.3.first_ref = bf16[16,2,32,128]{3,2,1,0:T(8,128)(2,1)S(1)} collective-permute-done((bf16[16,2,32,128]{3,2,1,0:T(8,128)(2,1)S(1)}, bf16[16,2,32,128]{3,2,1,0:T(8,128)(2,1)S(1)}, u32[]{:S(2)}, u32[]{:S(2)}) %collective-permute-start.3) | collective-permute-done | bytes 262176 | tf_op jit(solution)/shard_map/ppermute | solution.py:262
  38.6 3.5 %shard_map.111 = (f32[16,6,32,128]{3,2,1,0:T(8,128)S(1)}, bf16[6,32,128]{2,1,0:T(8,128)(2,1)S(1)}) custom-call(s32[3]{0:T(128)S(1)} %pad_add_fusion.edge_ref, bf16[16,4,32,128]{3,2,1,0:T(8,128)(2,1)S(1)} %copy-done.5, bf16[16,2,32,128]{3,2,1,0:T(8,128)(2,1)S(1)} %collective-permute-done.3.first_ref, ...), custom_call_target="tpu_custom_call" | custom-call | flops 905969664 | bytes 2973708 | tf_op jit(solution)/shard_map/pallas_call | solution.py:28
  42.1 1.3 %collective-permute-start.5 = (bf16[6,32,128]{2,1,0:T(8,128)(2,1)S(1)}, bf16[6,32,128]{2,1,0:T(8,128)(2,1)S(1)}, u32[]{:S(2)}, u32[]{:S(2)}) collective-permute-start(bf16[6,32,128]{2,1,0:T(8,128)(2,1)S(1)} %get-tuple-element.23), channel_id=1, source_target_pairs={{16,0},{17,1},{18,2},{19,3},{20,4},{21,5},{22,6},{23,7},{24,8},{25... | collective-permute-start | bytes 147464 | tf_op jit(solution)/shard_map/ppermute | solution.py:287
  43.4 1.7 %shard_map.114 = f32[3,3,128,128]{3,2,1,0:T(8,128)S(1)} custom-call(bf16[16,6,32,128]{3,2,1,0:T(8,128)(2,1)S(1)} %copy-done.2, bf16[16,4,32,128]{3,2,1,0:T(8,128)(2,1)S(1)} %copy-done.5), custom_call_target="tpu_custom_call" | custom-call | flops 603979776 | bytes 1900544 | tf_op jit(solution)/shard_map/pallas_call | solution.py:28
  45.1 3.0 %collective-permute-done.5.back_ref = bf16[6,32,128]{2,1,0:T(8,128)(2,1)S(1)} collective-permute-done((bf16[6,32,128]{2,1,0:T(8,128)(2,1)S(1)}, bf16[6,32,128]{2,1,0:T(8,128)(2,1)S(1)}, u32[]{:S(2)}, u32[]{:S(2)}) %collective-permute-start.5) | collective-permute-done | bytes 49184 | tf_op jit(solution)/shard_map/ppermute | solution.py:287
  48.1 1.8 %shard_map.112 = (bf16[16,6,32,128]{3,2,1,0:T(8,128)(2,1)S(1)}, f32[3,3,128,128]{3,2,1,0:T(8,128)S(1)}, f32[16,1,128]{2,1,0:T(1,128)S(1)}) custom-call(f32[16,6,32,128]{3,2,1,0:T(8,128)S(1)} %get-tuple-element.22.local_ref, bf16[6,32,128]{2,1,0:T(8,128)(2,1)S(1)} %collective-permute-done.5.back_ref, f32[16,1,128]{2,1,0:T(1,128)S(1)} %get-tuple-element.36.reach_ref, ...), custom_call_target="tpu_custom_call" | custom-call | flops 603979776 | bytes 4907008 | tf_op jit(solution)/shard_map/pallas_call | solution.py:28
  49.9 0.9 copy-done.7
  51.5 1.6 %collective-permute-done.6 = bf16[1184,128]{1,0:T(8,128)(2,1)S(1)} collective-permute-done((bf16[1184,128]{1,0:T(8,128)(2,1)S(1)}, bf16[1184,128]{1,0:T(8,128)(2,1)S(1)}, u32[]{:S(2)}, u32[]{:S(2)}) %collective-permute-start.6) | collective-permute-done | bytes 303136 | tf_op jit(solution)/shard_map/ppermute | solution.py:307
  53.1 1.6 %collective-permute-start.7 = (bf16[592,128]{1,0:T(8,128)(2,1)S(1)}, bf16[592,128]{1,0:T(8,128)(2,1)S(1)}, u32[]{:S(2)}, u32[]{:S(2)}) collective-permute-start(bf16[592,128]{1,0:T(8,128)(2,1)S(1)} %dynamic-slice_convert_fusion.1), channel_id=1, source_target_pairs={{0,2},{1,3},{2,0},{3,1},{4,6},{5,7},{6,4},{7,5},{8,10},{9,11},{10,... | collective-permute-start | bytes 454664 | tf_op jit(solution)/shard_map/ppermute | solution.py:307
  54.7 4.5 %collective-permute-done.7 = bf16[592,128]{1,0:T(8,128)(2,1)S(1)} collective-permute-done((bf16[592,128]{1,0:T(8,128)(2,1)S(1)}, bf16[592,128]{1,0:T(8,128)(2,1)S(1)}, u32[]{:S(2)}, u32[]{:S(2)}) %collective-permute-start.7) | collective-permute-done | bytes 151584 | tf_op jit(solution)/shard_map/ppermute | solution.py:307
  59.3 5.2 %collective-permute-done.8 = bf16[592,128]{1,0:T(8,128)(2,1)S(1)} collective-permute-done((bf16[592,128]{1,0:T(8,128)(2,1)S(1)}, bf16[592,128]{1,0:T(8,128)(2,1)S(1)}, u32[]{:S(2)}, u32[]{:S(2)}) %collective-permute-start.8) | collective-permute-done | bytes 151584 | tf_op jit(solution)/shard_map/ppermute | solution.py:307
  64.5 3.8 %collective-permute-start.9 = (bf16[592,128]{1,0:T(8,128)(2,1)S(1)}, bf16[592,128]{1,0:T(8,128)(2,1)S(1)}, u32[]{:S(2)}, u32[]{:S(2)}) collective-permute-start(bf16[592,128]{1,0:T(8,128)(2,1)S(1)} %add_convert_fusion.2), channel_id=1, source_target_pairs={{0,4},{4,0},{8,12},{12,8},{1,5},{5,1},{9,13},{13,9},{2,6},{6,2},{1... | collective-permute-start | bytes 454664 | tf_op jit(solution)/shard_map/ppermute | solution.py:307
  68.4 3.2 %collective-permute-done.9 = bf16[592,128]{1,0:T(8,128)(2,1)S(1)} collective-permute-done((bf16[592,128]{1,0:T(8,128)(2,1)S(1)}, bf16[592,128]{1,0:T(8,128)(2,1)S(1)}, u32[]{:S(2)}, u32[]{:S(2)}) %collective-permute-start.9) | collective-permute-done | bytes 151584 | tf_op jit(solution)/shard_map/ppermute | solution.py:307
  71.6 3.8 %collective-permute-start.10 = (bf16[592,128]{1,0:T(8,128)(2,1)S(1)}, bf16[592,128]{1,0:T(8,128)(2,1)S(1)}, u32[]{:S(2)}, u32[]{:S(2)}) collective-permute-start(bf16[592,128]{1,0:T(8,128)(2,1)S(1)} %add_convert_fusion.1), channel_id=1, source_target_pairs={{0,8},{4,12},{8,0},{12,4},{1,9},{5,13},{9,1},{13,5},{2,10},{6,14},... | collective-permute-start | bytes 454664 | tf_op jit(solution)/shard_map/ppermute | solution.py:307
  75.4 4.8 %collective-permute-done.10 = bf16[592,128]{1,0:T(8,128)(2,1)S(1)} collective-permute-done((bf16[592,128]{1,0:T(8,128)(2,1)S(1)}, bf16[592,128]{1,0:T(8,128)(2,1)S(1)}, u32[]{:S(2)}, u32[]{:S(2)}) %collective-permute-start.10) | collective-permute-done | bytes 151584 | tf_op jit(solution)/shard_map/ppermute | solution.py:307
  80.2 1.6 %collective-permute-start.11 = (bf16[592,128]{1,0:T(8,128)(2,1)S(1)}, bf16[592,128]{1,0:T(8,128)(2,1)S(1)}, u32[]{:S(2)}, u32[]{:S(2)}) collective-permute-start(bf16[592,128]{1,0:T(8,128)(2,1)S(1)} %add_convert_fusion), channel_id=1, source_target_pairs={{0,2},{1,3},{2,0},{3,1},{4,6},{5,7},{6,4},{7,5},{8,10},{9,11},{10,... | collective-permute-start | bytes 454664 | tf_op jit(solution)/shard_map/ppermute | solution.py:307
  81.8 3.7 %collective-permute-done.11 = bf16[592,128]{1,0:T(8,128)(2,1)S(1)} collective-permute-done((bf16[592,128]{1,0:T(8,128)(2,1)S(1)}, bf16[592,128]{1,0:T(8,128)(2,1)S(1)}, u32[]{:S(2)}, u32[]{:S(2)}) %collective-permute-start.11) | collective-permute-done | bytes 151584 | tf_op jit(solution)/shard_map/ppermute | solution.py:307
  86.0 3.0 %shard_map.113 = bf16[16,4,32,128]{3,2,1,0:T(8,128)(2,1)} custom-call(bf16[16,6,32,128]{3,2,1,0:T(8,128)(2,1)S(1)} %copy-done.8, bf16[16,4,32,128]{3,2,1,0:T(8,128)(2,1)S(1)} %copy-done.5, bf16[384,384]{1,0:T(8,128)(2,1)S(1)} %bitcast.59, f32[1,128]{1,0:T(1,128)S(1)} %bitcast.65), custom_call_target="tpu_custom_call" | custom-call | flops 603979776 | bytes 2130432 | tf_op jit(solution)/shard_map/pallas_call | solution.py:28
  89.2 1.1 %fusion.1 = (f32[1152,128]{1,0:T(8,128)}, f32[1152,128]{1,0:T(8,128)}) fusion(f32[2368,128]{1,0:T(8,128)S(1)} %fusion), kind=kLoop, calls=%fused_computation.28 | loop fusion | bytes 2359296 | tf_op jit(solution)/shard_map/slice | solution.py:439
  (67 shorter events, 7.4 us)
Async XLA Ops:
  0.6 6.5 %copy-start.12 = (bf16[3,3,128,128]{3,2,1,0:T(8,128)(2,1)S(1)}, bf16[3,3,128,128]{3,2,1,0:T(8,128)(2,1)}, u32[]{:S(2)}) copy-start(bf16[3,3,128,128]{3,2,1,0:T(8,128)(2,1)} %param.8) | copy-start | bytes 884740
  0.7 11.3 %copy-start = (bf16[1,16,4,32,128]{4,3,2,1,0:T(8,128)(2,1)S(1)}, bf16[1,16,4,32,128]{4,3,2,1,0:T(8,128)(2,1)}, u32[]{:S(2)}) copy-start(bf16[1,16,4,32,128]{4,3,2,1,0:T(8,128)(2,1)} %param.6) | copy-start | bytes 1572868
  1.8 9.4 %collective-permute-start = (bf16[16,2,32,128]{3,2,1,0:T(8,128)(2,1)S(1)}, bf16[16,2,32,128]{3,2,1,0:T(8,128)(2,1)S(1)}, u32[]{:S(2)}, u32[]{:S(2)}) collective-permute-start(bf16[16,2,32,128]{3,2,1,0:T(8,128)(2,1)S(1)} %get-tuple-element.35), channel_id=1, source_target_pairs={{0,4},{4,0},{8,12},{12,8},{1,5},{5,1},{9,13},{13,9},{2,6},{6,2},{1... | collective-permute-start | bytes 786440 | tf_op jit(solution)/shard_map/ppermute | solution.py:262
  4.9 6.3 %collective-permute-start.1 = (bf16[16,2,32,128]{3,2,1,0:T(8,128)(2,1)S(1)}, bf16[16,2,32,128]{3,2,1,0:T(8,128)(2,1)S(1)}, u32[]{:S(2)}, u32[]{:S(2)}) collective-permute-start(bf16[16,2,32,128]{3,2,1,0:T(8,128)(2,1)S(1)} %get-tuple-element.34), channel_id=1, source_target_pairs={{4,8},{8,4},{5,9},{9,5},{6,10},{10,6},{7,11},{11,7},{20,24},{24,20... | collective-permute-start | bytes 786440 | tf_op jit(solution)/shard_map/ppermute | solution.py:262
  11.2 0.7 copy-start.9
  11.9 1.0 %copy-start.10 = (bf16[16,2,32,128]{3,2,1,0:T(8,128)(2,1)S(1)}, bf16[16,2,32,128]{3,2,1,0:T(8,128)(2,1)}, u32[]{:S(2)}) copy-start(bf16[16,2,32,128]{3,2,1,0:T(8,128)(2,1)} %copy-done.9) | copy-start | bytes 786436
  12.9 7.7 %copy-start.11 = (bf16[3,3,128,128]{3,2,1,0:T(8,128)(2,1)S(1)}, bf16[3,3,128,128]{3,2,1,0:T(8,128)(2,1)}, u32[]{:S(2)}) copy-start(bf16[3,3,128,128]{3,2,1,0:T(8,128)(2,1)} %param.9) | copy-start | bytes 884740
  16.9 5.8 %copy-start.6 = (f32[128]{0:T(128)S(1)}, f32[128]{0:T(128)}, u32[]{:S(2)}) copy-start(f32[128]{0:T(128)} %param.10) | copy-start | bytes 1540
  16.9 5.8 %collective-permute-start.2 = (bf16[6,32,128]{2,1,0:T(8,128)(2,1)}, bf16[6,32,128]{2,1,0:T(8,128)(2,1)S(1)}, u32[]{:S(2)}, u32[]{:S(2)}) collective-permute-start(bf16[6,32,128]{2,1,0:T(8,128)(2,1)} %get-tuple-element.19), channel_id=1, source_target_pairs={{0,16},{1,17},{2,18},{3,19},{4,20},{5,21},{6,22},{7,23},{8,24},{9,... | collective-permute-start | bytes 147464 | tf_op jit(solution)/shard_map/ppermute | solution.py:270
  22.7 1.0 %copy-start.3 = (bf16[1,16,4,32,128]{4,3,2,1,0:T(8,128)(2,1)S(1)}, bf16[1,16,4,32,128]{4,3,2,1,0:T(8,128)(2,1)}, u32[]{:S(2)}) copy-start(bf16[1,16,4,32,128]{4,3,2,1,0:T(8,128)(2,1)} %param.7) | copy-start | bytes 1572868
  27.7 0.9 copy-start.1
  28.6 6.1 %copy-start.14 = (bf16[3,128,3,128]{1,3,2,0:T(8,128)(2,1)S(1)}, bf16[3,128,3,128]{1,3,2,0:T(8,128)(2,1)}, u32[]{:S(2)}) copy-start(bf16[3,128,3,128]{1,3,2,0:T(8,128)(2,1)} %reverse_bitcast_fusion.1) | copy-start | bytes 884740
  28.6 0.8 copy-start.4
  29.4 9.2 %copy-start.5 = (bf16[16,4,32,128]{3,2,1,0:T(8,128)(2,1)S(1)}, bf16[16,4,32,128]{3,2,1,0:T(8,128)(2,1)}, u32[]{:S(2)}) copy-start(bf16[16,4,32,128]{3,2,1,0:T(8,128)(2,1)} %copy-done.4) | copy-start | bytes 1572868
  29.4 9.2 %collective-permute-start.3 = (bf16[16,2,32,128]{3,2,1,0:T(8,128)(2,1)S(1)}, bf16[16,2,32,128]{3,2,1,0:T(8,128)(2,1)S(1)}, u32[]{:S(2)}, u32[]{:S(2)}) collective-permute-start(bf16[16,2,32,128]{3,2,1,0:T(8,128)(2,1)S(1)} %get-tuple-element.33), channel_id=1, source_target_pairs={{0,4},{4,0},{8,12},{12,8},{1,5},{5,1},{9,13},{13,9},{2,6},{6,2},{1... | collective-permute-start | bytes 786440 | tf_op jit(solution)/shard_map/ppermute | solution.py:262
  34.0 4.6 %collective-permute-start.4 = (bf16[16,2,32,128]{3,2,1,0:T(8,128)(2,1)S(1)}, bf16[16,2,32,128]{3,2,1,0:T(8,128)(2,1)S(1)}, u32[]{:S(2)}, u32[]{:S(2)}) collective-permute-start(bf16[16,2,32,128]{3,2,1,0:T(8,128)(2,1)S(1)} %get-tuple-element.32), channel_id=1, source_target_pairs={{4,8},{8,4},{5,9},{9,5},{6,10},{10,6},{7,11},{11,7},{20,24},{24,20... | collective-permute-start | bytes 786440 | tf_op jit(solution)/shard_map/ppermute | solution.py:262
  38.6 4.8 %copy-start.2 = (bf16[16,6,32,128]{3,2,1,0:T(8,128)(2,1)S(1)}, bf16[16,6,32,128]{3,2,1,0:T(8,128)(2,1)}, u32[]{:S(2)}) copy-start(bf16[16,6,32,128]{3,2,1,0:T(8,128)(2,1)} %copy-done.1) | copy-start | bytes 2359300
  42.1 6.0 %collective-permute-start.5 = (bf16[6,32,128]{2,1,0:T(8,128)(2,1)S(1)}, bf16[6,32,128]{2,1,0:T(8,128)(2,1)S(1)}, u32[]{:S(2)}, u32[]{:S(2)}) collective-permute-start(bf16[6,32,128]{2,1,0:T(8,128)(2,1)S(1)} %get-tuple-element.23), channel_id=1, source_target_pairs={{16,0},{17,1},{18,2},{19,3},{20,4},{21,5},{22,6},{23,7},{24,8},{25... | collective-permute-start | bytes 147464 | tf_op jit(solution)/shard_map/ppermute | solution.py:287
  49.9 0.9 copy-start.7
  51.4 1.7 %collective-permute-start.6 = (bf16[1184,128]{1,0:T(8,128)(2,1)S(1)}, bf16[1184,128]{1,0:T(8,128)(2,1)S(1)}, u32[]{:S(2)}, u32[]{:S(2)}) collective-permute-start(bf16[1184,128]{1,0:T(8,128)(2,1)S(1)} %dynamic-slice_convert_fusion), channel_id=1, source_target_pairs={{0,1},{1,0},{2,3},{3,2},{4,5},{5,4},{6,7},{7,6},{8,9},{9,8},{10,11... | collective-permute-start | bytes 909320 | tf_op jit(solution)/shard_map/ppermute | solution.py:307
  53.1 6.0 %collective-permute-start.7 = (bf16[592,128]{1,0:T(8,128)(2,1)S(1)}, bf16[592,128]{1,0:T(8,128)(2,1)S(1)}, u32[]{:S(2)}, u32[]{:S(2)}) collective-permute-start(bf16[592,128]{1,0:T(8,128)(2,1)S(1)} %dynamic-slice_convert_fusion.1), channel_id=1, source_target_pairs={{0,2},{1,3},{2,0},{3,1},{4,6},{5,7},{6,4},{7,5},{8,10},{9,11},{10,... | collective-permute-start | bytes 454664 | tf_op jit(solution)/shard_map/ppermute | solution.py:307
  54.7 31.0 %copy-start.13 = (bf16[3,3,128,128]{3,2,1,0:T(8,128)(2,1)S(1)}, bf16[3,3,128,128]{3,2,1,0:T(8,128)(2,1)}, u32[]{:S(2)}) copy-start(bf16[3,3,128,128]{3,2,1,0:T(8,128)(2,1)} %param.8) | copy-start | bytes 884740
  59.2 5.3 %collective-permute-start.8 = (bf16[592,128]{1,0:T(8,128)(2,1)S(1)}, bf16[592,128]{1,0:T(8,128)(2,1)S(1)}, u32[]{:S(2)}, u32[]{:S(2)}) collective-permute-start(bf16[592,128]{1,0:T(8,128)(2,1)S(1)} %add_convert_fusion.3), channel_id=1, source_target_pairs={{0,16},{16,0},{1,17},{17,1},{2,18},{18,2},{3,19},{19,3},{4,20},{20... | collective-permute-start | bytes 454664 | tf_op jit(solution)/shard_map/ppermute | solution.py:307
  64.5 7.0 %collective-permute-start.9 = (bf16[592,128]{1,0:T(8,128)(2,1)S(1)}, bf16[592,128]{1,0:T(8,128)(2,1)S(1)}, u32[]{:S(2)}, u32[]{:S(2)}) collective-permute-start(bf16[592,128]{1,0:T(8,128)(2,1)S(1)} %add_convert_fusion.2), channel_id=1, source_target_pairs={{0,4},{4,0},{8,12},{12,8},{1,5},{5,1},{9,13},{13,9},{2,6},{6,2},{1... | collective-permute-start | bytes 454664 | tf_op jit(solution)/shard_map/ppermute | solution.py:307
  71.6 8.6 %collective-permute-start.10 = (bf16[592,128]{1,0:T(8,128)(2,1)S(1)}, bf16[592,128]{1,0:T(8,128)(2,1)S(1)}, u32[]{:S(2)}, u32[]{:S(2)}) collective-permute-start(bf16[592,128]{1,0:T(8,128)(2,1)S(1)} %add_convert_fusion.1), channel_id=1, source_target_pairs={{0,8},{4,12},{8,0},{12,4},{1,9},{5,13},{9,1},{13,5},{2,10},{6,14},... | collective-permute-start | bytes 454664 | tf_op jit(solution)/shard_map/ppermute | solution.py:307
  80.2 5.3 %collective-permute-start.11 = (bf16[592,128]{1,0:T(8,128)(2,1)S(1)}, bf16[592,128]{1,0:T(8,128)(2,1)S(1)}, u32[]{:S(2)}, u32[]{:S(2)}) collective-permute-start(bf16[592,128]{1,0:T(8,128)(2,1)S(1)} %add_convert_fusion), channel_id=1, source_target_pairs={{0,2},{1,3},{2,0},{3,1},{4,6},{5,7},{6,4},{7,5},{8,10},{9,11},{10,... | collective-permute-start | bytes 454664 | tf_op jit(solution)/shard_map/ppermute | solution.py:307
  81.8 4.2 %copy-start.8 = (bf16[16,6,32,128]{3,2,1,0:T(8,128)(2,1)S(1)}, bf16[16,6,32,128]{3,2,1,0:T(8,128)(2,1)}, u32[]{:S(2)}) copy-start(bf16[16,6,32,128]{3,2,1,0:T(8,128)(2,1)} %copy-done.7) | copy-start | bytes 2359300
  85.6 3.5 %collective-permute-start.12 = (bf16[1184,128]{1,0:T(8,128)(2,1)S(1)}, bf16[1184,128]{1,0:T(8,128)(2,1)S(1)}, u32[]{:S(2)}, u32[]{:S(2)}) collective-permute-start(bf16[1184,128]{1,0:T(8,128)(2,1)S(1)} %maximum_select_fusion.1), channel_id=1, source_target_pairs={{0,1},{1,0},{2,3},{3,2},{4,5},{5,4},{6,7},{7,6},{8,9},{9,8},{10,11... | collective-permute-start | bytes 909320 | tf_op jit(solution)/shard_map/ppermute | solution.py:307

commit v2 on v1

--- a/solution.py
+++ b/solution.py
@@ -61,7 +61,7 @@
 
 
 def conv(field, first, rows, weights):
-    frames, _, cols, _ = field.shape
+    _, _, cols, _ = field.shape
     out = weights.shape[1] // 3
     wide = jnp.dot(taps(field, first, rows), weights, preferred_element_type=F32)
     column = columns(wide.shape[0], cols, out)
@@ -114,7 +114,7 @@
     frames, rows, cols, _ = own_ref.shape
     state_chans = kernel_ref.shape[1] // 3
     fill_halo(edge_ref, wide_ref, own_ref, first_ref, second_ref)
-    group = group_of(frames, 2)
+    group = group_of(frames, 16)
     many = (rows + 2) * cols
 
     def step(n, state):
@@ -135,7 +135,7 @@
     state_ref, act_ref, grad_ref, gain_grad_ref,
 ):
     frames, rows, cols, chans = own_ref.shape
-    group = group_of(frames, 2)
+    group = group_of(frames, 16)
     many = group * rows * cols
     carry = carry_ref[...].astype(F32)
 
@@ -171,7 +171,7 @@
 
 def out_grad_kernel(scale, state_ref, grad_ref, out_ref, total_ref):
     frames, rows, cols, chans = grad_ref.shape
-    group = group_of(frames, 4)
+    group = group_of(frames, 16)
     total_ref[...] = jnp.zeros_like(total_ref)
 
     def step(n, _):
@@ -189,7 +189,7 @@
     frames, rows, cols, _ = own_ref.shape
     state_chans = kernel_ref.shape[1] // 3
     fill_halo(edge_ref, wide_ref, own_ref, first_ref, second_ref)
-    group = group_of(frames, 2)
+    group = group_of(frames, 16)
     many = (rows + 2) * cols
 
     def step(n, carry):
@@ -211,7 +211,7 @@
 ):
     frames, rows_two, cols, chans = local_ref.shape
     rows = rows_two - 2
-    group = group_of(frames, 4)
+    group = group_of(frames, 16)
     many = rows * cols
     back = back_ref[...].astype(F32)
     total_ref[...] = jnp.zeros_like(total_ref)
@@ -238,7 +238,7 @@
 
 def video_grad_kernel(adjoint_ref, grad_ref, kernel_ref, gain_ref, out_ref):
     frames, rows, cols, chans = grad_ref.shape
-    group = group_of(frames, 2)
+    group = group_of(frames, 16)
 
     def step(n, _):
         base = n * group
@@ -297,34 +297,54 @@
 
 
 def tree_sum(part):
-    stages = []
-    for axis in ("dp", "tm", "rows"):
-        size, mask = lax.axis_size(axis), 1
-        while mask < size:
-            stages.append((axis, mask))
-            mask *= 2
-    split = 2 if part.shape[0] % 64 == 0 else 0
-    swap = lambda value, axis, mask: lax.ppermute(
-        value, axis, [(i, i ^ mask) for i in range(lax.axis_size(axis))]
-    )
-    bit = lambda axis, mask: jnp.where((lax.axis_index(axis) & mask) != 0, 1, 0)
+    axes = ("tm", "rows", "dp")
+    bits, scale = [], 1
+    for axis in reversed(axes):
+        size = 1
+        while size < lax.axis_size(axis):
+            bits.append((axis, size, size * scale))
+            size *= 2
+        scale *= lax.axis_size(axis)
+    near = [b for b in bits if b[0] == "dp"][:2] + [b for b in bits if b[0] == "tm"][:1]
+    far = [b for b in bits if b not in near]
+    devices = scale
+
+    def swap(value, mask):
+        return lax.ppermute(value, axes, [(i, i ^ mask) for i in range(devices)])
+
+    def place(group):
+        spot = 0
+        for n, (axis, mask, _) in enumerate(group):
+            spot = spot + jnp.where((lax.axis_index(axis) & mask) != 0, 1 << n, 0)
+        return spot
+
+    def combined(group, k):
+        return sum(mask for n, (_, _, mask) in enumerate(group) if (k >> n) & 1)
+
     done = []
-    for axis, mask in stages[:split]:
-        half = part.shape[0] // 2
-        mine = bit(axis, mask)
-        sent = lax.dynamic_slice_in_dim(part, (1 - mine) * half, half, axis=0).astype(BF)
-        kept = lax.dynamic_slice_in_dim(part, mine * half, half, axis=0)
-        part = kept.astype(F32) + swap(sent, axis, mask).astype(F32)
-        done.append((axis, mask))
+    for stage, group in enumerate((near[:1], near[1:])):
+        if not group:
+            continue
+        ways = 1 << len(group)
+        size = part.shape[0] // ways
+        spot = place(group)
+        chunk = lambda k: lax.dynamic_slice_in_dim(part, (spot ^ k) * size, size, axis=0)
+        sent = [chunk(k).astype(BF) for k in range(1, ways)]
+        found = [swap(v, combined(group, k + 1)) for k, v in enumerate(sent)]
+        part = chunk(0)
+        for piece in found:
+            part = part + piece.astype(F32)
+        done.append((stage, group, spot))
     whole = part.astype(BF)
-    for axis, mask in stages[split:]:
-        whole = (whole.astype(F32) + swap(whole, axis, mask).astype(F32)).astype(BF)
-    for axis, mask in reversed(done):
-        other = swap(whole, axis, mask)
-        mine = bit(axis, mask) == 1
-        whole = jnp.where(
-            mine, jnp.concatenate([other, whole], axis=0), jnp.concatenate([whole, other], axis=0)
-        )
+    for _, _, mask in far:
+        whole = (whole.astype(F32) + swap(whole, mask).astype(F32)).astype(BF)
+    for stage, group, spot in reversed(done):
+        ways, size = 1 << len(group), whole.shape[0]
+        found = [swap(whole, combined(group, k)) for k in range(1, ways)]
+        joined = jnp.zeros((ways * size, whole.shape[1]), BF)
+        for k, piece in enumerate([whole, *found]):
+            joined = lax.dynamic_update_slice_in_dim(joined, piece, (spot ^ k) * size, axis=0)
+        whole = joined
     return whole
 
 

time: 91.7 us -> 80.7 us (0.88)
  waiting for transfers between devices: 34 us -> 25.1 us
  Pallas kernels: 17.9 us -> 12.2 us
  starting transfers between devices: 25.1 us -> 28.6 us
    ppermute x7 -> x10, waiting for transfers between devices: 22.9 us -> 13.5 us  [swap(): return lax.ppermute(value, axes, [(i, i ^ mask) for i in range(devices)])]
    pallas_call x6, Pallas kernels: 17.9 us -> 12.2 us  [call(): pl.pallas_call(body, out_shape=outs, in_specs=[smem() if n < scalars else...]
    ppermute x7 -> x10, starting transfers between devices: 11 us -> 14.4 us  [swap(): return lax.ppermute(value, axes, [(i, i ^ mask) for i in range(devices)])]
  transfers between devices with their start and end apart: 13 -> 16, of which waited for: 10 -> 13; matrix products, arithmetic and copies ran while one was open for 4% -> 5% of each run, Pallas kernels for 5% -> 4%
where the time goes in v2:
time: 80.7 us; the launch traced here: 80.3 us
  starting transfers between devices  28.6 us (35%)
  waiting for transfers between devices  25.1 us (31%)
  local copies, waits for them, and re-layouts  12.3 us (15%)
  Pallas kernels  12.2 us (15%)
  other arithmetic  1.16 us (1%)
  between operations  1.04 us (1%)
    ppermute x10, starting transfers between devices, swap(): return lax.ppermute(value, axes, [(i, i ^ mask) for i in range(devices)])  14.4 us
    ppermute x10, waiting for transfers between devices, swap(): return lax.ppermute(value, axes, [(i, i ^ mask) for i in range(devices)])  13.5 us
    pallas_call x6, Pallas kernels, call(): pl.pallas_call(body, out_shape=outs, in_specs=[smem() if n < scalars else...  12.2 us
    ppermute x2, starting transfers between devices, halo_pair(): lax.ppermute(first, 'rows', swap(0))  7.71 us
    ppermute x2, waiting for transfers between devices, halo_pair(): lax.ppermute(first, 'rows', swap(0))  7.17 us
    unnamed x34, local copies, waits for them, and re-layouts  5.47 us
    ppermute x1, starting transfers between devices, from_earlier(): piece = lax.ppermute(end, 'tm', pairs)  3.71 us
    ppermute x1, waiting for transfers between devices, from_later(): piece = lax.ppermute(lead, 'tm', pairs)  3.48 us
  transfers between devices with their start and end apart: 16, of which 13 were waited for; matrix products, arithmetic and copies ran while one was open for 5% of the time, Pallas kernels for 4%

profile of v2, /device:TPU:0, one launch (start us, length us, event | category | flops | bytes accessed | tf_op | source)
XLA Modules:
  0.0 80.3 jit_solution(8378943851518207763)
XLA Ops:
  0.7 1.1 %dynamic-slice_bitcast_fusion = (bf16[16,2,32,128]{3,2,1,0:T(8,128)(2,1)S(1)}, bf16[16,2,32,128]{3,2,1,0:T(8,128)(2,1)S(1)}) fusion(bf16[1,16,4,32,128]{4,3,2,1,0:T(8,128)(2,1)} %param.6, s32[]{:T(128)S(6)} %select_n.59, s32[]{:T(128)S(6)} %select_n.58), kind=kLoop, calls=%fused_computation.8 | loop fusion | bytes 1048584 | tf_op jit(solution)/shard_map/dynamic_slice | solution.py:260
  1.8 3.1 %collective-permute-start = (bf16[16,2,32,128]{3,2,1,0:T(8,128)(2,1)S(1)}, bf16[16,2,32,128]{3,2,1,0:T(8,128)(2,1)S(1)}, u32[]{:S(2)}, u32[]{:S(2)}) collective-permute-start(bf16[16,2,32,128]{3,2,1,0:T(8,128)(2,1)S(1)} %get-tuple-element.40), channel_id=1, source_target_pairs={{0,4},{4,0},{8,12},{12,8},{1,5},{5,1},{9,13},{13,9},{2,6},{6,2},{1... | collective-permute-start | bytes 786440 | tf_op jit(solution)/shard_map/ppermute | solution.py:262
  7.5 3.7 %collective-permute-done.first_ref = bf16[16,2,32,128]{3,2,1,0:T(8,128)(2,1)S(1)} collective-permute-done((bf16[16,2,32,128]{3,2,1,0:T(8,128)(2,1)S(1)}, bf16[16,2,32,128]{3,2,1,0:T(8,128)(2,1)S(1)}, u32[]{:S(2)}, u32[]{:S(2)}) %collective-permute-start) | collective-permute-done | bytes 262176 | tf_op jit(solution)/shard_map/ppermute | solution.py:262
  11.9 0.9 %copy-done.10 = bf16[16,2,32,128]{3,2,1,0:T(8,128)(2,1)S(1)} copy-done((bf16[16,2,32,128]{3,2,1,0:T(8,128)(2,1)S(1)}, bf16[16,2,32,128]{3,2,1,0:T(8,128)(2,1)}, u32[]{:S(2)}) %copy-start.10) | copy-done | bytes 262168
  12.9 2.9 %shard_map.109 = (bf16[16,8,32,128]{3,2,1,0:T(8,128)(2,1)S(1)}, f32[16,6,32,128]{3,2,1,0:T(8,128)S(1)}, bf16[6,32,128]{2,1,0:T(8,128)(2,1)}) custom-call(s32[3]{0:T(128)S(1)} %pad_add_fusion.edge_ref, bf16[16,4,32,128]{3,2,1,0:T(8,128)(2,1)S(1)} %bitcast.51, bf16[16,2,32,128]{3,2,1,0:T(8,128)(2,1)S(1)} %collective-permute-done.first_ref, ...), custom_call_target="tpu_custom_call" | custom-call | flops 905969664 | bytes 4022284 | tf_op jit(solution)/shard_map/pallas_call | solution.py:28
  15.8 3.7 %collective-permute-start.2 = (bf16[6,32,128]{2,1,0:T(8,128)(2,1)}, bf16[6,32,128]{2,1,0:T(8,128)(2,1)S(1)}, u32[]{:S(2)}, u32[]{:S(2)}) collective-permute-start(bf16[6,32,128]{2,1,0:T(8,128)(2,1)} %get-tuple-element.19), channel_id=1, source_target_pairs={{0,16},{1,17},{2,18},{3,19},{4,20},{5,21},{6,22},{7,23},{8,24},{9,... | collective-permute-start | bytes 147464 | tf_op jit(solution)/shard_map/ppermute | solution.py:270
  20.6 1.0 %collective-permute-done.2.carry_ref = bf16[6,32,128]{2,1,0:T(8,128)(2,1)S(1)} collective-permute-done((bf16[6,32,128]{2,1,0:T(8,128)(2,1)}, bf16[6,32,128]{2,1,0:T(8,128)(2,1)S(1)}, u32[]{:S(2)}, u32[]{:S(2)}) %collective-permute-start.2) | collective-permute-done | bytes 49184 | tf_op jit(solution)/shard_map/ppermute | solution.py:270
  21.6 1.0 %copy-done.3 = bf16[1,16,4,32,128]{4,3,2,1,0:T(8,128)(2,1)S(1)} copy-done((bf16[1,16,4,32,128]{4,3,2,1,0:T(8,128)(2,1)S(1)}, bf16[1,16,4,32,128]{4,3,2,1,0:T(8,128)(2,1)}, u32[]{:S(2)}) %copy-start.3) | copy-done | bytes 524312
  22.6 2.9 %shard_map.110 = (bf16[16,6,32,128]{3,2,1,0:T(8,128)(2,1)S(1)}, bf16[16,4,32,128]{3,2,1,0:T(8,128)(2,1)}, bf16[16,4,32,128]{3,2,1,0:T(8,128)(2,1)S(1)}, f32[1,128]{1,0:T(1,128)S(1)}) custom-call(f32[16,6,32,128]{3,2,1,0:T(8,128)S(1)} %get-tuple-element.18.local_ref, bf16[6,32,128]{2,1,0:T(8,128)(2,1)S(1)} %collective-permute-done.2.carry_ref, ...), custom_call_target="tpu_custom_call" | custom-call | flops 603979776 | bytes 4809728 | tf_op jit(solution)/shard_map/pallas_call | solution.py:28
  25.5 0.9 %copy-done.1 = bf16[16,6,32,128]{3,2,1,0:T(8,128)(2,1)} copy-done((bf16[16,6,32,128]{3,2,1,0:T(8,128)(2,1)}, bf16[16,6,32,128]{3,2,1,0:T(8,128)(2,1)S(1)}, u32[]{:S(2)}) %copy-start.1) | copy-done | bytes 786456
  27.3 4.6 %collective-permute-start.3 = (bf16[16,2,32,128]{3,2,1,0:T(8,128)(2,1)S(1)}, bf16[16,2,32,128]{3,2,1,0:T(8,128)(2,1)S(1)}, u32[]{:S(2)}, u32[]{:S(2)}) collective-permute-start(bf16[16,2,32,128]{3,2,1,0:T(8,128)(2,1)S(1)} %get-tuple-element.38), channel_id=1, source_target_pairs={{0,4},{4,0},{8,12},{12,8},{1,5},{5,1},{9,13},{13,9},{2,6},{6,2},{1... | collective-permute-start | bytes 786440 | tf_op jit(solution)/shard_map/ppermute | solution.py:262
  33.0 3.4 %collective-permute-done.3.first_ref = bf16[16,2,32,128]{3,2,1,0:T(8,128)(2,1)S(1)} collective-permute-done((bf16[16,2,32,128]{3,2,1,0:T(8,128)(2,1)S(1)}, bf16[16,2,32,128]{3,2,1,0:T(8,128)(2,1)S(1)}, u32[]{:S(2)}, u32[]{:S(2)}) %collective-permute-start.3) | collective-permute-done | bytes 262176 | tf_op jit(solution)/shard_map/ppermute | solution.py:262
  36.5 2.3 %shard_map.111 = (f32[16,6,32,128]{3,2,1,0:T(8,128)S(1)}, bf16[6,32,128]{2,1,0:T(8,128)(2,1)S(1)}) custom-call(s32[3]{0:T(128)S(1)} %pad_add_fusion.edge_ref, bf16[16,4,32,128]{3,2,1,0:T(8,128)(2,1)S(1)} %copy-done.5, bf16[16,2,32,128]{3,2,1,0:T(8,128)(2,1)S(1)} %collective-permute-done.3.first_ref, ...), custom_call_target="tpu_custom_call" | custom-call | flops 905969664 | bytes 2973708 | tf_op jit(solution)/shard_map/pallas_call | solution.py:28
  38.8 1.5 %collective-permute-start.5 = (bf16[6,32,128]{2,1,0:T(8,128)(2,1)S(1)}, bf16[6,32,128]{2,1,0:T(8,128)(2,1)S(1)}, u32[]{:S(2)}, u32[]{:S(2)}) collective-permute-start(bf16[6,32,128]{2,1,0:T(8,128)(2,1)S(1)} %get-tuple-element.23), channel_id=1, source_target_pairs={{16,0},{17,1},{18,2},{19,3},{20,4},{21,5},{22,6},{23,7},{24,8},{25... | collective-permute-start | bytes 147464 | tf_op jit(solution)/shard_map/ppermute | solution.py:287
  40.2 1.0 %shard_map.114 = f32[3,3,128,128]{3,2,1,0:T(8,128)S(1)} custom-call(bf16[16,6,32,128]{3,2,1,0:T(8,128)(2,1)S(1)} %copy-done.2, bf16[16,4,32,128]{3,2,1,0:T(8,128)(2,1)S(1)} %copy-done.5), custom_call_target="tpu_custom_call" | custom-call | flops 603979776 | bytes 1900544 | tf_op jit(solution)/shard_map/pallas_call | solution.py:28
  41.3 3.5 %collective-permute-done.5.back_ref = bf16[6,32,128]{2,1,0:T(8,128)(2,1)S(1)} collective-permute-done((bf16[6,32,128]{2,1,0:T(8,128)(2,1)S(1)}, bf16[6,32,128]{2,1,0:T(8,128)(2,1)S(1)}, u32[]{:S(2)}, u32[]{:S(2)}) %collective-permute-start.5) | collective-permute-done | bytes 49184 | tf_op jit(solution)/shard_map/ppermute | solution.py:287
  44.7 1.0 %shard_map.112 = (bf16[16,6,32,128]{3,2,1,0:T(8,128)(2,1)S(1)}, f32[3,3,128,128]{3,2,1,0:T(8,128)S(1)}, f32[16,1,128]{2,1,0:T(1,128)S(1)}) custom-call(f32[16,6,32,128]{3,2,1,0:T(8,128)S(1)} %get-tuple-element.22.local_ref, bf16[6,32,128]{2,1,0:T(8,128)(2,1)S(1)} %collective-permute-done.5.back_ref, f32[16,1,128]{2,1,0:T(1,128)S(1)} %get-tuple-element.41.reach_ref, ...), custom_call_target="tpu_custom_call" | custom-call | flops 603979776 | bytes 4907008 | tf_op jit(solution)/shard_map/pallas_call | solution.py:28
  45.8 0.9 %copy-done.7 = bf16[16,6,32,128]{3,2,1,0:T(8,128)(2,1)} copy-done((bf16[16,6,32,128]{3,2,1,0:T(8,128)(2,1)}, bf16[16,6,32,128]{3,2,1,0:T(8,128)(2,1)S(1)}, u32[]{:S(2)}) %copy-start.7) | copy-done | bytes 786456
  47.4 1.5 %collective-permute-done.6 = bf16[1184,128]{1,0:T(8,128)(2,1)S(1)} collective-permute-done((bf16[1184,128]{1,0:T(8,128)(2,1)S(1)}, bf16[1184,128]{1,0:T(8,128)(2,1)S(1)}, u32[]{:S(2)}, u32[]{:S(2)}) %collective-permute-start.6) | collective-permute-done | bytes 303136 | tf_op jit(solution)/shard_map/ppermute | solution.py:313
  49.7 2.3 %collective-permute-start.8 = (bf16[296,128]{1,0:T(8,128)(2,1)S(1)}, bf16[296,128]{1,0:T(8,128)(2,1)S(1)}, u32[]{:S(2)}, u32[]{:S(2)}) collective-permute-start(bf16[296,128]{1,0:T(8,128)(2,1)S(1)} %get-tuple-element.36), channel_id=1, source_target_pairs={{0,16},{1,17},{2,18},{3,19},{4,20},{5,21},{6,22},{7,23},{8,24},{9,... | collective-permute-start | bytes 227336 | tf_op jit(solution)/shard_map/ppermute | solution.py:313
  52.6 2.2 %collective-permute-done.9 = bf16[296,128]{1,0:T(8,128)(2,1)S(1)} collective-permute-done((bf16[296,128]{1,0:T(8,128)(2,1)S(1)}, bf16[296,128]{1,0:T(8,128)(2,1)S(1)}, u32[]{:S(2)}, u32[]{:S(2)}) %collective-permute-start.9) | collective-permute-done | bytes 75808 | tf_op jit(solution)/shard_map/ppermute | solution.py:313
  54.8 1.2 %collective-permute-done.8 = bf16[296,128]{1,0:T(8,128)(2,1)S(1)} collective-permute-done((bf16[296,128]{1,0:T(8,128)(2,1)S(1)}, bf16[296,128]{1,0:T(8,128)(2,1)S(1)}, u32[]{:S(2)}, u32[]{:S(2)}) %collective-permute-start.8) | collective-permute-done | bytes 75808 | tf_op jit(solution)/shard_map/ppermute | solution.py:313
  56.5 3.9 %collective-permute-start.10 = (bf16[296,128]{1,0:T(8,128)(2,1)S(1)}, bf16[296,128]{1,0:T(8,128)(2,1)S(1)}, u32[]{:S(2)}, u32[]{:S(2)}) collective-permute-start(bf16[296,128]{1,0:T(8,128)(2,1)S(1)} %add_convert_fusion.2), channel_id=1, source_target_pairs={{0,4},{1,5},{2,6},{3,7},{4,0},{5,1},{6,2},{7,3},{8,12},{9,13},{10,... | collective-permute-start | bytes 227336 | tf_op jit(solution)/shard_map/ppermute | solution.py:313
  60.3 2.4 %collective-permute-done.10 = bf16[296,128]{1,0:T(8,128)(2,1)S(1)} collective-permute-done((bf16[296,128]{1,0:T(8,128)(2,1)S(1)}, bf16[296,128]{1,0:T(8,128)(2,1)S(1)}, u32[]{:S(2)}, u32[]{:S(2)}) %collective-permute-start.10) | collective-permute-done | bytes 75808 | tf_op jit(solution)/shard_map/ppermute | solution.py:313
  62.7 3.3 %collective-permute-start.11 = (bf16[296,128]{1,0:T(8,128)(2,1)S(1)}, bf16[296,128]{1,0:T(8,128)(2,1)S(1)}, u32[]{:S(2)}, u32[]{:S(2)}) collective-permute-start(bf16[296,128]{1,0:T(8,128)(2,1)S(1)} %add_convert_fusion.1), channel_id=1, source_target_pairs={{0,8},{1,9},{2,10},{3,11},{4,12},{5,13},{6,14},{7,15},{8,0},{9,1},... | collective-permute-start | bytes 227336 | tf_op jit(solution)/shard_map/ppermute | solution.py:313
  66.0 2.4 %collective-permute-done.11 = bf16[296,128]{1,0:T(8,128)(2,1)S(1)} collective-permute-done((bf16[296,128]{1,0:T(8,128)(2,1)S(1)}, bf16[296,128]{1,0:T(8,128)(2,1)S(1)}, u32[]{:S(2)}, u32[]{:S(2)}) %collective-permute-start.11) | collective-permute-done | bytes 75808 | tf_op jit(solution)/shard_map/ppermute | solution.py:313
  69.0 1.1 %collective-permute-start.13 = (bf16[296,128]{1,0:T(8,128)(2,1)S(1)}, bf16[296,128]{1,0:T(8,128)(2,1)S(1)}, u32[]{:S(2)}, u32[]{:S(2)}) collective-permute-start(bf16[296,128]{1,0:T(8,128)(2,1)S(1)} %get-tuple-element.31), channel_id=1, source_target_pairs={{0,16},{1,17},{2,18},{3,19},{4,20},{5,21},{6,22},{7,23},{8,24},{9,... | collective-permute-start | bytes 227336 | tf_op jit(solution)/shard_map/ppermute | solution.py:313
  70.1 1.9 %collective-permute-start.14 = (bf16[296,128]{1,0:T(8,128)(2,1)S(1)}, bf16[296,128]{1,0:T(8,128)(2,1)S(1)}, u32[]{:S(2)}, u32[]{:S(2)}) collective-permute-start(bf16[296,128]{1,0:T(8,128)(2,1)S(1)} %get-tuple-element.31), channel_id=1, source_target_pairs={{0,18},{1,19},{2,16},{3,17},{4,22},{5,23},{6,20},{7,21},{8,26},{9,... | collective-permute-start | bytes 227336 | tf_op jit(solution)/shard_map/ppermute | solution.py:313
  72.0 0.9 %collective-permute-done.12 = bf16[296,128]{1,0:T(8,128)(2,1)S(1)} collective-permute-done((bf16[296,128]{1,0:T(8,128)(2,1)S(1)}, bf16[296,128]{1,0:T(8,128)(2,1)S(1)}, u32[]{:S(2)}, u32[]{:S(2)}) %collective-permute-start.12) | collective-permute-done | bytes 75808 | tf_op jit(solution)/shard_map/ppermute | solution.py:313
  73.4 1.9 %collective-permute-done.14 = bf16[296,128]{1,0:T(8,128)(2,1)S(1)} collective-permute-done((bf16[296,128]{1,0:T(8,128)(2,1)S(1)}, bf16[296,128]{1,0:T(8,128)(2,1)S(1)}, u32[]{:S(2)}, u32[]{:S(2)}) %collective-permute-start.14) | collective-permute-done | bytes 75808 | tf_op jit(solution)/shard_map/ppermute | solution.py:313
  75.8 2.0 %shard_map.113 = bf16[16,4,32,128]{3,2,1,0:T(8,128)(2,1)} custom-call(bf16[16,6,32,128]{3,2,1,0:T(8,128)(2,1)S(1)} %copy-done.8, bf16[16,4,32,128]{3,2,1,0:T(8,128)(2,1)S(1)} %copy-done.5, bf16[384,384]{1,0:T(8,128)(2,1)S(1)} %bitcast.59, f32[1,128]{1,0:T(1,128)S(1)} %bitcast.65), custom_call_target="tpu_custom_call" | custom-call | flops 603979776 | bytes 2130432 | tf_op jit(solution)/shard_map/pallas_call | solution.py:28
  78.0 1.1 %fusion = (f32[1152,128]{1,0:T(8,128)}, f32[1152,128]{1,0:T(8,128)}) fusion(bf16[2368,128]{1,0:T(8,128)(2,1)S(1)} %constant_dynamic-update-slice_fusion), kind=kLoop, calls=%fused_computation.32 | loop fusion | bytes 2359296 | tf_op jit(solution)/shard_map/slice | solution.py:459
  (78 shorter events, 11.8 us)
Async XLA Ops:
  0.6 6.5 %copy-start.12 = (bf16[3,3,128,128]{3,2,1,0:T(8,128)(2,1)S(1)}, bf16[3,3,128,128]{3,2,1,0:T(8,128)(2,1)}, u32[]{:S(2)}) copy-start(bf16[3,3,128,128]{3,2,1,0:T(8,128)(2,1)} %param.8) | copy-start | bytes 884740
  0.7 11.3 %copy-start = (bf16[1,16,4,32,128]{4,3,2,1,0:T(8,128)(2,1)S(1)}, bf16[1,16,4,32,128]{4,3,2,1,0:T(8,128)(2,1)}, u32[]{:S(2)}) copy-start(bf16[1,16,4,32,128]{4,3,2,1,0:T(8,128)(2,1)} %param.6) | copy-start | bytes 1572868
  1.8 9.4 %collective-permute-start = (bf16[16,2,32,128]{3,2,1,0:T(8,128)(2,1)S(1)}, bf16[16,2,32,128]{3,2,1,0:T(8,128)(2,1)S(1)}, u32[]{:S(2)}, u32[]{:S(2)}) collective-permute-start(bf16[16,2,32,128]{3,2,1,0:T(8,128)(2,1)S(1)} %get-tuple-element.40), channel_id=1, source_target_pairs={{0,4},{4,0},{8,12},{12,8},{1,5},{5,1},{9,13},{13,9},{2,6},{6,2},{1... | collective-permute-start | bytes 786440 | tf_op jit(solution)/shard_map/ppermute | solution.py:262
  4.9 6.3 %collective-permute-start.1 = (bf16[16,2,32,128]{3,2,1,0:T(8,128)(2,1)S(1)}, bf16[16,2,32,128]{3,2,1,0:T(8,128)(2,1)S(1)}, u32[]{:S(2)}, u32[]{:S(2)}) collective-permute-start(bf16[16,2,32,128]{3,2,1,0:T(8,128)(2,1)S(1)} %get-tuple-element.39), channel_id=1, source_target_pairs={{4,8},{8,4},{5,9},{9,5},{6,10},{10,6},{7,11},{11,7},{20,24},{24,20... | collective-permute-start | bytes 786440 | tf_op jit(solution)/shard_map/ppermute | solution.py:262
  11.2 0.7 copy-start.9
  11.9 1.0 %copy-start.10 = (bf16[16,2,32,128]{3,2,1,0:T(8,128)(2,1)S(1)}, bf16[16,2,32,128]{3,2,1,0:T(8,128)(2,1)}, u32[]{:S(2)}) copy-start(bf16[16,2,32,128]{3,2,1,0:T(8,128)(2,1)} %copy-done.9) | copy-start | bytes 786436
  12.9 6.6 %copy-start.11 = (bf16[3,3,128,128]{3,2,1,0:T(8,128)(2,1)S(1)}, bf16[3,3,128,128]{3,2,1,0:T(8,128)(2,1)}, u32[]{:S(2)}) copy-start(bf16[3,3,128,128]{3,2,1,0:T(8,128)(2,1)} %param.9) | copy-start | bytes 884740
  15.8 5.8 %copy-start.6 = (f32[128]{0:T(128)S(1)}, f32[128]{0:T(128)}, u32[]{:S(2)}) copy-start(f32[128]{0:T(128)} %param.10) | copy-start | bytes 1540
  15.8 5.8 %collective-permute-start.2 = (bf16[6,32,128]{2,1,0:T(8,128)(2,1)}, bf16[6,32,128]{2,1,0:T(8,128)(2,1)S(1)}, u32[]{:S(2)}, u32[]{:S(2)}) collective-permute-start(bf16[6,32,128]{2,1,0:T(8,128)(2,1)} %get-tuple-element.19), channel_id=1, source_target_pairs={{0,16},{1,17},{2,18},{3,19},{4,20},{5,21},{6,22},{7,23},{8,24},{9,... | collective-permute-start | bytes 147464 | tf_op jit(solution)/shard_map/ppermute | solution.py:270
  21.6 1.0 %copy-start.3 = (bf16[1,16,4,32,128]{4,3,2,1,0:T(8,128)(2,1)S(1)}, bf16[1,16,4,32,128]{4,3,2,1,0:T(8,128)(2,1)}, u32[]{:S(2)}) copy-start(bf16[1,16,4,32,128]{4,3,2,1,0:T(8,128)(2,1)} %param.7) | copy-start | bytes 1572868
  25.5 0.9 %copy-start.1 = (bf16[16,6,32,128]{3,2,1,0:T(8,128)(2,1)}, bf16[16,6,32,128]{3,2,1,0:T(8,128)(2,1)S(1)}, u32[]{:S(2)}) copy-start(bf16[16,6,32,128]{3,2,1,0:T(8,128)(2,1)S(1)} %get-tuple-element.25.state_ref) | copy-start | bytes 2359300
  26.4 6.1 %copy-start.14 = (bf16[3,128,3,128]{1,3,2,0:T(8,128)(2,1)S(1)}, bf16[3,128,3,128]{1,3,2,0:T(8,128)(2,1)}, u32[]{:S(2)}) copy-start(bf16[3,128,3,128]{1,3,2,0:T(8,128)(2,1)} %reverse_bitcast_fusion.1) | copy-start | bytes 884740
  26.5 0.8 copy-start.4
  27.3 9.2 %copy-start.5 = (bf16[16,4,32,128]{3,2,1,0:T(8,128)(2,1)S(1)}, bf16[16,4,32,128]{3,2,1,0:T(8,128)(2,1)}, u32[]{:S(2)}) copy-start(bf16[16,4,32,128]{3,2,1,0:T(8,128)(2,1)} %copy-done.4) | copy-start | bytes 1572868
  27.3 9.2 %collective-permute-start.3 = (bf16[16,2,32,128]{3,2,1,0:T(8,128)(2,1)S(1)}, bf16[16,2,32,128]{3,2,1,0:T(8,128)(2,1)S(1)}, u32[]{:S(2)}, u32[]{:S(2)}) collective-permute-start(bf16[16,2,32,128]{3,2,1,0:T(8,128)(2,1)S(1)} %get-tuple-element.38), channel_id=1, source_target_pairs={{0,4},{4,0},{8,12},{12,8},{1,5},{5,1},{9,13},{13,9},{2,6},{6,2},{1... | collective-permute-start | bytes 786440 | tf_op jit(solution)/shard_map/ppermute | solution.py:262
  31.9 4.6 %collective-permute-start.4 = (bf16[16,2,32,128]{3,2,1,0:T(8,128)(2,1)S(1)}, bf16[16,2,32,128]{3,2,1,0:T(8,128)(2,1)S(1)}, u32[]{:S(2)}, u32[]{:S(2)}) collective-permute-start(bf16[16,2,32,128]{3,2,1,0:T(8,128)(2,1)S(1)} %get-tuple-element.37), channel_id=1, source_target_pairs={{4,8},{8,4},{5,9},{9,5},{6,10},{10,6},{7,11},{11,7},{20,24},{24,20... | collective-permute-start | bytes 786440 | tf_op jit(solution)/shard_map/ppermute | solution.py:262
  36.5 3.8 %copy-start.2 = (bf16[16,6,32,128]{3,2,1,0:T(8,128)(2,1)S(1)}, bf16[16,6,32,128]{3,2,1,0:T(8,128)(2,1)}, u32[]{:S(2)}) copy-start(bf16[16,6,32,128]{3,2,1,0:T(8,128)(2,1)} %copy-done.1) | copy-start | bytes 2359300
  38.8 6.0 %collective-permute-start.5 = (bf16[6,32,128]{2,1,0:T(8,128)(2,1)S(1)}, bf16[6,32,128]{2,1,0:T(8,128)(2,1)S(1)}, u32[]{:S(2)}, u32[]{:S(2)}) collective-permute-start(bf16[6,32,128]{2,1,0:T(8,128)(2,1)S(1)} %get-tuple-element.23), channel_id=1, source_target_pairs={{16,0},{17,1},{18,2},{19,3},{20,4},{21,5},{22,6},{23,7},{24,8},{25... | collective-permute-start | bytes 147464 | tf_op jit(solution)/shard_map/ppermute | solution.py:287
  45.8 0.9 %copy-start.7 = (bf16[16,6,32,128]{3,2,1,0:T(8,128)(2,1)}, bf16[16,6,32,128]{3,2,1,0:T(8,128)(2,1)S(1)}, u32[]{:S(2)}) copy-start(bf16[16,6,32,128]{3,2,1,0:T(8,128)(2,1)S(1)} %get-tuple-element.26.adjoint_ref) | copy-start | bytes 2359300
  47.3 1.7 %collective-permute-start.6 = (bf16[1184,128]{1,0:T(8,128)(2,1)S(1)}, bf16[1184,128]{1,0:T(8,128)(2,1)S(1)}, u32[]{:S(2)}, u32[]{:S(2)}) collective-permute-start(bf16[1184,128]{1,0:T(8,128)(2,1)S(1)} %dynamic-slice_convert_fusion), channel_id=1, source_target_pairs={{0,1},{1,0},{2,3},{3,2},{4,5},{5,4},{6,7},{7,6},{8,9},{9,8},{10,11... | collective-permute-start | bytes 909320 | tf_op jit(solution)/shard_map/ppermute | solution.py:313
  49.0 26.5 %copy-start.13 = (bf16[3,3,128,128]{3,2,1,0:T(8,128)(2,1)S(1)}, bf16[3,3,128,128]{3,2,1,0:T(8,128)(2,1)}, u32[]{:S(2)}) copy-start(bf16[3,3,128,128]{3,2,1,0:T(8,128)(2,1)} %param.8) | copy-start | bytes 884740
  49.1 5.8 %collective-permute-start.9 = (bf16[296,128]{1,0:T(8,128)(2,1)S(1)}, bf16[296,128]{1,0:T(8,128)(2,1)S(1)}, u32[]{:S(2)}, u32[]{:S(2)}) collective-permute-start(bf16[296,128]{1,0:T(8,128)(2,1)S(1)} %get-tuple-element.35), channel_id=1, source_target_pairs={{0,18},{1,19},{2,16},{3,17},{4,22},{5,23},{6,20},{7,21},{8,26},{9,... | collective-permute-start | bytes 227336 | tf_op jit(solution)/shard_map/ppermute | solution.py:313
  49.7 6.3 %collective-permute-start.8 = (bf16[296,128]{1,0:T(8,128)(2,1)S(1)}, bf16[296,128]{1,0:T(8,128)(2,1)S(1)}, u32[]{:S(2)}, u32[]{:S(2)}) collective-permute-start(bf16[296,128]{1,0:T(8,128)(2,1)S(1)} %get-tuple-element.36), channel_id=1, source_target_pairs={{0,16},{1,17},{2,18},{3,19},{4,20},{5,21},{6,22},{7,23},{8,24},{9,... | collective-permute-start | bytes 227336 | tf_op jit(solution)/shard_map/ppermute | solution.py:313
  52.1 4.4 %collective-permute-start.7 = (bf16[296,128]{1,0:T(8,128)(2,1)S(1)}, bf16[296,128]{1,0:T(8,128)(2,1)S(1)}, u32[]{:S(2)}, u32[]{:S(2)}) collective-permute-start(bf16[296,128]{1,0:T(8,128)(2,1)S(1)} %get-tuple-element.34), channel_id=1, source_target_pairs={{0,2},{1,3},{2,0},{3,1},{4,6},{5,7},{6,4},{7,5},{8,10},{9,11},{10,... | collective-permute-start | bytes 227336 | tf_op jit(solution)/shard_map/ppermute | solution.py:313
  56.5 6.2 %collective-permute-start.10 = (bf16[296,128]{1,0:T(8,128)(2,1)S(1)}, bf16[296,128]{1,0:T(8,128)(2,1)S(1)}, u32[]{:S(2)}, u32[]{:S(2)}) collective-permute-start(bf16[296,128]{1,0:T(8,128)(2,1)S(1)} %add_convert_fusion.2), channel_id=1, source_target_pairs={{0,4},{1,5},{2,6},{3,7},{4,0},{5,1},{6,2},{7,3},{8,12},{9,13},{10,... | collective-permute-start | bytes 227336 | tf_op jit(solution)/shard_map/ppermute | solution.py:313
  62.7 5.6 %collective-permute-start.11 = (bf16[296,128]{1,0:T(8,128)(2,1)S(1)}, bf16[296,128]{1,0:T(8,128)(2,1)S(1)}, u32[]{:S(2)}, u32[]{:S(2)}) collective-permute-start(bf16[296,128]{1,0:T(8,128)(2,1)S(1)} %add_convert_fusion.1), channel_id=1, source_target_pairs={{0,8},{1,9},{2,10},{3,11},{4,12},{5,13},{6,14},{7,15},{8,0},{9,1},... | collective-permute-start | bytes 227336 | tf_op jit(solution)/shard_map/ppermute | solution.py:313
  68.4 4.4 %collective-permute-start.12 = (bf16[296,128]{1,0:T(8,128)(2,1)S(1)}, bf16[296,128]{1,0:T(8,128)(2,1)S(1)}, u32[]{:S(2)}, u32[]{:S(2)}) collective-permute-start(bf16[296,128]{1,0:T(8,128)(2,1)S(1)} %get-tuple-element.31), channel_id=1, source_target_pairs={{0,2},{1,3},{2,0},{3,1},{4,6},{5,7},{6,4},{7,5},{8,10},{9,11},{10,... | collective-permute-start | bytes 227336 | tf_op jit(solution)/shard_map/ppermute | solution.py:313
  69.0 4.4 %collective-permute-start.13 = (bf16[296,128]{1,0:T(8,128)(2,1)S(1)}, bf16[296,128]{1,0:T(8,128)(2,1)S(1)}, u32[]{:S(2)}, u32[]{:S(2)}) collective-permute-start(bf16[296,128]{1,0:T(8,128)(2,1)S(1)} %get-tuple-element.31), channel_id=1, source_target_pairs={{0,16},{1,17},{2,18},{3,19},{4,20},{5,21},{6,22},{7,23},{8,24},{9,... | collective-permute-start | bytes 227336 | tf_op jit(solution)/shard_map/ppermute | solution.py:313
  70.1 5.3 %collective-permute-start.14 = (bf16[296,128]{1,0:T(8,128)(2,1)S(1)}, bf16[296,128]{1,0:T(8,128)(2,1)S(1)}, u32[]{:S(2)}, u32[]{:S(2)}) collective-permute-start(bf16[296,128]{1,0:T(8,128)(2,1)S(1)} %get-tuple-element.31), channel_id=1, source_target_pairs={{0,18},{1,19},{2,16},{3,17},{4,22},{5,23},{6,20},{7,21},{8,26},{9,... | collective-permute-start | bytes 227336 | tf_op jit(solution)/shard_map/ppermute | solution.py:313
  72.9 2.9 %copy-start.8 = (bf16[16,6,32,128]{3,2,1,0:T(8,128)(2,1)S(1)}, bf16[16,6,32,128]{3,2,1,0:T(8,128)(2,1)}, u32[]{:S(2)}) copy-start(bf16[16,6,32,128]{3,2,1,0:T(8,128)(2,1)} %copy-done.7) | copy-start | bytes 2359300
  75.4 2.6 %collective-permute-start.15 = (bf16[1184,128]{1,0:T(8,128)(2,1)S(1)}, bf16[1184,128]{1,0:T(8,128)(2,1)S(1)}, u32[]{:S(2)}, u32[]{:S(2)}) collective-permute-start(bf16[1184,128]{1,0:T(8,128)(2,1)S(1)} %constant_dynamic-update-slice_fusion.2), channel_id=1, source_target_pairs={{0,1},{1,0},{2,3},{3,2},{4,5},{5,4},{6,7},{7,6},{8,9},{9,8},{10,11... | collective-permute-start | bytes 909320 | tf_op jit(solution)/shard_map/ppermute | solution.py:313

commit v3 on v2

--- a/solution.py
+++ b/solution.py
@@ -11,29 +11,41 @@
 BF = jnp.bfloat16
 F32 = jnp.float32
 VMEM_LIMIT = 24 * 1024 * 1024
+LAYER_GROUP = 8
+LAST_GROUP = 8
+OUTER_GROUP = 16
 GELU_A = math.sqrt(2.0 / math.pi)
 GELU_B = 0.044715
 
 
-def vmem():
-    return pl.BlockSpec(memory_space=pltpu.VMEM)
-
-
-def smem():
-    return pl.BlockSpec(memory_space=pltpu.SMEM)
-
-
-def call(body, outs, ins, scalars, scratch=(), flops=0):
+PLACES = {"s": pltpu.SMEM, "v": pltpu.VMEM, "h": pltpu.HBM}
+
+
+def call(body, outs, ins, places, scratch=(), flops=0):
     moved = sum(math.prod(a.shape) * a.dtype.itemsize for a in list(ins) + list(outs))
+    specs = [pl.BlockSpec(memory_space=PLACES[p]) for p in places]
+    ins = [
+        pltpu.with_memory_space_constraint(a, pltpu.HBM) if p == "h" else a for a, p in zip(ins, places)
+    ]
+    outs = [pltpu.HBM(a.shape, a.dtype) if p == "h" else a for a, p in zip(outs, places[len(ins) :])]
     return pl.pallas_call(
         body,
         out_shape=outs,
-        in_specs=[smem() if n < scalars else vmem() for n in range(len(ins))],
-        out_specs=[vmem() for _ in outs],
+        in_specs=specs[: len(ins)],
+        out_specs=specs[len(ins) :],
         scratch_shapes=list(scratch),
         compiler_params=pltpu.CompilerParams(vmem_limit_bytes=VMEM_LIMIT),
         cost_estimate=pl.CostEstimate(flops=flops, bytes_accessed=moved, transcendentals=0),
     )(*ins)
+
+
+def piece_copy(source, target, sems, n, group):
+    span = pl.ds(n * group, group)
+    return pltpu.make_async_copy(source.at[span], target.at[span], sems.at[n])
+
+
+def held(array):
+    return pltpu.VMEM(array.shape, array.dtype)
 
 
 def shape(dims, dtype):
@@ -110,10 +122,15 @@
     return jnp.concatenate([upper, field[width : count - width], lower], axis=0)
 
 
-def drive_kernel(edge_ref, own_ref, first_ref, second_ref, kernel_ref, lam_ref, wide_ref, local_ref, end_ref):
+def drive_kernel(
+    edge_ref, own_ref, first_ref, second_ref, kernel_ref, lam_ref,
+    kept_ref, local_ref, end_ref, wide_ref, sem,
+):
     frames, rows, cols, _ = own_ref.shape
     state_chans = kernel_ref.shape[1] // 3
     fill_halo(edge_ref, wide_ref, own_ref, first_ref, second_ref)
+    keep = pltpu.make_async_copy(wide_ref, kept_ref, sem)
+    keep.start()
     group = group_of(frames, 16)
     many = (rows + 2) * cols
 
@@ -128,16 +145,26 @@
 
     last = lax.fori_loop(0, frames // group, step, jnp.zeros((many, state_chans), F32))
     end_ref[...] = last.reshape(rows + 2, cols, state_chans).astype(BF)
+    keep.wait()
 
 
 def layer_kernel(
     local_ref, carry_ref, reach_ref, own_ref, cot_ref, kernel_ref, gain_ref,
-    state_ref, act_ref, grad_ref, gain_grad_ref,
+    state_out, act_out, grad_ref, gain_grad_ref,
+    own_in, cot_in, state_ref, act_ref, sems,
 ):
     frames, rows, cols, chans = own_ref.shape
-    group = group_of(frames, 16)
+    group = group_of(frames, LAYER_GROUP)
     many = group * rows * cols
     carry = carry_ref[...].astype(F32)
+    steps = frames // group
+
+    def start(n, _):
+        piece_copy(own_ref, own_in, sems.at[0], n, group).start()
+        piece_copy(cot_ref, cot_in, sems.at[1], n, group).start()
+        return 0
+
+    lax.fori_loop(0, steps, start, 0)
 
     def step(n, total):
         base = n * group
@@ -145,28 +172,41 @@
             [(local_ref[base + k] + reach_ref[base + k] * carry).astype(BF) for k in range(group)]
         )
         state_ref[pl.ds(base, group)] = state
-        own = own_ref[pl.ds(base, group)].reshape(many, chans).astype(F32)
-        pre = conv(state, 0, rows, kernel_ref[...]) + gain_ref[...] * own
+        piece_copy(state_ref, state_out, sems.at[2], n, group).start()
+        flow = conv(state, 0, rows, kernel_ref[...])
+        piece_copy(own_ref, own_in, sems.at[0], n, group).wait()
+        piece_copy(cot_ref, cot_in, sems.at[1], n, group).wait()
+        own = own_in[pl.ds(base, group)].reshape(many, chans).astype(F32)
+        pre = flow + gain_ref[...] * own
         square = pre * pre
         bend = jnp.tanh(GELU_A * (pre + GELU_B * square * pre))
         half = 0.5 * (1.0 + bend)
         slope = half + 0.5 * pre * (1.0 - bend * bend) * (GELU_A * (1.0 + 3.0 * GELU_B * square))
-        grad = cot_ref[pl.ds(base, group)].reshape(many, chans).astype(F32) * slope
+        grad = cot_in[pl.ds(base, group)].reshape(many, chans).astype(F32) * slope
         act_ref[pl.ds(base, group)] = (pre * half).astype(BF).reshape(group, rows, cols, chans)
+        piece_copy(act_ref, act_out, sems.at[3], n, group).start()
         grad_ref[pl.ds(base, group)] = grad.astype(BF).reshape(group, rows, cols, chans)
         return total + jnp.sum((grad * own).reshape(many // 8, 8, chans), axis=0)
 
-    total = lax.fori_loop(0, frames // group, step, jnp.zeros((8, chans), F32))
+    total = lax.fori_loop(0, steps, step, jnp.zeros((8, chans), F32))
     gain_grad_ref[...] = jnp.sum(total, axis=0, keepdims=True)
 
-
-def put_blocks(total, out_ref, scale):
-    left, right = out_ref.shape[2:]
+    def finish(n, _):
+        piece_copy(state_ref, state_out, sems.at[2], n, group).wait()
+        piece_copy(act_ref, act_out, sems.at[3], n, group).wait()
+        return 0
+
+    lax.fori_loop(0, steps, finish, 0)
+
+
+def put_blocks(total_ref, out_ref, scale):
+    left, right = total_ref.shape[0] // 3, total_ref.shape[1] // 3
     for i in range(3):
         for j in range(3):
-            out_ref[i, j] = (
-                total[i * left : (i + 1) * left, j * right : (j + 1) * right] * scale
-            ).astype(out_ref.dtype)
+            at = (3 * i + j) * left
+            out_ref[at : at + left] = (
+                total_ref[i * left : (i + 1) * left, j * right : (j + 1) * right] * scale
+            )
 
 
 def out_grad_kernel(scale, state_ref, grad_ref, out_ref, total_ref):
@@ -182,7 +222,7 @@
         return 0
 
     lax.fori_loop(0, frames // group, step, 0)
-    put_blocks(total_ref[...], out_ref, scale)
+    put_blocks(total_ref, out_ref, scale)
 
 
 def back_kernel(edge_ref, own_ref, first_ref, second_ref, kernel_ref, lam_ref, local_ref, lead_ref, wide_ref):
@@ -206,12 +246,13 @@
 
 
 def in_grad_kernel(
-    scale, decay_scale, local_ref, back_ref, reach_ref, lam_ref, wide_ref, state_ref, carry_ref,
-    adjoint_ref, out_ref, decay_ref, total_ref,
+    scale, decay_scale, blocks, place_ref, local_ref, back_ref, reach_ref, lam_ref, wide_ref, state_ref,
+    carry_ref, other_ref, gain_ref,
+    adjoint_out, sent_ref, kept_ref, total_ref, adjoint_ref, mine_ref, decay_ref, sems,
 ):
     frames, rows_two, cols, chans = local_ref.shape
     rows = rows_two - 2
-    group = group_of(frames, 16)
+    group = group_of(frames, OUTER_GROUP)
     many = rows * cols
     back = back_ref[...].astype(F32)
     total_ref[...] = jnp.zeros_like(total_ref)
@@ -225,20 +266,78 @@
             mine = adjoint[1 : 1 + rows].reshape(many, chans)
             kept.append(mine)
             part = jnp.sum((mine * previous).reshape(many // 8, 8, chans), axis=0)
-            decay_ref[base + k] = jnp.sum(part, axis=0, keepdims=True) * lam_ref[base + k] * decay_scale
+            decay_ref[pl.ds(base + k, 1)] = (
+                jnp.sum(part, axis=0, keepdims=True) * lam_ref[base + k] * decay_scale
+            )
             previous = state_ref[base + k, 1 : 1 + rows].reshape(many, chans).astype(F32)
+        piece_copy(adjoint_ref, adjoint_out, sems, n, group).start()
         left = taps(wide_ref[pl.ds(base, group)], 1, rows)
         total_ref[...] += outer(left, spread(jnp.concatenate(kept, axis=0), cols))
         return previous
 
     before = carry_ref[1 : 1 + rows].reshape(many, chans).astype(F32)
     lax.fori_loop(0, frames // group, step, before)
-    put_blocks(total_ref[...], out_ref, scale)
-
-
-def video_grad_kernel(adjoint_ref, grad_ref, kernel_ref, gain_ref, out_ref):
+    count, full = other_ref.shape[0], mine_ref.shape[0]
+    used = count + blocks * frames
+    put_blocks(total_ref, mine_ref, scale)
+    for n in range(blocks):
+        mine_ref[count + n * frames : count + (n + 1) * frames] = jnp.where(
+            place_ref[1] == n, decay_ref[...], 0.0
+        )
+    if full > used:
+        mine_ref[used:] = jnp.zeros((full - used, chans), F32)
+    row = lax.broadcasted_iota(jnp.int32, (full - count, chans), 0)
+    rest = jnp.where(row == 0, gain_ref[...] * scale, 0.0)
+
+    @pl.when(place_ref[0] == 0)
+    def _():
+        kept_ref[...] = mine_ref[...]
+        sent_ref[:count] = other_ref[...].astype(BF)
+        sent_ref[count:] = rest.astype(BF)
+
+    @pl.when(place_ref[0] != 0)
+    def _():
+        sent_ref[...] = mine_ref[...].astype(BF)
+        kept_ref[:count] = other_ref[...]
+        kept_ref[count:] = rest
+
+    def finish(n, _):
+        piece_copy(adjoint_ref, adjoint_out, sems, n, group).wait()
+        return 0
+
+    lax.fori_loop(0, frames // group, finish, 0)
+
+
+def result_kernel(blocks, place_ref, own_ref, other_ref, in_ref, out_ref, gain_ref, decay_ref):
+    frames, chans = decay_ref.shape
+    size = in_ref.shape[2]
+    count = 9 * size
+
+    def put(first, second):
+        for i in range(3):
+            for j in range(3):
+                at = (3 * i + j) * size
+                in_ref[i, j] = first[at : at + size].astype(F32)
+                out_ref[i, j] = second[at : at + size].astype(F32)
+        gain_ref[...] = second[count : count + 16].astype(F32)[:1]
+        decay = jnp.zeros((frames, chans), F32)
+        for n in range(blocks):
+            slot = first[count + n * frames : count + (n + 1) * frames].astype(F32)
+            decay = jnp.where(place_ref[1] == n, slot, decay)
+        decay_ref[...] = decay
+
+    @pl.when(place_ref[0] == 0)
+    def _():
+        put(own_ref, other_ref)
+
+    @pl.when(place_ref[0] != 0)
+    def _():
+        put(other_ref, own_ref)
+
+
+def video_grad_kernel(adjoint_ref, grad_ref, kernel_ref, gain_ref, video_out, out_ref, sems):
     frames, rows, cols, chans = grad_ref.shape
-    group = group_of(frames, 16)
+    group = group_of(frames, LAST_GROUP)
 
     def step(n, _):
         base = n * group
@@ -247,9 +346,15 @@
         out_ref[pl.ds(base, group)] = (
             (flow + gain_ref[...] * grad).astype(BF).reshape(group, rows, cols, chans)
         )
+        piece_copy(out_ref, video_out, sems, n, group).start()
         return 0
 
+    def finish(n, _):
+        piece_copy(out_ref, video_out, sems, n, group).wait()
+        return 0
+
     lax.fori_loop(0, frames // group, step, 0)
+    lax.fori_loop(0, frames // group, finish, 0)
 
 
 def halo_pair(field, deep):
@@ -296,56 +401,45 @@
     return found.astype(BF)
 
 
-def tree_sum(part):
+def tree_sum(sent, kept):
     axes = ("tm", "rows", "dp")
-    bits, scale = [], 1
+    bits, devices = [], 1
     for axis in reversed(axes):
         size = 1
         while size < lax.axis_size(axis):
-            bits.append((axis, size, size * scale))
+            bits.append((axis, size, size * devices))
             size *= 2
-        scale *= lax.axis_size(axis)
-    near = [b for b in bits if b[0] == "dp"][:2] + [b for b in bits if b[0] == "tm"][:1]
-    far = [b for b in bits if b not in near]
-    devices = scale
+        devices *= lax.axis_size(axis)
+    halves = [b for b in bits if b[0] == "dp"][0]
+    group = [b for b in bits if b[0] == "dp"][1:2] + [b for b in bits if b[0] == "tm"][:1]
+    far = [b for b in bits if b != halves and b not in group]
 
     def swap(value, mask):
         return lax.ppermute(value, axes, [(i, i ^ mask) for i in range(devices)])
 
-    def place(group):
-        spot = 0
-        for n, (axis, mask, _) in enumerate(group):
-            spot = spot + jnp.where((lax.axis_index(axis) & mask) != 0, 1 << n, 0)
-        return spot
-
-    def combined(group, k):
+    def combined(k):
         return sum(mask for n, (_, _, mask) in enumerate(group) if (k >> n) & 1)
 
-    done = []
-    for stage, group in enumerate((near[:1], near[1:])):
-        if not group:
-            continue
-        ways = 1 << len(group)
-        size = part.shape[0] // ways
-        spot = place(group)
-        chunk = lambda k: lax.dynamic_slice_in_dim(part, (spot ^ k) * size, size, axis=0)
-        sent = [chunk(k).astype(BF) for k in range(1, ways)]
-        found = [swap(v, combined(group, k + 1)) for k, v in enumerate(sent)]
-        part = chunk(0)
-        for piece in found:
-            part = part + piece.astype(F32)
-        done.append((stage, group, spot))
-    whole = part.astype(BF)
+    spot = 0
+    for n, (axis, mask, _) in enumerate(group):
+        spot = spot + jnp.where((lax.axis_index(axis) & mask) != 0, 1 << n, 0)
+    ways = 1 << len(group)
+    size = kept.shape[0] // ways
+    half = kept + swap(sent, halves[2]).astype(F32)
+    chunk = lambda k: lax.dynamic_slice_in_dim(half, (spot ^ k) * size, size, axis=0)
+    chunks = lax.optimization_barrier([chunk(0)] + [chunk(k).astype(BF) for k in range(1, ways)])
+    found = [swap(chunks[k], combined(k)) for k in range(1, ways)]
+    total = chunks[0]
+    for piece in found:
+        total = total + piece.astype(F32)
+    total = total.astype(BF)
     for _, _, mask in far:
-        whole = (whole.astype(F32) + swap(whole, mask).astype(F32)).astype(BF)
-    for stage, group, spot in reversed(done):
-        ways, size = 1 << len(group), whole.shape[0]
-        found = [swap(whole, combined(group, k)) for k in range(1, ways)]
-        joined = jnp.zeros((ways * size, whole.shape[1]), BF)
-        for k, piece in enumerate([whole, *found]):
-            joined = lax.dynamic_update_slice_in_dim(joined, piece, (spot ^ k) * size, axis=0)
-        whole = joined
-    return whole
+        total = (total.astype(F32) + swap(total, mask).astype(F32)).astype(BF)
+    found = [total] + [swap(total, combined(k)) for k in range(1, ways)]
+    own = jnp.zeros(sent.shape, BF)
+    for k, piece in enumerate(found):
+        own = lax.dynamic_update_slice_in_dim(own, piece, (spot ^ k) * size, axis=0)
+    return own, swap(own, halves[2])
 
 
 def on_device(video, cotangent, in_kernel, out_kernel, skip_gain, log_decay):
@@ -355,7 +449,7 @@
     devices = sizes["tm"] * sizes["rows"] * sizes["dp"]
     for size in sizes.values():
         assert size & (size - 1) == 0
-    assert seqs == 1 and rows >= 2
+    assert seqs == 1 and rows >= 2 and sizes["dp"] >= 2 and chans == state_chans
     video, cotangent = video[0], cotangent[0]
     band = lax.axis_index("rows")
     edge = jnp.stack(
@@ -384,7 +478,11 @@
             shape((rows + 2, cols, state_chans), BF),
         ],
         [edge, video, first, second, flat(in_kernel), lam],
-        1,
+        "svvvvv" + "hvv",
+        scratch=[
+            pltpu.VMEM((frames, rows + 4, cols, chans), BF),
+            pltpu.SemaphoreType.DMA(()),
+        ],
         flops=each * wide_rows,
     )
     carry = from_earlier(end, totals)
@@ -397,15 +495,22 @@
             shape((1, chans), F32),
         ],
         [local, carry, reach, video, cotangent, flat(out_kernel), gain],
-        0,
+        "vvvhhvv" + "hhvv",
+        scratch=[
+            held(video),
+            held(video),
+            pltpu.VMEM((frames, rows + 2, cols, state_chans), BF),
+            held(video),
+            pltpu.SemaphoreType.DMA((4, frames // group_of(frames, LAYER_GROUP))),
+        ],
         flops=each * narrow_rows,
     )
     first, second = halo_pair(grad, 2)
     (out_part,) = call(
         functools.partial(out_grad_kernel, weight_scale),
-        [shape((3, 3, state_chans, chans), F32)],
+        [shape((9 * state_chans, chans), F32)],
         [state, grad],
-        0,
+        "vvv",
         scratch=[pltpu.VMEM((3 * state_chans, 3 * chans), F32)],
         flops=each * narrow_rows,
     )
@@ -416,56 +521,57 @@
             shape((rows + 2, cols, state_chans), BF),
         ],
         [edge, grad, first, second, flip(out_kernel), lam],
-        1,
+        "svvvvv" + "vv",
         scratch=[pltpu.VMEM((frames, rows + 4, cols, chans), BF)],
         flops=each * wide_rows,
     )
     back = from_later(lead, totals)
-    adjoint, in_part, decay_part = call(
-        functools.partial(in_grad_kernel, weight_scale, decay_scale),
+    blocks = sizes["tm"]
+    full = 9 * chans + blocks * frames
+    full += -full % 64 if full % 32 else 0
+    place = jnp.stack([lax.rem(lax.axis_index("dp"), 2), lax.axis_index("tm")]).astype(jnp.int32)
+    adjoint, sent, kept = call(
+        functools.partial(in_grad_kernel, weight_scale, decay_scale, blocks),
         [
             shape((frames, rows + 2, cols, state_chans), BF),
-            shape((3, 3, chans, state_chans), F32),
-            shape((frames, 1, state_chans), F32),
-        ],
-        [local, back, back_reach, lam, wide, state, carry],
-        0,
-        scratch=[pltpu.VMEM((3 * chans, 3 * state_chans), F32)],
+            shape((full, chans), BF),
+            shape((full, chans), F32),
+        ],
+        [place, local, back, back_reach, lam, wide, state, carry, out_part, gain_part],
+        "svvvvvvvvv" + "hvv",
+        scratch=[
+            pltpu.VMEM((3 * chans, 3 * state_chans), F32),
+            pltpu.VMEM((frames, rows + 2, cols, state_chans), BF),
+            pltpu.VMEM((full, chans), F32),
+            pltpu.VMEM((frames, state_chans), F32),
+            pltpu.SemaphoreType.DMA((frames // group_of(frames, OUTER_GROUP),)),
+        ],
         flops=each * narrow_rows,
     )
     (video_grad,) = call(
         video_grad_kernel,
         [shape(video.shape, BF)],
         [adjoint, grad, flip(in_kernel), gain],
-        0,
+        "vvvv" + "h",
+        scratch=[
+            held(video),
+            pltpu.SemaphoreType.DMA((frames // group_of(frames, LAST_GROUP),)),
+        ],
         flops=each * narrow_rows,
     )
-    block = lax.axis_index("tm")
-    slots = jnp.where(
-        jnp.arange(sizes["tm"])[:, None, None] == block, decay_part[:, 0][None], 0.0
-    ).reshape(-1, state_chans)
-    pieces = [
-        in_part.reshape(-1, state_chans),
-        out_part.reshape(-1, chans),
-        slots,
-        gain_part * weight_scale,
-    ]
-    used = sum(p.shape[0] for p in pieces)
-    pieces.append(jnp.zeros((-used % 64, chans), F32))
-    total = tree_sum(jnp.concatenate(pieces, axis=0)).astype(F32)
-    at = 0
-    sums = []
-    for piece in pieces[:4]:
-        sums.append(lax.slice_in_dim(total, at, at + piece.shape[0], axis=0))
-        at += piece.shape[0]
-    return (
-        act[None],
-        video_grad[None],
-        sums[0].reshape(3, 3, chans, state_chans),
-        sums[1].reshape(3, 3, state_chans, chans),
-        sums[3][0],
-        lax.dynamic_slice_in_dim(sums[2], block * frames, frames, axis=0),
-    )
+    own, other = tree_sum(sent, kept)
+    in_grad, out_grad, gain_grad, decay_grad = call(
+        functools.partial(result_kernel, blocks),
+        [
+            shape((3, 3, chans, state_chans), F32),
+            shape((3, 3, state_chans, chans), F32),
+            shape((1, chans), F32),
+            shape((frames, state_chans), F32),
+        ],
+        [place, own, other],
+        "svv" + "vvvv",
+    )
+    return act[None], video_grad[None], in_grad, out_grad, gain_grad[0], decay_grad
 
 
 def solution(mesh):

time: 80.7 us -> 74.5 us (0.923)
  local copies, waits for them, and re-layouts: 12.3 us -> 3.56 us
  Pallas kernels: 12.2 us -> 14.6 us
  waiting for transfers between devices: 25.1 us -> 26.2 us
    unnamed x34 -> x20, local copies, waits for them, and re-layouts: 5.47 us -> 0.22 us
    pallas_call x6 -> x7, Pallas kernels: 12.2 us -> 14.6 us  [call(): pl.pallas_call(body, out_shape=outs, in_specs=specs[:len(ins)], out_specs...]
    slice x2 -> x0, local copies, waits for them, and re-layouts: 1.09 us -> none  [on_device(): sums.append(lax.slice_in_dim(total, at, at + piece.shape[0], axis=0))]
    transpose x2, local copies, waits for them, and re-layouts: 0.51 us -> 1.47 us  [on_device(): k.transpose(0, 2, 1, 3).reshape(3 * k.shape[2], 3 * k.shape[3])]
  transfers between devices with their start and end apart: 16 -> 16, of which waited for: 13 -> 13; matrix products, arithmetic and copies ran while one was open for 5% -> 3% of each run, Pallas kernels for 4% -> 4%
where the time goes in v3:
time: 74.5 us; the launch traced here: 74.2 us
  starting transfers between devices  28.4 us (38%)
  waiting for transfers between devices  26.2 us (35%)
  Pallas kernels  14.6 us (20%)
  local copies, waits for them, and re-layouts  3.56 us (5%)
  between operations  1.03 us (1%)
    pallas_call x7, Pallas kernels, call(): pl.pallas_call(body, out_shape=outs, in_specs=specs[:len(ins)], out_specs...  14.6 us
    ppermute x10, starting transfers between devices, swap(): return lax.ppermute(value, axes, [(i, i ^ mask) for i in range(devices)])  14.2 us
    ppermute x10, waiting for transfers between devices, swap(): return lax.ppermute(value, axes, [(i, i ^ mask) for i in range(devices)])  13.5 us
    ppermute x2, starting transfers between devices, halo_pair(): lax.ppermute(first, 'rows', swap(0))  7.76 us
    ppermute x2, waiting for transfers between devices, halo_pair(): lax.ppermute(first, 'rows', swap(0))  7.7 us
    ppermute x1, waiting for transfers between devices, from_later(): piece = lax.ppermute(lead, 'tm', pairs)  3.67 us
    ppermute x1, starting transfers between devices, from_earlier(): piece = lax.ppermute(end, 'tm', pairs)  3.59 us
  transfers between devices with their start and end apart: 16, of which 13 were waited for; matrix products, arithmetic and copies ran while one was open for 3% of the time, Pallas kernels for 4%

profile of v3, /device:TPU:0, one launch (start us, length us, event | category | flops | bytes accessed | tf_op | source)
XLA Modules:
  0.0 74.2 jit_solution(14187850459753541329)
XLA Ops:
  0.7 1.1 %dynamic-slice_bitcast_fusion = (bf16[16,2,32,128]{3,2,1,0:T(8,128)(2,1)S(1)}, bf16[16,2,32,128]{3,2,1,0:T(8,128)(2,1)S(1)}) fusion(bf16[1,16,4,32,128]{4,3,2,1,0:T(8,128)(2,1)} %param.6, s32[]{:T(128)S(6)} %select_n.40, s32[]{:T(128)S(6)} %select_n.39), kind=kLoop, calls=%fused_computation.7 | loop fusion | bytes 1048584 | tf_op jit(solution)/shard_map/dynamic_slice | solution.py:365
  1.8 3.1 %collective-permute-start = (bf16[16,2,32,128]{3,2,1,0:T(8,128)(2,1)S(1)}, bf16[16,2,32,128]{3,2,1,0:T(8,128)(2,1)S(1)}, u32[]{:S(2)}, u32[]{:S(2)}) collective-permute-start(bf16[16,2,32,128]{3,2,1,0:T(8,128)(2,1)S(1)} %get-tuple-element.54), channel_id=1, source_target_pairs={{0,4},{4,0},{8,12},{12,8},{1,5},{5,1},{9,13},{13,9},{2,6},{6,2},{1... | collective-permute-start | bytes 786440 | tf_op jit(solution)/shard_map/ppermute | solution.py:367
  4.9 0.7 collective-permute-start.1
  5.7 1.2 %copy.16 = bf16[3,128,3,128]{3,2,1,0:T(4,128)(2,1)S(1)} copy(bf16[3,128,3,128]{3,1,2,0:T(8,128)(2,1)} %bitcast.61) | data formatting | bytes 589824 | tf_op jit(solution)/shard_map/transpose | solution.py:464
  7.0 4.2 %collective-permute-done.first_ref = bf16[16,2,32,128]{3,2,1,0:T(8,128)(2,1)S(1)} collective-permute-done((bf16[16,2,32,128]{3,2,1,0:T(8,128)(2,1)S(1)}, bf16[16,2,32,128]{3,2,1,0:T(8,128)(2,1)S(1)}, u32[]{:S(2)}, u32[]{:S(2)}) %collective-permute-start) | collective-permute-done | bytes 262176 | tf_op jit(solution)/shard_map/ppermute | solution.py:367
  11.2 2.3 %shard_map.109 = (bf16[16,8,32,128]{3,2,1,0:T(8,128)(2,1)}, f32[16,6,32,128]{3,2,1,0:T(8,128)S(1)}, bf16[6,32,128]{2,1,0:T(8,128)(2,1)S(1)}) custom-call(s32[3]{0:T(128)S(1)} %pad_add_fusion.edge_ref, bf16[16,4,32,128]{3,2,1,0:T(8,128)(2,1)S(1)} %bitcast.46, bf16[16,2,32,128]{3,2,1,0:T(8,128)(2,1)S(1)} %collective-permute-done.first_ref, ...), custom_call_target="tpu_custom_call" | custom-call | flops 905969664 | bytes 4022284 | tf_op jit(solution)/shard_map/pallas_call | solution.py:31
  13.6 3.6 %collective-permute-start.2 = (bf16[6,32,128]{2,1,0:T(8,128)(2,1)S(1)}, bf16[6,32,128]{2,1,0:T(8,128)(2,1)S(1)}, u32[]{:S(2)}, u32[]{:S(2)}) collective-permute-start(bf16[6,32,128]{2,1,0:T(8,128)(2,1)S(1)} %get-tuple-element.27), channel_id=1, source_target_pairs={{0,16},{1,17},{2,18},{3,19},{4,20},{5,21},{6,22},{7,23},{8,24},{9,... | collective-permute-start | bytes 147464 | tf_op jit(solution)/shard_map/ppermute | solution.py:375
  17.5 1.4 %collective-permute-done.2.carry_ref = bf16[6,32,128]{2,1,0:T(8,128)(2,1)S(1)} collective-permute-done((bf16[6,32,128]{2,1,0:T(8,128)(2,1)S(1)}, bf16[6,32,128]{2,1,0:T(8,128)(2,1)S(1)}, u32[]{:S(2)}, u32[]{:S(2)}) %collective-permute-start.2) | collective-permute-done | bytes 49184 | tf_op jit(solution)/shard_map/ppermute | solution.py:375
  18.9 3.1 %shard_map.110 = (bf16[16,6,32,128]{3,2,1,0:T(8,128)(2,1)}, bf16[16,4,32,128]{3,2,1,0:T(8,128)(2,1)}, bf16[16,4,32,128]{3,2,1,0:T(8,128)(2,1)S(1)}, f32[1,128]{1,0:T(1,128)S(1)}) custom-call(f32[16,6,32,128]{3,2,1,0:T(8,128)S(1)} %get-tuple-element.26.local_ref, bf16[6,32,128]{2,1,0:T(8,128)(2,1)S(1)} %collective-permute-done.2.carry_ref, ...), custom_call_target="tpu_custom_call" | custom-call | flops 603979776 | bytes 4809728 | tf_op jit(solution)/shard_map/pallas_call | solution.py:31
  22.1 4.6 %collective-permute-start.3 = (bf16[16,2,32,128]{3,2,1,0:T(8,128)(2,1)S(1)}, bf16[16,2,32,128]{3,2,1,0:T(8,128)(2,1)S(1)}, u32[]{:S(2)}, u32[]{:S(2)}) collective-permute-start(bf16[16,2,32,128]{3,2,1,0:T(8,128)(2,1)S(1)} %get-tuple-element.52), channel_id=1, source_target_pairs={{0,4},{4,0},{8,12},{12,8},{1,5},{5,1},{9,13},{13,9},{2,6},{6,2},{1... | collective-permute-start | bytes 786440 | tf_op jit(solution)/shard_map/ppermute | solution.py:367
  26.7 0.7 collective-permute-start.4
  27.8 3.5 %collective-permute-done.3.first_ref = bf16[16,2,32,128]{3,2,1,0:T(8,128)(2,1)S(1)} collective-permute-done((bf16[16,2,32,128]{3,2,1,0:T(8,128)(2,1)S(1)}, bf16[16,2,32,128]{3,2,1,0:T(8,128)(2,1)S(1)}, u32[]{:S(2)}, u32[]{:S(2)}) %collective-permute-start.3) | collective-permute-done | bytes 262176 | tf_op jit(solution)/shard_map/ppermute | solution.py:367
  31.3 2.3 %shard_map.111 = (f32[16,6,32,128]{3,2,1,0:T(8,128)S(1)}, bf16[6,32,128]{2,1,0:T(8,128)(2,1)S(1)}) custom-call(s32[3]{0:T(128)S(1)} %pad_add_fusion.edge_ref, bf16[16,4,32,128]{3,2,1,0:T(8,128)(2,1)S(1)} %get-tuple-element.29.own_ref.grad_ref, bf16[16,2,32,128]{3,2,1,0:T(8,128)(2,1)S(1)} %collective-permute-done.3.first_ref, ...), custom_call_target="tpu_custom_call" | custom-call | flops 905969664 | bytes 2973708 | tf_op jit(solution)/shard_map/pallas_call | solution.py:31
  33.7 1.4 %collective-permute-start.5 = (bf16[6,32,128]{2,1,0:T(8,128)(2,1)S(1)}, bf16[6,32,128]{2,1,0:T(8,128)(2,1)S(1)}, u32[]{:S(2)}, u32[]{:S(2)}) collective-permute-start(bf16[6,32,128]{2,1,0:T(8,128)(2,1)S(1)} %get-tuple-element.31), channel_id=1, source_target_pairs={{16,0},{17,1},{18,2},{19,3},{20,4},{21,5},{22,6},{23,7},{24,8},{25... | collective-permute-start | bytes 147464 | tf_op jit(solution)/shard_map/ppermute | solution.py:392
  35.1 1.0 %shard_map.112.other_ref = f32[1152,128]{1,0:T(8,128)S(1)} custom-call(bf16[16,6,32,128]{3,2,1,0:T(8,128)(2,1)S(1)} %copy-done.2, bf16[16,4,32,128]{3,2,1,0:T(8,128)(2,1)S(1)} %get-tuple-element.29.own_ref.grad_ref), custom_call_target="tpu_custom_call" | custom-call | flops 603979776 | bytes 1900544 | tf_op jit(solution)/shard_map/pallas_call | solution.py:31
  36.1 3.7 %collective-permute-done.5.back_ref = bf16[6,32,128]{2,1,0:T(8,128)(2,1)S(1)} collective-permute-done((bf16[6,32,128]{2,1,0:T(8,128)(2,1)S(1)}, bf16[6,32,128]{2,1,0:T(8,128)(2,1)S(1)}, u32[]{:S(2)}, u32[]{:S(2)}) %collective-permute-start.5) | collective-permute-done | bytes 49184 | tf_op jit(solution)/shard_map/ppermute | solution.py:392
  39.8 2.2 %shard_map.113 = (bf16[16,6,32,128]{3,2,1,0:T(8,128)(2,1)}, bf16[1184,128]{1,0:T(8,128)(2,1)S(1)}, f32[1184,128]{1,0:T(8,128)S(1)}) custom-call(s32[2]{0:T(128)S(1)} %pad_add_fusion.1.place_ref, f32[16,6,32,128]{3,2,1,0:T(8,128)S(1)} %get-tuple-element.30.local_ref, bf16[6,32,128]{2,1,0:T(8,128)(2,1)S(1)} %collective-permute-done.5.back_ref, ...), custom_call_target="tpu_custom_call" | custom-call | flops 603979776 | bytes 5808648 | tf_op jit(solution)/shard_map/pallas_call | solution.py:31
  42.1 1.5 %collective-permute-done.6 = bf16[1184,128]{1,0:T(8,128)(2,1)S(1)} collective-permute-done((bf16[1184,128]{1,0:T(8,128)(2,1)S(1)}, bf16[1184,128]{1,0:T(8,128)(2,1)S(1)}, u32[]{:S(2)}, u32[]{:S(2)}) %collective-permute-start.6) | collective-permute-done | bytes 303136 | tf_op jit(solution)/shard_map/ppermute | solution.py:418
  43.8 0.7 collective-permute-start.9
  44.5 2.3 %collective-permute-start.8 = (bf16[296,128]{1,0:T(8,128)(2,1)S(1)}, bf16[296,128]{1,0:T(8,128)(2,1)S(1)}, u32[]{:S(2)}, u32[]{:S(2)}) collective-permute-start(bf16[296,128]{1,0:T(8,128)(2,1)S(1)} %get-tuple-element.40), channel_id=1, source_target_pairs={{0,16},{1,17},{2,18},{3,19},{4,20},{5,21},{6,22},{7,23},{8,24},{9,... | collective-permute-start | bytes 227336 | tf_op jit(solution)/shard_map/ppermute | solution.py:418
  47.4 2.2 %collective-permute-done.9 = bf16[296,128]{1,0:T(8,128)(2,1)S(1)} collective-permute-done((bf16[296,128]{1,0:T(8,128)(2,1)S(1)}, bf16[296,128]{1,0:T(8,128)(2,1)S(1)}, u32[]{:S(2)}, u32[]{:S(2)}) %collective-permute-start.9) | collective-permute-done | bytes 75808 | tf_op jit(solution)/shard_map/ppermute | solution.py:418
  49.6 1.2 %collective-permute-done.8 = bf16[296,128]{1,0:T(8,128)(2,1)S(1)} collective-permute-done((bf16[296,128]{1,0:T(8,128)(2,1)S(1)}, bf16[296,128]{1,0:T(8,128)(2,1)S(1)}, u32[]{:S(2)}, u32[]{:S(2)}) %collective-permute-start.8) | collective-permute-done | bytes 75808 | tf_op jit(solution)/shard_map/ppermute | solution.py:418
  51.2 3.7 %collective-permute-start.10 = (bf16[296,128]{1,0:T(8,128)(2,1)S(1)}, bf16[296,128]{1,0:T(8,128)(2,1)S(1)}, u32[]{:S(2)}, u32[]{:S(2)}) collective-permute-start(bf16[296,128]{1,0:T(8,128)(2,1)S(1)} %add_convert_fusion.2), channel_id=1, source_target_pairs={{0,4},{1,5},{2,6},{3,7},{4,0},{5,1},{6,2},{7,3},{8,12},{9,13},{10,... | collective-permute-start | bytes 227336 | tf_op jit(solution)/shard_map/ppermute | solution.py:418
  55.0 2.4 %collective-permute-done.10 = bf16[296,128]{1,0:T(8,128)(2,1)S(1)} collective-permute-done((bf16[296,128]{1,0:T(8,128)(2,1)S(1)}, bf16[296,128]{1,0:T(8,128)(2,1)S(1)}, u32[]{:S(2)}, u32[]{:S(2)}) %collective-permute-start.10) | collective-permute-done | bytes 75808 | tf_op jit(solution)/shard_map/ppermute | solution.py:418
  57.4 3.3 %collective-permute-start.11 = (bf16[296,128]{1,0:T(8,128)(2,1)S(1)}, bf16[296,128]{1,0:T(8,128)(2,1)S(1)}, u32[]{:S(2)}, u32[]{:S(2)}) collective-permute-start(bf16[296,128]{1,0:T(8,128)(2,1)S(1)} %add_convert_fusion.1), channel_id=1, source_target_pairs={{0,8},{1,9},{2,10},{3,11},{4,12},{5,13},{6,14},{7,15},{8,0},{9,1},... | collective-permute-start | bytes 227336 | tf_op jit(solution)/shard_map/ppermute | solution.py:418
  60.6 2.4 %collective-permute-done.11 = bf16[296,128]{1,0:T(8,128)(2,1)S(1)} collective-permute-done((bf16[296,128]{1,0:T(8,128)(2,1)S(1)}, bf16[296,128]{1,0:T(8,128)(2,1)S(1)}, u32[]{:S(2)}, u32[]{:S(2)}) %collective-permute-start.11) | collective-permute-done | bytes 75808 | tf_op jit(solution)/shard_map/ppermute | solution.py:418
  63.7 1.1 %collective-permute-start.13 = (bf16[296,128]{1,0:T(8,128)(2,1)S(1)}, bf16[296,128]{1,0:T(8,128)(2,1)S(1)}, u32[]{:S(2)}, u32[]{:S(2)}) collective-permute-start(bf16[296,128]{1,0:T(8,128)(2,1)S(1)} %get-tuple-element.47), channel_id=1, source_target_pairs={{0,16},{1,17},{2,18},{3,19},{4,20},{5,21},{6,22},{7,23},{8,24},{9,... | collective-permute-start | bytes 227336 | tf_op jit(solution)/shard_map/ppermute | solution.py:418
  64.8 1.9 %collective-permute-start.14 = (bf16[296,128]{1,0:T(8,128)(2,1)S(1)}, bf16[296,128]{1,0:T(8,128)(2,1)S(1)}, u32[]{:S(2)}, u32[]{:S(2)}) collective-permute-start(bf16[296,128]{1,0:T(8,128)(2,1)S(1)} %get-tuple-element.47), channel_id=1, source_target_pairs={{0,18},{1,19},{2,16},{3,17},{4,22},{5,23},{6,20},{7,21},{8,26},{9,... | collective-permute-start | bytes 227336 | tf_op jit(solution)/shard_map/ppermute | solution.py:418
  66.6 0.9 %collective-permute-done.12 = bf16[296,128]{1,0:T(8,128)(2,1)S(1)} collective-permute-done((bf16[296,128]{1,0:T(8,128)(2,1)S(1)}, bf16[296,128]{1,0:T(8,128)(2,1)S(1)}, u32[]{:S(2)}, u32[]{:S(2)}) %collective-permute-start.12) | collective-permute-done | bytes 75808 | tf_op jit(solution)/shard_map/ppermute | solution.py:418
  68.1 2.0 %collective-permute-done.14 = bf16[296,128]{1,0:T(8,128)(2,1)S(1)} collective-permute-done((bf16[296,128]{1,0:T(8,128)(2,1)S(1)}, bf16[296,128]{1,0:T(8,128)(2,1)S(1)}, u32[]{:S(2)}, u32[]{:S(2)}) %collective-permute-start.14) | collective-permute-done | bytes 75808 | tf_op jit(solution)/shard_map/ppermute | solution.py:418
  70.5 2.1 %shard_map.114 = bf16[16,4,32,128]{3,2,1,0:T(8,128)(2,1)} custom-call(bf16[16,6,32,128]{3,2,1,0:T(8,128)(2,1)S(1)} %copy-done.4, bf16[16,4,32,128]{3,2,1,0:T(8,128)(2,1)S(1)} %get-tuple-element.29.own_ref.grad_ref, bf16[384,384]{1,0:T(8,128)(2,1)S(1)} %bitcast.50, f32[1,128]{1,0:T(1,128)S(1)} %bitcast.55), custom_call_target="tpu_custom_call" | custom-call | flops 603979776 | bytes 2130432 | tf_op jit(solution)/shard_map/pallas_call | solution.py:31
  72.5 1.6 %shard_map.115 = (f32[3,3,128,128]{3,2,1,0:T(8,128)}, f32[3,3,128,128]{3,2,1,0:T(8,128)}, f32[1,128]{1,0:T(1,128)}, f32[16,128]{1,0:T(8,128)}) custom-call(s32[2]{0:T(128)S(1)} %pad_add_fusion.1.place_ref, bf16[1184,128]{1,0:T(8,128)(2,1)S(1)} %constant_dynamic-update-slice_fusion.own_ref, bf16[1184,128]{1,0:T(8,128)(2,1)S(1)} %collective-permute-done.15.other_ref), custom_call_target="tpu_custom_call" | custom-call | bytes 1794568 | tf_op jit(solution)/shard_map/pallas_call | solution.py:31
  (51 shorter events, 3.9 us)
Async XLA Ops:
  0.6 10.6 %copy-start = (bf16[1,16,4,32,128]{4,3,2,1,0:T(8,128)(2,1)S(1)}, bf16[1,16,4,32,128]{4,3,2,1,0:T(8,128)(2,1)}, u32[]{:S(2)}) copy-start(bf16[1,16,4,32,128]{4,3,2,1,0:T(8,128)(2,1)} %param.6) | copy-start | bytes 1572868
  0.6 6.3 %copy-start.7 = (f32[16,128]{1,0:T(8,128)S(1)}, f32[16,128]{1,0:T(8,128)}, u32[]{:S(2)}) copy-start(f32[16,128]{1,0:T(8,128)} %param.11) | copy-start | bytes 24580
  1.8 9.4 %collective-permute-start = (bf16[16,2,32,128]{3,2,1,0:T(8,128)(2,1)S(1)}, bf16[16,2,32,128]{3,2,1,0:T(8,128)(2,1)S(1)}, u32[]{:S(2)}, u32[]{:S(2)}) collective-permute-start(bf16[16,2,32,128]{3,2,1,0:T(8,128)(2,1)S(1)} %get-tuple-element.54), channel_id=1, source_target_pairs={{0,4},{4,0},{8,12},{12,8},{1,5},{5,1},{9,13},{13,9},{2,6},{6,2},{1... | collective-permute-start | bytes 786440 | tf_op jit(solution)/shard_map/ppermute | solution.py:367
  4.9 6.3 %collective-permute-start.1 = (bf16[16,2,32,128]{3,2,1,0:T(8,128)(2,1)S(1)}, bf16[16,2,32,128]{3,2,1,0:T(8,128)(2,1)S(1)}, u32[]{:S(2)}, u32[]{:S(2)}) collective-permute-start(bf16[16,2,32,128]{3,2,1,0:T(8,128)(2,1)S(1)} %get-tuple-element.53), channel_id=1, source_target_pairs={{4,8},{8,4},{5,9},{9,5},{6,10},{10,6},{7,11},{11,7},{20,24},{24,20... | collective-permute-start | bytes 786440 | tf_op jit(solution)/shard_map/ppermute | solution.py:367
  11.2 6.0 %copy-start.5 = (bf16[3,3,128,128]{3,2,1,0:T(8,128)(2,1)S(1)}, bf16[3,3,128,128]{3,2,1,0:T(8,128)(2,1)}, u32[]{:S(2)}) copy-start(bf16[3,3,128,128]{3,2,1,0:T(8,128)(2,1)} %param.9) | copy-start | bytes 884740
  11.2 7.7 %copy-start.3 = (f32[128]{0:T(128)S(1)}, f32[128]{0:T(128)}, u32[]{:S(2)}) copy-start(f32[128]{0:T(128)} %param.10) | copy-start | bytes 1540
  13.6 5.3 %collective-permute-start.2 = (bf16[6,32,128]{2,1,0:T(8,128)(2,1)S(1)}, bf16[6,32,128]{2,1,0:T(8,128)(2,1)S(1)}, u32[]{:S(2)}, u32[]{:S(2)}) collective-permute-start(bf16[6,32,128]{2,1,0:T(8,128)(2,1)S(1)} %get-tuple-element.27), channel_id=1, source_target_pairs={{0,16},{1,17},{2,18},{3,19},{4,20},{5,21},{6,22},{7,23},{8,24},{9,... | collective-permute-start | bytes 147464 | tf_op jit(solution)/shard_map/ppermute | solution.py:375
  22.1 9.2 %collective-permute-start.3 = (bf16[16,2,32,128]{3,2,1,0:T(8,128)(2,1)S(1)}, bf16[16,2,32,128]{3,2,1,0:T(8,128)(2,1)S(1)}, u32[]{:S(2)}, u32[]{:S(2)}) collective-permute-start(bf16[16,2,32,128]{3,2,1,0:T(8,128)(2,1)S(1)} %get-tuple-element.52), channel_id=1, source_target_pairs={{0,4},{4,0},{8,12},{12,8},{1,5},{5,1},{9,13},{13,9},{2,6},{6,2},{1... | collective-permute-start | bytes 786440 | tf_op jit(solution)/shard_map/ppermute | solution.py:367
  26.7 4.6 %collective-permute-start.4 = (bf16[16,2,32,128]{3,2,1,0:T(8,128)(2,1)S(1)}, bf16[16,2,32,128]{3,2,1,0:T(8,128)(2,1)S(1)}, u32[]{:S(2)}, u32[]{:S(2)}) collective-permute-start(bf16[16,2,32,128]{3,2,1,0:T(8,128)(2,1)S(1)} %get-tuple-element.51), channel_id=1, source_target_pairs={{4,8},{8,4},{5,9},{9,5},{6,10},{10,6},{7,11},{11,7},{20,24},{24,20... | collective-permute-start | bytes 786440 | tf_op jit(solution)/shard_map/ppermute | solution.py:367
  31.3 3.8 %copy-start.2 = (bf16[16,6,32,128]{3,2,1,0:T(8,128)(2,1)S(1)}, bf16[16,6,32,128]{3,2,1,0:T(8,128)(2,1)}, u32[]{:S(2)}) copy-start(bf16[16,6,32,128]{3,2,1,0:T(8,128)(2,1)} %get-tuple-element.33.state_ref) | copy-start | bytes 2359300
  33.6 6.1 %copy-start.1 = (bf16[16,8,32,128]{3,2,1,0:T(8,128)(2,1)S(1)}, bf16[16,8,32,128]{3,2,1,0:T(8,128)(2,1)}, u32[]{:S(2)}) copy-start(bf16[16,8,32,128]{3,2,1,0:T(8,128)(2,1)} %get-tuple-element.32.wide_ref) | copy-start | bytes 3145732
  33.7 6.1 %collective-permute-start.5 = (bf16[6,32,128]{2,1,0:T(8,128)(2,1)S(1)}, bf16[6,32,128]{2,1,0:T(8,128)(2,1)S(1)}, u32[]{:S(2)}, u32[]{:S(2)}) collective-permute-start(bf16[6,32,128]{2,1,0:T(8,128)(2,1)S(1)} %get-tuple-element.31), channel_id=1, source_target_pairs={{16,0},{17,1},{18,2},{19,3},{20,4},{21,5},{22,6},{23,7},{24,8},{25... | collective-permute-start | bytes 147464 | tf_op jit(solution)/shard_map/ppermute | solution.py:392
  42.0 1.7 %collective-permute-start.6 = (bf16[1184,128]{1,0:T(8,128)(2,1)S(1)}, bf16[1184,128]{1,0:T(8,128)(2,1)S(1)}, u32[]{:S(2)}, u32[]{:S(2)}) collective-permute-start(bf16[1184,128]{1,0:T(8,128)(2,1)S(1)} %get-tuple-element.37), channel_id=1, source_target_pairs={{0,1},{1,0},{2,3},{3,2},{4,5},{5,4},{6,7},{7,6},{8,9},{9,8},{10,11... | collective-permute-start | bytes 909320 | tf_op jit(solution)/shard_map/ppermute | solution.py:418
  43.7 26.4 %copy-start.6 = (bf16[3,3,128,128]{3,2,1,0:T(8,128)(2,1)S(1)}, bf16[3,3,128,128]{3,2,1,0:T(8,128)(2,1)}, u32[]{:S(2)}) copy-start(bf16[3,3,128,128]{3,2,1,0:T(8,128)(2,1)} %param.8) | copy-start | bytes 884740
  43.8 5.8 %collective-permute-start.9 = (bf16[296,128]{1,0:T(8,128)(2,1)S(1)}, bf16[296,128]{1,0:T(8,128)(2,1)S(1)}, u32[]{:S(2)}, u32[]{:S(2)}) collective-permute-start(bf16[296,128]{1,0:T(8,128)(2,1)S(1)} %get-tuple-element.41), channel_id=1, source_target_pairs={{0,18},{1,19},{2,16},{3,17},{4,22},{5,23},{6,20},{7,21},{8,26},{9,... | collective-permute-start | bytes 227336 | tf_op jit(solution)/shard_map/ppermute | solution.py:418
  44.5 6.3 %collective-permute-start.8 = (bf16[296,128]{1,0:T(8,128)(2,1)S(1)}, bf16[296,128]{1,0:T(8,128)(2,1)S(1)}, u32[]{:S(2)}, u32[]{:S(2)}) collective-permute-start(bf16[296,128]{1,0:T(8,128)(2,1)S(1)} %get-tuple-element.40), channel_id=1, source_target_pairs={{0,16},{1,17},{2,18},{3,19},{4,20},{5,21},{6,22},{7,23},{8,24},{9,... | collective-permute-start | bytes 227336 | tf_op jit(solution)/shard_map/ppermute | solution.py:418
  46.8 4.4 %collective-permute-start.7 = (bf16[296,128]{1,0:T(8,128)(2,1)S(1)}, bf16[296,128]{1,0:T(8,128)(2,1)S(1)}, u32[]{:S(2)}, u32[]{:S(2)}) collective-permute-start(bf16[296,128]{1,0:T(8,128)(2,1)S(1)} %get-tuple-element.39), channel_id=1, source_target_pairs={{0,2},{1,3},{2,0},{3,1},{4,6},{5,7},{6,4},{7,5},{8,10},{9,11},{10,... | collective-permute-start | bytes 227336 | tf_op jit(solution)/shard_map/ppermute | solution.py:418
  51.2 6.1 %collective-permute-start.10 = (bf16[296,128]{1,0:T(8,128)(2,1)S(1)}, bf16[296,128]{1,0:T(8,128)(2,1)S(1)}, u32[]{:S(2)}, u32[]{:S(2)}) collective-permute-start(bf16[296,128]{1,0:T(8,128)(2,1)S(1)} %add_convert_fusion.2), channel_id=1, source_target_pairs={{0,4},{1,5},{2,6},{3,7},{4,0},{5,1},{6,2},{7,3},{8,12},{9,13},{10,... | collective-permute-start | bytes 227336 | tf_op jit(solution)/shard_map/ppermute | solution.py:418
  57.4 13.1 %copy-start.4 = (bf16[16,6,32,128]{3,2,1,0:T(8,128)(2,1)S(1)}, bf16[16,6,32,128]{3,2,1,0:T(8,128)(2,1)}, u32[]{:S(2)}) copy-start(bf16[16,6,32,128]{3,2,1,0:T(8,128)(2,1)} %get-tuple-element.35.adjoint_ref) | copy-start | bytes 2359300
  57.4 5.6 %collective-permute-start.11 = (bf16[296,128]{1,0:T(8,128)(2,1)S(1)}, bf16[296,128]{1,0:T(8,128)(2,1)S(1)}, u32[]{:S(2)}, u32[]{:S(2)}) collective-permute-start(bf16[296,128]{1,0:T(8,128)(2,1)S(1)} %add_convert_fusion.1), channel_id=1, source_target_pairs={{0,8},{1,9},{2,10},{3,11},{4,12},{5,13},{6,14},{7,15},{8,0},{9,1},... | collective-permute-start | bytes 227336 | tf_op jit(solution)/shard_map/ppermute | solution.py:418
  63.1 4.4 %collective-permute-start.12 = (bf16[296,128]{1,0:T(8,128)(2,1)S(1)}, bf16[296,128]{1,0:T(8,128)(2,1)S(1)}, u32[]{:S(2)}, u32[]{:S(2)}) collective-permute-start(bf16[296,128]{1,0:T(8,128)(2,1)S(1)} %get-tuple-element.47), channel_id=1, source_target_pairs={{0,2},{1,3},{2,0},{3,1},{4,6},{5,7},{6,4},{7,5},{8,10},{9,11},{10,... | collective-permute-start | bytes 227336 | tf_op jit(solution)/shard_map/ppermute | solution.py:418
  63.7 4.4 %collective-permute-start.13 = (bf16[296,128]{1,0:T(8,128)(2,1)S(1)}, bf16[296,128]{1,0:T(8,128)(2,1)S(1)}, u32[]{:S(2)}, u32[]{:S(2)}) collective-permute-start(bf16[296,128]{1,0:T(8,128)(2,1)S(1)} %get-tuple-element.47), channel_id=1, source_target_pairs={{0,16},{1,17},{2,18},{3,19},{4,20},{5,21},{6,22},{7,23},{8,24},{9,... | collective-permute-start | bytes 227336 | tf_op jit(solution)/shard_map/ppermute | solution.py:418
  64.8 5.3 %collective-permute-start.14 = (bf16[296,128]{1,0:T(8,128)(2,1)S(1)}, bf16[296,128]{1,0:T(8,128)(2,1)S(1)}, u32[]{:S(2)}, u32[]{:S(2)}) collective-permute-start(bf16[296,128]{1,0:T(8,128)(2,1)S(1)} %get-tuple-element.47), channel_id=1, source_target_pairs={{0,18},{1,19},{2,16},{3,17},{4,22},{5,23},{6,20},{7,21},{8,26},{9,... | collective-permute-start | bytes 227336 | tf_op jit(solution)/shard_map/ppermute | solution.py:418
  70.0 2.5 %collective-permute-start.15 = (bf16[1184,128]{1,0:T(8,128)(2,1)S(1)}, bf16[1184,128]{1,0:T(8,128)(2,1)S(1)}, u32[]{:S(2)}, u32[]{:S(2)}) collective-permute-start(bf16[1184,128]{1,0:T(8,128)(2,1)S(1)} %constant_dynamic-update-slice_fusion.own_ref), channel_id=1, source_target_pairs={{0,1},{1,0},{2,3},{3,2},{4,5},{5,4},{6,7},{7,6},{8,9},{9,8},{10,11... | collective-permute-start | bytes 909320 | tf_op jit(solution)/shard_map/ppermute | solution.py:418

commit v4 on v3

--- a/solution.py
+++ b/solution.py
@@ -14,6 +14,8 @@
 LAYER_GROUP = 8
 LAST_GROUP = 8
 OUTER_GROUP = 16
+NEAR_GROUP = 8
+SCAN_GROUP = 4
 GELU_A = math.sqrt(2.0 / math.pi)
 GELU_B = 0.044715
 
@@ -21,7 +23,7 @@
 PLACES = {"s": pltpu.SMEM, "v": pltpu.VMEM, "h": pltpu.HBM}
 
 
-def call(body, outs, ins, places, scratch=(), flops=0):
+def call(body, outs, ins, places, scratch=(), flops=0, aliases=()):
     moved = sum(math.prod(a.shape) * a.dtype.itemsize for a in list(ins) + list(outs))
     specs = [pl.BlockSpec(memory_space=PLACES[p]) for p in places]
     ins = [
@@ -34,6 +36,7 @@
         in_specs=specs[: len(ins)],
         out_specs=specs[len(ins) :],
         scratch_shapes=list(scratch),
+        input_output_aliases=dict(aliases),
         compiler_params=pltpu.CompilerParams(vmem_limit_bytes=VMEM_LIMIT),
         cost_estimate=pl.CostEstimate(flops=flops, bytes_accessed=moved, transcendentals=0),
     )(*ins)
@@ -107,44 +110,94 @@
     return size
 
 
-def fill_halo(edge_ref, wide_ref, own_ref, first_ref, second_ref):
+def fill_halo(wide_ref, own_ref, first_ref, second_ref):
     rows, deep = own_ref.shape[1], first_ref.shape[1]
-    odd = edge_ref[2] == 1
+    odd = lax.rem(lax.axis_index("rows"), 2) == 1
     wide_ref[:, deep : deep + rows] = own_ref[...]
     wide_ref[:, pl.ds(jnp.where(odd, 0, rows + deep), deep)] = first_ref[...]
     wide_ref[:, pl.ds(jnp.where(odd, rows + deep, 0), deep)] = second_ref[...]
 
 
-def inside(edge_ref, field, width):
+def inside(field, width):
     count = field.shape[0]
-    upper = jnp.where(edge_ref[0] == 1, field[:width], 0.0)
-    lower = jnp.where(edge_ref[1] == 1, field[count - width :], 0.0)
+    upper = jnp.where(lax.axis_index("rows") > 0, field[:width], 0.0)
+    lower = jnp.where(lax.axis_index("rows") < lax.axis_size("rows") - 1, field[count - width :], 0.0)
     return jnp.concatenate([upper, field[width : count - width], lower], axis=0)
 
 
+def near_kernel(own_ref, kernel_ref, near_ref, wide_ref):
+    frames, rows, cols, chans = own_ref.shape
+    group = group_of(frames, NEAR_GROUP)
+    none = jnp.zeros((group, 2, cols, chans), BF)
+
+    def step(n, _):
+        span = pl.ds(n * group, group)
+        wide_ref[:, :2] = none
+        wide_ref[:, 2 : 2 + rows] = own_ref[span]
+        wide_ref[:, 2 + rows :] = none
+        near = conv(wide_ref[...], 0, rows + 2, kernel_ref[...])
+        near_ref[span] = near.reshape(group, rows + 2, cols, near.shape[1])
+        return 0
+
+    lax.fori_loop(0, frames // group, step, 0)
+
+
+def halo_part(first_ref, second_ref, kernel_ref, upper_ref, lower_ref):
+    frames, deep, cols, chans = first_ref.shape
+    state_chans = kernel_ref.shape[1] // 3
+    odd = lax.rem(lax.axis_index("rows"), 2) == 1
+
+    def put(out_ref, left, right, weights):
+        pair = jnp.concatenate([left, right], axis=3).reshape(frames * deep * cols, 2 * chans)
+        wide = jnp.dot(pair, weights, preferred_element_type=F32)
+        column = columns(wide.shape[0], cols, state_chans)
+        out_ref[...] = (
+            wide[:, state_chans : 2 * state_chans]
+            + from_left(wide[:, :state_chans], column)
+            + from_right(wide[:, 2 * state_chans :], column, cols)
+        ).reshape(frames, deep, cols, state_chans)
+
+    def both(above_ref, below_ref):
+        none = jnp.zeros((frames, 1, cols, chans), BF)
+        above, below = above_ref[...], below_ref[...]
+        put(upper_ref, above, jnp.concatenate([above[:, 1:], none], axis=1), kernel_ref[: 2 * chans])
+        put(lower_ref, jnp.concatenate([none, below[:, :1]], axis=1), below, kernel_ref[chans:])
+
+    @pl.when(odd)
+    def _():
+        both(first_ref, second_ref)
+
+    @pl.when(jnp.logical_not(odd))
+    def _():
+        both(second_ref, first_ref)
+
+
+def whole_rows(near, upper, lower):
+    count, cols, chans = near.shape
+    field = jnp.concatenate([near[:2] + upper, near[2 : count - 2], near[count - 2 :] + lower], axis=0)
+    return inside(field.reshape(count * cols, chans), cols)
+
+
 def drive_kernel(
-    edge_ref, own_ref, first_ref, second_ref, kernel_ref, lam_ref,
-    kept_ref, local_ref, end_ref, wide_ref, sem,
+    near_ref, own_ref, first_ref, second_ref, kernel_ref, lam_ref,
+    kept_ref, local_ref, end_ref, wide_ref, upper_ref, lower_ref, sem,
 ):
-    frames, rows, cols, _ = own_ref.shape
-    state_chans = kernel_ref.shape[1] // 3
-    fill_halo(edge_ref, wide_ref, own_ref, first_ref, second_ref)
+    frames, rows_two, cols, state_chans = near_ref.shape
+    fill_halo(wide_ref, own_ref, first_ref, second_ref)
     keep = pltpu.make_async_copy(wide_ref, kept_ref, sem)
     keep.start()
-    group = group_of(frames, 16)
-    many = (rows + 2) * cols
+    halo_part(first_ref, second_ref, kernel_ref, upper_ref, lower_ref)
+    group = group_of(frames, SCAN_GROUP)
 
     def step(n, state):
-        base = n * group
-        drive = conv(wide_ref[pl.ds(base, group)], 0, rows + 2, kernel_ref[...])
         for k in range(group):
-            now = inside(edge_ref, drive[k * many : (k + 1) * many], cols)
-            state = lam_ref[base + k] * state + now
-            local_ref[base + k] = state.reshape(rows + 2, cols, state_chans)
+            t = n * group + k
+            state = lam_ref[t] * state + whole_rows(near_ref[t], upper_ref[t], lower_ref[t])
+            local_ref[t] = state.reshape(rows_two, cols, state_chans)
         return state
 
-    last = lax.fori_loop(0, frames // group, step, jnp.zeros((many, state_chans), F32))
-    end_ref[...] = last.reshape(rows + 2, cols, state_chans).astype(BF)
+    last = lax.fori_loop(0, frames // group, step, jnp.zeros((rows_two * cols, state_chans), F32))
+    end_ref[...] = last.reshape(rows_two, cols, state_chans).astype(BF)
     keep.wait()
 
 
@@ -225,37 +278,37 @@
     put_blocks(total_ref, out_ref, scale)
 
 
-def back_kernel(edge_ref, own_ref, first_ref, second_ref, kernel_ref, lam_ref, local_ref, lead_ref, wide_ref):
-    frames, rows, cols, _ = own_ref.shape
-    state_chans = kernel_ref.shape[1] // 3
-    fill_halo(edge_ref, wide_ref, own_ref, first_ref, second_ref)
-    group = group_of(frames, 16)
-    many = (rows + 2) * cols
+def back_kernel(
+    near_ref, first_ref, second_ref, kernel_ref, lam_ref,
+    local_ref, lead_ref, upper_ref, lower_ref,
+):
+    frames, rows_two, cols, state_chans = near_ref.shape
+    halo_part(first_ref, second_ref, kernel_ref, upper_ref, lower_ref)
+    group = group_of(frames, SCAN_GROUP)
 
     def step(n, carry):
-        base = frames - (n + 1) * group
-        flow = conv(wide_ref[pl.ds(base, group)], 0, rows + 2, kernel_ref[...])
-        for k in reversed(range(group)):
-            adjoint = inside(edge_ref, flow[k * many : (k + 1) * many], cols) + carry
-            local_ref[base + k] = adjoint.reshape(rows + 2, cols, state_chans)
-            carry = lam_ref[base + k] * adjoint
+        for k in range(group):
+            t = frames - 1 - (n * group + k)
+            adjoint = whole_rows(near_ref[t], upper_ref[t], lower_ref[t]) + carry
+            local_ref[t] = adjoint.reshape(rows_two, cols, state_chans)
+            carry = lam_ref[t] * adjoint
         return carry
 
-    lead = lax.fori_loop(0, frames // group, step, jnp.zeros((many, state_chans), F32))
-    lead_ref[...] = lead.reshape(rows + 2, cols, state_chans).astype(BF)
+    lead = lax.fori_loop(0, frames // group, step, jnp.zeros((rows_two * cols, state_chans), F32))
+    lead_ref[...] = lead.reshape(rows_two, cols, state_chans).astype(BF)
 
 
 def in_grad_kernel(
-    scale, decay_scale, blocks, place_ref, local_ref, back_ref, reach_ref, lam_ref, wide_ref, state_ref,
+    scale, decay_scale, blocks, local_ref, back_ref, reach_ref, lam_ref, wide_ref, state_ref,
     carry_ref, other_ref, gain_ref,
-    adjoint_out, sent_ref, kept_ref, total_ref, adjoint_ref, mine_ref, decay_ref, sems,
+    adjoint_ref, sent_ref, kept_ref, total_ref, mine_ref, decay_ref,
 ):
     frames, rows_two, cols, chans = local_ref.shape
     rows = rows_two - 2
     group = group_of(frames, OUTER_GROUP)
     many = rows * cols
     back = back_ref[...].astype(F32)
-    total_ref[...] = jnp.zeros_like(total_ref)
+    alone = group == frames
 
     def step(n, previous):
         base = n * group
@@ -270,45 +323,42 @@
                 jnp.sum(part, axis=0, keepdims=True) * lam_ref[base + k] * decay_scale
             )
             previous = state_ref[base + k, 1 : 1 + rows].reshape(many, chans).astype(F32)
-        piece_copy(adjoint_ref, adjoint_out, sems, n, group).start()
         left = taps(wide_ref[pl.ds(base, group)], 1, rows)
-        total_ref[...] += outer(left, spread(jnp.concatenate(kept, axis=0), cols))
+        found = outer(left, spread(jnp.concatenate(kept, axis=0), cols))
+        total_ref[...] = found if alone else jnp.where(n == 0, found, total_ref[...] + found)
         return previous
 
     before = carry_ref[1 : 1 + rows].reshape(many, chans).astype(F32)
-    lax.fori_loop(0, frames // group, step, before)
+    if alone:
+        step(0, before)
+    else:
+        lax.fori_loop(0, frames // group, step, before)
     count, full = other_ref.shape[0], mine_ref.shape[0]
     used = count + blocks * frames
     put_blocks(total_ref, mine_ref, scale)
     for n in range(blocks):
         mine_ref[count + n * frames : count + (n + 1) * frames] = jnp.where(
-            place_ref[1] == n, decay_ref[...], 0.0
+            lax.axis_index("tm") == n, decay_ref[...], 0.0
         )
     if full > used:
         mine_ref[used:] = jnp.zeros((full - used, chans), F32)
     row = lax.broadcasted_iota(jnp.int32, (full - count, chans), 0)
     rest = jnp.where(row == 0, gain_ref[...] * scale, 0.0)
 
-    @pl.when(place_ref[0] == 0)
+    @pl.when(lax.rem(lax.axis_index("dp"), 2) == 0)
     def _():
         kept_ref[...] = mine_ref[...]
         sent_ref[:count] = other_ref[...].astype(BF)
         sent_ref[count:] = rest.astype(BF)
 
-    @pl.when(place_ref[0] != 0)
+    @pl.when(lax.rem(lax.axis_index("dp"), 2) != 0)
     def _():
         sent_ref[...] = mine_ref[...].astype(BF)
         kept_ref[:count] = other_ref[...]
         kept_ref[count:] = rest
 
-    def finish(n, _):
-        piece_copy(adjoint_ref, adjoint_out, sems, n, group).wait()
-        return 0
-
-    lax.fori_loop(0, frames // group, finish, 0)
-
-
-def result_kernel(blocks, place_ref, own_ref, other_ref, in_ref, out_ref, gain_ref, decay_ref):
+
+def result_kernel(blocks, own_ref, other_ref, in_ref, out_ref, gain_ref, decay_ref):
     frames, chans = decay_ref.shape
     size = in_ref.shape[2]
     count = 9 * size
@@ -323,14 +373,14 @@
         decay = jnp.zeros((frames, chans), F32)
         for n in range(blocks):
             slot = first[count + n * frames : count + (n + 1) * frames].astype(F32)
-            decay = jnp.where(place_ref[1] == n, slot, decay)
+            decay = jnp.where(lax.axis_index("tm") == n, slot, decay)
         decay_ref[...] = decay
 
-    @pl.when(place_ref[0] == 0)
+    @pl.when(lax.rem(lax.axis_index("dp"), 2) == 0)
     def _():
         put(own_ref, other_ref)
 
-    @pl.when(place_ref[0] != 0)
+    @pl.when(lax.rem(lax.axis_index("dp"), 2) != 0)
     def _():
         put(other_ref, own_ref)
 
@@ -357,14 +407,34 @@
     lax.fori_loop(0, frames // group, finish, 0)
 
 
-def halo_pair(field, deep):
+def edge_kernel(field_ref, first_ref, second_ref, sems):
+    deep = first_ref.shape[1]
+    last = field_ref.shape[1] - deep
+    odd = lax.rem(lax.axis_index("rows"), 2)
+    one = pltpu.make_async_copy(field_ref.at[:, pl.ds((1 - odd) * last, deep)], first_ref, sems.at[0])
+    two = pltpu.make_async_copy(field_ref.at[:, pl.ds(odd * last, deep)], second_ref, sems.at[1])
+    one.start()
+    two.start()
+    one.wait()
+    two.wait()
+
+
+def halo_pair(field, deep, read=False):
     count = lax.axis_size("rows")
     odd = lax.rem(lax.axis_index("rows"), 2)
     rows = field.shape[1]
     swap = lambda low: [p for i in range(low, count - 1, 2) for p in ((i, i + 1), (i + 1, i))]
     pick = lambda flag: lax.dynamic_slice_in_dim(field, flag * (rows - deep), deep, axis=1)
-    first, second = pick(1 - odd), pick(odd)
-    return lax.ppermute(first, "rows", swap(0)), lax.ppermute(second, "rows", swap(1))
+    if read:
+        edges = shape((field.shape[0], deep) + field.shape[2:], field.dtype)
+        first, second = call(
+            edge_kernel, [edges, edges], [field], "hvv", scratch=[pltpu.SemaphoreType.DMA((2,))]
+        )
+    else:
+        first, second = pick(1 - odd), pick(odd)
+    first = lax.ppermute(first, "rows", swap(0))
+    second = lax.ppermute(second, "rows", swap(1))
+    return first, second
 
 
 def from_earlier(end, totals):
@@ -451,10 +521,6 @@
         assert size & (size - 1) == 0
     assert seqs == 1 and rows >= 2 and sizes["dp"] >= 2 and chans == state_chans
     video, cotangent = video[0], cotangent[0]
-    band = lax.axis_index("rows")
-    edge = jnp.stack(
-        [jnp.where(band > 0, 1, 0), jnp.where(band < sizes["rows"] - 1, 1, 0), lax.rem(band, 2)]
-    ).astype(jnp.int32)
     cum = jnp.cumsum(log_decay, axis=0)
     totals = cum[-1:]
     lam = jnp.exp(log_decay)[:, None, :]
@@ -469,21 +535,30 @@
     weight_scale = 1.0 / math.sqrt(devices * narrow_rows * seqs)
     decay_scale = 1.0 / math.sqrt(seqs * rows * cols * sizes["rows"] * sizes["dp"])
 
-    first, second = halo_pair(video, 2)
+    first, second = halo_pair(video, 2, True)
+    near_shape = shape((frames, rows + 2, cols, state_chans), F32)
+    near_scratch = [pltpu.VMEM((group_of(frames, NEAR_GROUP), rows + 4, cols, chans), BF)]
+    halo_scratch = [pltpu.VMEM((frames, 2, cols, state_chans), F32)] * 2
+    (near,) = call(
+        near_kernel, [near_shape], [video, flat(in_kernel)], "vvv",
+        scratch=near_scratch, flops=each * wide_rows,
+    )
     wide, local, end = call(
         drive_kernel,
         [
             shape((frames, rows + 4, cols, chans), BF),
-            shape((frames, rows + 2, cols, state_chans), F32),
+            near_shape,
             shape((rows + 2, cols, state_chans), BF),
         ],
-        [edge, video, first, second, flat(in_kernel), lam],
-        "svvvvv" + "hvv",
+        [near, video, first, second, flat(in_kernel), lam],
+        "vvvvvv" + "hvv",
         scratch=[
             pltpu.VMEM((frames, rows + 4, cols, chans), BF),
+            *halo_scratch,
             pltpu.SemaphoreType.DMA(()),
         ],
-        flops=each * wide_rows,
+        flops=each * narrow_rows // 3,
+        aliases=((0, 1),),
     )
     carry = from_earlier(end, totals)
     state, act, grad, gain_part = call(
@@ -506,6 +581,10 @@
         flops=each * narrow_rows,
     )
     first, second = halo_pair(grad, 2)
+    (near,) = call(
+        near_kernel, [near_shape], [grad, flip(out_kernel)], "vvv",
+        scratch=near_scratch, flops=each * wide_rows,
+    )
     (out_part,) = call(
         functools.partial(out_grad_kernel, weight_scale),
         [shape((9 * state_chans, chans), F32)],
@@ -516,20 +595,17 @@
     )
     local, lead = call(
         back_kernel,
-        [
-            shape((frames, rows + 2, cols, state_chans), F32),
-            shape((rows + 2, cols, state_chans), BF),
-        ],
-        [edge, grad, first, second, flip(out_kernel), lam],
-        "svvvvv" + "vv",
-        scratch=[pltpu.VMEM((frames, rows + 4, cols, chans), BF)],
-        flops=each * wide_rows,
+        [near_shape, shape((rows + 2, cols, state_chans), BF)],
+        [near, first, second, flip(out_kernel), lam],
+        "vvvvv" + "vv",
+        scratch=halo_scratch,
+        flops=each * narrow_rows // 3,
+        aliases=((0, 0),),
     )
     back = from_later(lead, totals)
     blocks = sizes["tm"]
     full = 9 * chans + blocks * frames
     full += -full % 64 if full % 32 else 0
-    place = jnp.stack([lax.rem(lax.axis_index("dp"), 2), lax.axis_index("tm")]).astype(jnp.int32)
     adjoint, sent, kept = call(
         functools.partial(in_grad_kernel, weight_scale, decay_scale, blocks),
         [
@@ -537,14 +613,12 @@
             shape((full, chans), BF),
             shape((full, chans), F32),
         ],
-        [place, local, back, back_reach, lam, wide, state, carry, out_part, gain_part],
-        "svvvvvvvvv" + "hvv",
+        [local, back, back_reach, lam, wide, state, carry, out_part, gain_part],
+        "vvvvvvvvv" + "vvv",
         scratch=[
             pltpu.VMEM((3 * chans, 3 * state_chans), F32),
-            pltpu.VMEM((frames, rows + 2, cols, state_chans), BF),
             pltpu.VMEM((full, chans), F32),
             pltpu.VMEM((frames, state_chans), F32),
-            pltpu.SemaphoreType.DMA((frames // group_of(frames, OUTER_GROUP),)),
         ],
         flops=each * narrow_rows,
     )
@@ -568,8 +642,8 @@
             shape((1, chans), F32),
             shape((frames, state_chans), F32),
         ],
-        [place, own, other],
-        "svv" + "vvvv",
+        [own, other],
+        "vv" + "vvvv",
     )
     return act[None], video_grad[None], in_grad, out_grad, gain_grad[0], decay_grad
 

time: 74.5 us -> 70.6 us (0.948)
  waiting for transfers between devices: 26.2 us -> 22.7 us
  local copies, waits for them, and re-layouts: 3.56 us -> 2.43 us
    ppermute x4, waiting for transfers between devices: 7.71 us -> 4.23 us  [the longest x2 4.22 us: halo_pair(): first = lax.ppermute(first, 'rows', swap(0))]
    dynamic_slice x2 -> x1, local copies, waits for them, and re-layouts: 1.17 us -> 0.04 us  [halo_pair(): lax.dynamic_slice_in_dim(field, flag * (rows - deep), deep, axis=1)]
    pallas_call x7 -> x10, Pallas kernels: 14.6 us -> 15.1 us  [call(): pl.pallas_call(body, out_shape=outs, in_specs=specs[:len(ins)], out_specs...]
  transfers between devices with their start and end apart: 16 -> 16, of which waited for: 13 -> 12; matrix products, arithmetic and copies ran while one was open for 3% -> 3% of each run, Pallas kernels for 4% -> 9%
where the time goes in v4:
time: 70.6 us; the launch traced here: 70.4 us
  starting transfers between devices  28.8 us (41%)
  waiting for transfers between devices  22.7 us (32%)
  Pallas kernels  15.1 us (21%)
  local copies, waits for them, and re-layouts  2.43 us (3%)
  between operations  1.03 us (1%)
    pallas_call x10, Pallas kernels, call(): pl.pallas_call(body, out_shape=outs, in_specs=specs[:len(ins)], out_specs...  15.1 us
    ppermute x10, starting transfers between devices, swap(): return lax.ppermute(value, axes, [(i, i ^ mask) for i in range(devices)])  14.7 us
    ppermute x10, waiting for transfers between devices, swap(): return lax.ppermute(value, axes, [(i, i ^ mask) for i in range(devices)])  13.5 us
    ppermute x2, starting transfers between devices, halo_pair(): first = lax.ppermute(first, 'rows', swap(0))  7.77 us
    ppermute x2, waiting for transfers between devices, halo_pair(): first = lax.ppermute(first, 'rows', swap(0))  4.22 us
    ppermute x1, waiting for transfers between devices, from_later(): piece = lax.ppermute(lead, 'tm', pairs)  3.67 us
    ppermute x1, starting transfers between devices, from_earlier(): piece = lax.ppermute(end, 'tm', pairs)  3.59 us
    transpose x2, local copies, waits for them, and re-layouts, on_device(): k.transpose(0, 2, 1, 3).reshape(3 * k.shape[2], 3 * k.shape[3])  1.48 us
  transfers between devices with their start and end apart: 16, of which 12 were waited for; matrix products, arithmetic and copies ran while one was open for 3% of the time, Pallas kernels for 9%

profile of v4, /device:TPU:0, one launch (start us, length us, event | category | flops | bytes accessed | tf_op | source)
XLA Modules:
  0.0 70.4 jit_solution(10014941266446913929)
XLA Ops:
  0.6 1.1 %shard_map.110 = (bf16[16,2,32,128]{3,2,1,0:T(8,128)(2,1)S(1)}, bf16[16,2,32,128]{3,2,1,0:T(8,128)(2,1)S(1)}) custom-call(bf16[16,4,32,128]{3,2,1,0:T(8,128)(2,1)} %bitcast.36), custom_call_target="tpu_custom_call" | custom-call | bytes 1048576 | tf_op jit(solution)/shard_map/pallas_call | solution.py:33
  1.8 3.1 %collective-permute-start = (bf16[16,2,32,128]{3,2,1,0:T(8,128)(2,1)S(1)}, bf16[16,2,32,128]{3,2,1,0:T(8,128)(2,1)S(1)}, u32[]{:S(2)}, u32[]{:S(2)}) collective-permute-start(bf16[16,2,32,128]{3,2,1,0:T(8,128)(2,1)S(1)} %get-tuple-element.28), channel_id=1, source_target_pairs={{0,4},{4,0},{8,12},{12,8},{1,5},{5,1},{9,13},{13,9},{2,6},{6,2},{1... | collective-permute-start | bytes 786440 | tf_op jit(solution)/shard_map/ppermute | solution.py:435
  5.6 1.2 %copy.18 = bf16[3,128,3,128]{3,2,1,0:T(4,128)(2,1)S(1)} copy(bf16[3,128,3,128]{3,1,2,0:T(8,128)(2,1)} %bitcast.56) | data formatting | bytes 589824 | tf_op jit(solution)/shard_map/transpose | solution.py:530
  6.9 1.8 %shard_map.109.near_ref = f32[16,6,32,128]{3,2,1,0:T(8,128)S(1)} custom-call(bf16[16,4,32,128]{3,2,1,0:T(8,128)(2,1)S(1)} %bitcast.38, bf16[384,384]{1,0:T(8,128)(2,1)S(1)} %bitcast.43), custom_call_target="tpu_custom_call" | custom-call | flops 905969664 | bytes 2392064 | tf_op jit(solution)/shard_map/pallas_call | solution.py:33
  8.7 2.5 %collective-permute-done.first_ref = bf16[16,2,32,128]{3,2,1,0:T(8,128)(2,1)S(1)} collective-permute-done((bf16[16,2,32,128]{3,2,1,0:T(8,128)(2,1)S(1)}, bf16[16,2,32,128]{3,2,1,0:T(8,128)(2,1)S(1)}, u32[]{:S(2)}, u32[]{:S(2)}) %collective-permute-start) | collective-permute-done | bytes 262176 | tf_op jit(solution)/shard_map/ppermute | solution.py:435
  11.2 1.1 %shard_map.111 = (bf16[16,8,32,128]{3,2,1,0:T(8,128)(2,1)}, f32[16,6,32,128]{3,2,1,0:T(8,128)S(1)}, bf16[6,32,128]{2,1,0:T(8,128)(2,1)S(1)}) custom-call(f32[16,6,32,128]{3,2,1,0:T(8,128)S(1)} %shard_map.109.near_ref, bf16[16,4,32,128]{3,2,1,0:T(8,128)(2,1)S(1)} %bitcast.39, ...), custom_call_target="tpu_custom_call", output_to_operand_aliasing={{1}: (0, {})} | custom-call | flops 201326592 | bytes 5595136 | tf_op jit(solution)/shard_map/pallas_call | solution.py:33
  12.3 3.6 %collective-permute-start.2 = (bf16[6,32,128]{2,1,0:T(8,128)(2,1)S(1)}, bf16[6,32,128]{2,1,0:T(8,128)(2,1)S(1)}, u32[]{:S(2)}, u32[]{:S(2)}) collective-permute-start(bf16[6,32,128]{2,1,0:T(8,128)(2,1)S(1)} %get-tuple-element.31), channel_id=1, source_target_pairs={{0,16},{1,17},{2,18},{3,19},{4,20},{5,21},{6,22},{7,23},{8,24},{9,... | collective-permute-start | bytes 147464 | tf_op jit(solution)/shard_map/ppermute | solution.py:445
  16.3 1.4 %collective-permute-done.2.carry_ref = bf16[6,32,128]{2,1,0:T(8,128)(2,1)S(1)} collective-permute-done((bf16[6,32,128]{2,1,0:T(8,128)(2,1)S(1)}, bf16[6,32,128]{2,1,0:T(8,128)(2,1)S(1)}, u32[]{:S(2)}, u32[]{:S(2)}) %collective-permute-start.2) | collective-permute-done | bytes 49184 | tf_op jit(solution)/shard_map/ppermute | solution.py:445
  17.6 3.1 %shard_map.112 = (bf16[16,6,32,128]{3,2,1,0:T(8,128)(2,1)}, bf16[16,4,32,128]{3,2,1,0:T(8,128)(2,1)}, bf16[16,4,32,128]{3,2,1,0:T(8,128)(2,1)S(1)}, f32[1,128]{1,0:T(1,128)S(1)}) custom-call(f32[16,6,32,128]{3,2,1,0:T(8,128)S(1)} %get-tuple-element.30.local_ref, bf16[6,32,128]{2,1,0:T(8,128)(2,1)S(1)} %collective-permute-done.2.carry_ref, ...), custom_call_target="tpu_custom_call" | custom-call | flops 603979776 | bytes 4809728 | tf_op jit(solution)/shard_map/pallas_call | solution.py:33
  20.8 4.7 %collective-permute-start.3 = (bf16[16,2,32,128]{3,2,1,0:T(8,128)(2,1)S(1)}, bf16[16,2,32,128]{3,2,1,0:T(8,128)(2,1)S(1)}, u32[]{:S(2)}, u32[]{:S(2)}) collective-permute-start(bf16[16,2,32,128]{3,2,1,0:T(8,128)(2,1)S(1)} %get-tuple-element.56), channel_id=1, source_target_pairs={{0,4},{4,0},{8,12},{12,8},{1,5},{5,1},{9,13},{13,9},{2,6},{6,2},{1... | collective-permute-start | bytes 786440 | tf_op jit(solution)/shard_map/ppermute | solution.py:435
  26.5 1.8 %shard_map.113.near_ref = f32[16,6,32,128]{3,2,1,0:T(8,128)S(1)} custom-call(bf16[16,4,32,128]{3,2,1,0:T(8,128)(2,1)S(1)} %get-tuple-element.33.own_ref.grad_ref, bf16[384,384]{1,0:T(8,128)(2,1)S(1)} %bitcast.41), custom_call_target="tpu_custom_call" | custom-call | flops 905969664 | bytes 2392064 | tf_op jit(solution)/shard_map/pallas_call | solution.py:33
  28.3 1.8 %collective-permute-done.3.first_ref = bf16[16,2,32,128]{3,2,1,0:T(8,128)(2,1)S(1)} collective-permute-done((bf16[16,2,32,128]{3,2,1,0:T(8,128)(2,1)S(1)}, bf16[16,2,32,128]{3,2,1,0:T(8,128)(2,1)S(1)}, u32[]{:S(2)}, u32[]{:S(2)}) %collective-permute-start.3) | collective-permute-done | bytes 262176 | tf_op jit(solution)/shard_map/ppermute | solution.py:435
  30.1 0.9 %shard_map.114 = (f32[16,6,32,128]{3,2,1,0:T(8,128)S(1)}, bf16[6,32,128]{2,1,0:T(8,128)(2,1)S(1)}) custom-call(f32[16,6,32,128]{3,2,1,0:T(8,128)S(1)} %shard_map.113.near_ref, bf16[16,2,32,128]{3,2,1,0:T(8,128)(2,1)S(1)} %collective-permute-done.3.first_ref, ...), custom_call_target="tpu_custom_call", output_to_operand_aliasing={{0}: (0, {})} | custom-call | flops 201326592 | bytes 4022272 | tf_op jit(solution)/shard_map/pallas_call | solution.py:33
  31.0 1.4 %collective-permute-start.5 = (bf16[6,32,128]{2,1,0:T(8,128)(2,1)S(1)}, bf16[6,32,128]{2,1,0:T(8,128)(2,1)S(1)}, u32[]{:S(2)}, u32[]{:S(2)}) collective-permute-start(bf16[6,32,128]{2,1,0:T(8,128)(2,1)S(1)} %get-tuple-element.35), channel_id=1, source_target_pairs={{16,0},{17,1},{18,2},{19,3},{20,4},{21,5},{22,6},{23,7},{24,8},{25... | collective-permute-start | bytes 147464 | tf_op jit(solution)/shard_map/ppermute | solution.py:462
  32.4 1.0 %shard_map.115.other_ref = f32[1152,128]{1,0:T(8,128)S(1)} custom-call(bf16[16,6,32,128]{3,2,1,0:T(8,128)(2,1)S(1)} %copy-done.2, bf16[16,4,32,128]{3,2,1,0:T(8,128)(2,1)S(1)} %get-tuple-element.33.own_ref.grad_ref), custom_call_target="tpu_custom_call" | custom-call | flops 603979776 | bytes 1900544 | tf_op jit(solution)/shard_map/pallas_call | solution.py:33
  33.5 3.7 %collective-permute-done.5.back_ref = bf16[6,32,128]{2,1,0:T(8,128)(2,1)S(1)} collective-permute-done((bf16[6,32,128]{2,1,0:T(8,128)(2,1)S(1)}, bf16[6,32,128]{2,1,0:T(8,128)(2,1)S(1)}, u32[]{:S(2)}, u32[]{:S(2)}) %collective-permute-start.5) | collective-permute-done | bytes 49184 | tf_op jit(solution)/shard_map/ppermute | solution.py:462
  37.1 1.1 %shard_map.116 = (bf16[16,6,32,128]{3,2,1,0:T(8,128)(2,1)S(1)}, bf16[1184,128]{1,0:T(8,128)(2,1)S(1)}, f32[1184,128]{1,0:T(8,128)S(1)}) custom-call(f32[16,6,32,128]{3,2,1,0:T(8,128)S(1)} %get-tuple-element.34.local_ref, bf16[6,32,128]{2,1,0:T(8,128)(2,1)S(1)} %collective-permute-done.5.back_ref, f32[16,1,128]{2,1,0:T(1,128)S(1)} %get-tuple-element.57.reach_ref, ...), custom_call_target="tpu_custom_call" | custom-call | flops 603979776 | bytes 5808640 | tf_op jit(solution)/shard_map/pallas_call | solution.py:33
  38.4 1.5 %collective-permute-done.6 = bf16[1184,128]{1,0:T(8,128)(2,1)S(1)} collective-permute-done((bf16[1184,128]{1,0:T(8,128)(2,1)S(1)}, bf16[1184,128]{1,0:T(8,128)(2,1)S(1)}, u32[]{:S(2)}, u32[]{:S(2)}) %collective-permute-start.6) | collective-permute-done | bytes 303136 | tf_op jit(solution)/shard_map/ppermute | solution.py:488
  40.0 1.6 %collective-permute-start.7 = (bf16[296,128]{1,0:T(8,128)(2,1)S(1)}, bf16[296,128]{1,0:T(8,128)(2,1)S(1)}, u32[]{:S(2)}, u32[]{:S(2)}) collective-permute-start(bf16[296,128]{1,0:T(8,128)(2,1)S(1)} %get-tuple-element.43), channel_id=1, source_target_pairs={{0,2},{1,3},{2,0},{3,1},{4,6},{5,7},{6,4},{7,5},{8,10},{9,11},{10,... | collective-permute-start | bytes 227336 | tf_op jit(solution)/shard_map/ppermute | solution.py:488
  41.6 2.0 %collective-permute-start.9 = (bf16[296,128]{1,0:T(8,128)(2,1)S(1)}, bf16[296,128]{1,0:T(8,128)(2,1)S(1)}, u32[]{:S(2)}, u32[]{:S(2)}) collective-permute-start(bf16[296,128]{1,0:T(8,128)(2,1)S(1)} %get-tuple-element.45), channel_id=1, source_target_pairs={{0,18},{1,19},{2,16},{3,17},{4,22},{5,23},{6,20},{7,21},{8,26},{9,... | collective-permute-start | bytes 227336 | tf_op jit(solution)/shard_map/ppermute | solution.py:488
  43.6 0.9 %collective-permute-done.7 = bf16[296,128]{1,0:T(8,128)(2,1)S(1)} collective-permute-done((bf16[296,128]{1,0:T(8,128)(2,1)S(1)}, bf16[296,128]{1,0:T(8,128)(2,1)S(1)}, u32[]{:S(2)}, u32[]{:S(2)}) %collective-permute-start.7) | collective-permute-done | bytes 75808 | tf_op jit(solution)/shard_map/ppermute | solution.py:488
  44.5 2.9 %collective-permute-done.8 = bf16[296,128]{1,0:T(8,128)(2,1)S(1)} collective-permute-done((bf16[296,128]{1,0:T(8,128)(2,1)S(1)}, bf16[296,128]{1,0:T(8,128)(2,1)S(1)}, u32[]{:S(2)}, u32[]{:S(2)}) %collective-permute-start.8) | collective-permute-done | bytes 75808 | tf_op jit(solution)/shard_map/ppermute | solution.py:488
  47.4 3.7 %collective-permute-start.10 = (bf16[296,128]{1,0:T(8,128)(2,1)S(1)}, bf16[296,128]{1,0:T(8,128)(2,1)S(1)}, u32[]{:S(2)}, u32[]{:S(2)}) collective-permute-start(bf16[296,128]{1,0:T(8,128)(2,1)S(1)} %add_convert_fusion.2), channel_id=1, source_target_pairs={{0,4},{1,5},{2,6},{3,7},{4,0},{5,1},{6,2},{7,3},{8,12},{9,13},{10,... | collective-permute-start | bytes 227336 | tf_op jit(solution)/shard_map/ppermute | solution.py:488
  51.2 2.4 %collective-permute-done.10 = bf16[296,128]{1,0:T(8,128)(2,1)S(1)} collective-permute-done((bf16[296,128]{1,0:T(8,128)(2,1)S(1)}, bf16[296,128]{1,0:T(8,128)(2,1)S(1)}, u32[]{:S(2)}, u32[]{:S(2)}) %collective-permute-start.10) | collective-permute-done | bytes 75808 | tf_op jit(solution)/shard_map/ppermute | solution.py:488
  53.6 3.7 %collective-permute-start.11 = (bf16[296,128]{1,0:T(8,128)(2,1)S(1)}, bf16[296,128]{1,0:T(8,128)(2,1)S(1)}, u32[]{:S(2)}, u32[]{:S(2)}) collective-permute-start(bf16[296,128]{1,0:T(8,128)(2,1)S(1)} %add_convert_fusion.1), channel_id=1, source_target_pairs={{0,8},{1,9},{2,10},{3,11},{4,12},{5,13},{6,14},{7,15},{8,0},{9,1},... | collective-permute-start | bytes 227336 | tf_op jit(solution)/shard_map/ppermute | solution.py:488
  57.3 2.4 %collective-permute-done.11 = bf16[296,128]{1,0:T(8,128)(2,1)S(1)} collective-permute-done((bf16[296,128]{1,0:T(8,128)(2,1)S(1)}, bf16[296,128]{1,0:T(8,128)(2,1)S(1)}, u32[]{:S(2)}, u32[]{:S(2)}) %collective-permute-start.11) | collective-permute-done | bytes 75808 | tf_op jit(solution)/shard_map/ppermute | solution.py:488
  60.4 1.1 %collective-permute-start.13 = (bf16[296,128]{1,0:T(8,128)(2,1)S(1)}, bf16[296,128]{1,0:T(8,128)(2,1)S(1)}, u32[]{:S(2)}, u32[]{:S(2)}) collective-permute-start(bf16[296,128]{1,0:T(8,128)(2,1)S(1)} %get-tuple-element.51), channel_id=1, source_target_pairs={{0,16},{1,17},{2,18},{3,19},{4,20},{5,21},{6,22},{7,23},{8,24},{9,... | collective-permute-start | bytes 227336 | tf_op jit(solution)/shard_map/ppermute | solution.py:488
  61.5 1.8 %collective-permute-start.14 = (bf16[296,128]{1,0:T(8,128)(2,1)S(1)}, bf16[296,128]{1,0:T(8,128)(2,1)S(1)}, u32[]{:S(2)}, u32[]{:S(2)}) collective-permute-start(bf16[296,128]{1,0:T(8,128)(2,1)S(1)} %get-tuple-element.51), channel_id=1, source_target_pairs={{0,18},{1,19},{2,16},{3,17},{4,22},{5,23},{6,20},{7,21},{8,26},{9,... | collective-permute-start | bytes 227336 | tf_op jit(solution)/shard_map/ppermute | solution.py:488
  63.3 0.9 %collective-permute-done.12 = bf16[296,128]{1,0:T(8,128)(2,1)S(1)} collective-permute-done((bf16[296,128]{1,0:T(8,128)(2,1)S(1)}, bf16[296,128]{1,0:T(8,128)(2,1)S(1)}, u32[]{:S(2)}, u32[]{:S(2)}) %collective-permute-start.12) | collective-permute-done | bytes 75808 | tf_op jit(solution)/shard_map/ppermute | solution.py:488
  64.8 2.0 %collective-permute-done.14 = bf16[296,128]{1,0:T(8,128)(2,1)S(1)} collective-permute-done((bf16[296,128]{1,0:T(8,128)(2,1)S(1)}, bf16[296,128]{1,0:T(8,128)(2,1)S(1)}, u32[]{:S(2)}, u32[]{:S(2)}) %collective-permute-start.14) | collective-permute-done | bytes 75808 | tf_op jit(solution)/shard_map/ppermute | solution.py:488
  67.2 2.0 %shard_map.117 = bf16[16,4,32,128]{3,2,1,0:T(8,128)(2,1)} custom-call(bf16[16,6,32,128]{3,2,1,0:T(8,128)(2,1)S(1)} %get-tuple-element.39.adjoint_ref, bf16[16,4,32,128]{3,2,1,0:T(8,128)(2,1)S(1)} %get-tuple-element.33.own_ref.grad_ref, bf16[384,384]{1,0:T(8,128)(2,1)S(1)} %bitcast.45, f32[1,128]{1,0:T(1,128)S(1)} %bitcast.50), custom_call_target="tpu_custom_call" | custom-call | flops 603979776 | bytes 2130432 | tf_op jit(solution)/shard_map/pallas_call | solution.py:33
  69.3 1.1 %shard_map.118 = (f32[3,3,128,128]{3,2,1,0:T(8,128)}, f32[3,3,128,128]{3,2,1,0:T(8,128)}, f32[1,128]{1,0:T(1,128)}, f32[16,128]{1,0:T(8,128)}) custom-call(bf16[1184,128]{1,0:T(8,128)(2,1)S(1)} %constant_dynamic-update-slice_fusion.own_ref, bf16[1184,128]{1,0:T(8,128)(2,1)S(1)} %collective-permute-done.15.other_ref), custom_call_target="tpu_custom_call" | custom-call | bytes 1794560 | tf_op jit(solution)/shard_map/pallas_call | solution.py:33
  (49 shorter events, 4.1 us)
Async XLA Ops:
  0.6 6.2 %copy-start = (bf16[1,16,4,32,128]{4,3,2,1,0:T(8,128)(2,1)S(1)}, bf16[1,16,4,32,128]{4,3,2,1,0:T(8,128)(2,1)}, u32[]{:S(2)}) copy-start(bf16[1,16,4,32,128]{4,3,2,1,0:T(8,128)(2,1)} %param.6) | copy-start | bytes 1572868
  1.8 9.4 %collective-permute-start = (bf16[16,2,32,128]{3,2,1,0:T(8,128)(2,1)S(1)}, bf16[16,2,32,128]{3,2,1,0:T(8,128)(2,1)S(1)}, u32[]{:S(2)}, u32[]{:S(2)}) collective-permute-start(bf16[16,2,32,128]{3,2,1,0:T(8,128)(2,1)S(1)} %get-tuple-element.28), channel_id=1, source_target_pairs={{0,4},{4,0},{8,12},{12,8},{1,5},{5,1},{9,13},{13,9},{2,6},{6,2},{1... | collective-permute-start | bytes 786440 | tf_op jit(solution)/shard_map/ppermute | solution.py:435
  4.9 6.3 %collective-permute-start.1 = (bf16[16,2,32,128]{3,2,1,0:T(8,128)(2,1)S(1)}, bf16[16,2,32,128]{3,2,1,0:T(8,128)(2,1)S(1)}, u32[]{:S(2)}, u32[]{:S(2)}) collective-permute-start(bf16[16,2,32,128]{3,2,1,0:T(8,128)(2,1)S(1)} %get-tuple-element.29), channel_id=1, source_target_pairs={{4,8},{8,4},{5,9},{9,5},{6,10},{10,6},{7,11},{11,7},{20,24},{24,20... | collective-permute-start | bytes 786440 | tf_op jit(solution)/shard_map/ppermute | solution.py:436
  6.8 1.8 %copy-start.6 = (f32[16,128]{1,0:T(8,128)S(1)}, f32[16,128]{1,0:T(8,128)}, u32[]{:S(2)}) copy-start(f32[16,128]{1,0:T(8,128)} %param.11) | copy-start | bytes 24580
  11.2 4.7 %copy-start.4 = (bf16[3,3,128,128]{3,2,1,0:T(8,128)(2,1)S(1)}, bf16[3,3,128,128]{3,2,1,0:T(8,128)(2,1)}, u32[]{:S(2)}) copy-start(bf16[3,3,128,128]{3,2,1,0:T(8,128)(2,1)} %param.9) | copy-start | bytes 884740
  11.2 6.4 %copy-start.3 = (f32[128]{0:T(128)S(1)}, f32[128]{0:T(128)}, u32[]{:S(2)}) copy-start(f32[128]{0:T(128)} %param.10) | copy-start | bytes 1540
  12.3 5.3 %collective-permute-start.2 = (bf16[6,32,128]{2,1,0:T(8,128)(2,1)S(1)}, bf16[6,32,128]{2,1,0:T(8,128)(2,1)S(1)}, u32[]{:S(2)}, u32[]{:S(2)}) collective-permute-start(bf16[6,32,128]{2,1,0:T(8,128)(2,1)S(1)} %get-tuple-element.31), channel_id=1, source_target_pairs={{0,16},{1,17},{2,18},{3,19},{4,20},{5,21},{6,22},{7,23},{8,24},{9,... | collective-permute-start | bytes 147464 | tf_op jit(solution)/shard_map/ppermute | solution.py:445
  20.8 9.3 %collective-permute-start.3 = (bf16[16,2,32,128]{3,2,1,0:T(8,128)(2,1)S(1)}, bf16[16,2,32,128]{3,2,1,0:T(8,128)(2,1)S(1)}, u32[]{:S(2)}, u32[]{:S(2)}) collective-permute-start(bf16[16,2,32,128]{3,2,1,0:T(8,128)(2,1)S(1)} %get-tuple-element.56), channel_id=1, source_target_pairs={{0,4},{4,0},{8,12},{12,8},{1,5},{5,1},{9,13},{13,9},{2,6},{6,2},{1... | collective-permute-start | bytes 786440 | tf_op jit(solution)/shard_map/ppermute | solution.py:435
  25.5 4.6 %collective-permute-start.4 = (bf16[16,2,32,128]{3,2,1,0:T(8,128)(2,1)S(1)}, bf16[16,2,32,128]{3,2,1,0:T(8,128)(2,1)S(1)}, u32[]{:S(2)}, u32[]{:S(2)}) collective-permute-start(bf16[16,2,32,128]{3,2,1,0:T(8,128)(2,1)S(1)} %get-tuple-element.55), channel_id=1, source_target_pairs={{4,8},{8,4},{5,9},{9,5},{6,10},{10,6},{7,11},{11,7},{20,24},{24,20... | collective-permute-start | bytes 786440 | tf_op jit(solution)/shard_map/ppermute | solution.py:436
  28.3 4.2 %copy-start.2 = (bf16[16,6,32,128]{3,2,1,0:T(8,128)(2,1)S(1)}, bf16[16,6,32,128]{3,2,1,0:T(8,128)(2,1)}, u32[]{:S(2)}) copy-start(bf16[16,6,32,128]{3,2,1,0:T(8,128)(2,1)} %get-tuple-element.37.state_ref) | copy-start | bytes 2359300
  31.0 6.1 %copy-start.1 = (bf16[16,8,32,128]{3,2,1,0:T(8,128)(2,1)S(1)}, bf16[16,8,32,128]{3,2,1,0:T(8,128)(2,1)}, u32[]{:S(2)}) copy-start(bf16[16,8,32,128]{3,2,1,0:T(8,128)(2,1)} %get-tuple-element.36.wide_ref) | copy-start | bytes 3145732
  31.0 6.1 %collective-permute-start.5 = (bf16[6,32,128]{2,1,0:T(8,128)(2,1)S(1)}, bf16[6,32,128]{2,1,0:T(8,128)(2,1)S(1)}, u32[]{:S(2)}, u32[]{:S(2)}) collective-permute-start(bf16[6,32,128]{2,1,0:T(8,128)(2,1)S(1)} %get-tuple-element.35), channel_id=1, source_target_pairs={{16,0},{17,1},{18,2},{19,3},{20,4},{21,5},{22,6},{23,7},{24,8},{25... | collective-permute-start | bytes 147464 | tf_op jit(solution)/shard_map/ppermute | solution.py:462
  38.2 1.7 %collective-permute-start.6 = (bf16[1184,128]{1,0:T(8,128)(2,1)S(1)}, bf16[1184,128]{1,0:T(8,128)(2,1)S(1)}, u32[]{:S(2)}, u32[]{:S(2)}) collective-permute-start(bf16[1184,128]{1,0:T(8,128)(2,1)S(1)} %get-tuple-element.41), channel_id=1, source_target_pairs={{0,1},{1,0},{2,3},{3,2},{4,5},{5,4},{6,7},{7,6},{8,9},{9,8},{10,11... | collective-permute-start | bytes 909320 | tf_op jit(solution)/shard_map/ppermute | solution.py:488
  40.0 26.9 %copy-start.5 = (bf16[3,3,128,128]{3,2,1,0:T(8,128)(2,1)S(1)}, bf16[3,3,128,128]{3,2,1,0:T(8,128)(2,1)}, u32[]{:S(2)}) copy-start(bf16[3,3,128,128]{3,2,1,0:T(8,128)(2,1)} %param.8) | copy-start | bytes 884740
  40.0 4.4 %collective-permute-start.7 = (bf16[296,128]{1,0:T(8,128)(2,1)S(1)}, bf16[296,128]{1,0:T(8,128)(2,1)S(1)}, u32[]{:S(2)}, u32[]{:S(2)}) collective-permute-start(bf16[296,128]{1,0:T(8,128)(2,1)S(1)} %get-tuple-element.43), channel_id=1, source_target_pairs={{0,2},{1,3},{2,0},{3,1},{4,6},{5,7},{6,4},{7,5},{8,10},{9,11},{10,... | collective-permute-start | bytes 227336 | tf_op jit(solution)/shard_map/ppermute | solution.py:488
  41.6 5.8 %collective-permute-start.8 = (bf16[296,128]{1,0:T(8,128)(2,1)S(1)}, bf16[296,128]{1,0:T(8,128)(2,1)S(1)}, u32[]{:S(2)}, u32[]{:S(2)}) collective-permute-start(bf16[296,128]{1,0:T(8,128)(2,1)S(1)} %get-tuple-element.44), channel_id=1, source_target_pairs={{0,16},{1,17},{2,18},{3,19},{4,20},{5,21},{6,22},{7,23},{8,24},{9,... | collective-permute-start | bytes 227336 | tf_op jit(solution)/shard_map/ppermute | solution.py:488
  41.6 5.8 %collective-permute-start.9 = (bf16[296,128]{1,0:T(8,128)(2,1)S(1)}, bf16[296,128]{1,0:T(8,128)(2,1)S(1)}, u32[]{:S(2)}, u32[]{:S(2)}) collective-permute-start(bf16[296,128]{1,0:T(8,128)(2,1)S(1)} %get-tuple-element.45), channel_id=1, source_target_pairs={{0,18},{1,19},{2,16},{3,17},{4,22},{5,23},{6,20},{7,21},{8,26},{9,... | collective-permute-start | bytes 227336 | tf_op jit(solution)/shard_map/ppermute | solution.py:488
  47.4 6.1 %collective-permute-start.10 = (bf16[296,128]{1,0:T(8,128)(2,1)S(1)}, bf16[296,128]{1,0:T(8,128)(2,1)S(1)}, u32[]{:S(2)}, u32[]{:S(2)}) collective-permute-start(bf16[296,128]{1,0:T(8,128)(2,1)S(1)} %add_convert_fusion.2), channel_id=1, source_target_pairs={{0,4},{1,5},{2,6},{3,7},{4,0},{5,1},{6,2},{7,3},{8,12},{9,13},{10,... | collective-permute-start | bytes 227336 | tf_op jit(solution)/shard_map/ppermute | solution.py:488
  53.6 6.1 %collective-permute-start.11 = (bf16[296,128]{1,0:T(8,128)(2,1)S(1)}, bf16[296,128]{1,0:T(8,128)(2,1)S(1)}, u32[]{:S(2)}, u32[]{:S(2)}) collective-permute-start(bf16[296,128]{1,0:T(8,128)(2,1)S(1)} %add_convert_fusion.1), channel_id=1, source_target_pairs={{0,8},{1,9},{2,10},{3,11},{4,12},{5,13},{6,14},{7,15},{8,0},{9,1},... | collective-permute-start | bytes 227336 | tf_op jit(solution)/shard_map/ppermute | solution.py:488
  59.8 4.4 %collective-permute-start.12 = (bf16[296,128]{1,0:T(8,128)(2,1)S(1)}, bf16[296,128]{1,0:T(8,128)(2,1)S(1)}, u32[]{:S(2)}, u32[]{:S(2)}) collective-permute-start(bf16[296,128]{1,0:T(8,128)(2,1)S(1)} %get-tuple-element.51), channel_id=1, source_target_pairs={{0,2},{1,3},{2,0},{3,1},{4,6},{5,7},{6,4},{7,5},{8,10},{9,11},{10,... | collective-permute-start | bytes 227336 | tf_op jit(solution)/shard_map/ppermute | solution.py:488
  60.4 4.4 %collective-permute-start.13 = (bf16[296,128]{1,0:T(8,128)(2,1)S(1)}, bf16[296,128]{1,0:T(8,128)(2,1)S(1)}, u32[]{:S(2)}, u32[]{:S(2)}) collective-permute-start(bf16[296,128]{1,0:T(8,128)(2,1)S(1)} %get-tuple-element.51), channel_id=1, source_target_pairs={{0,16},{1,17},{2,18},{3,19},{4,20},{5,21},{6,22},{7,23},{8,24},{9,... | collective-permute-start | bytes 227336 | tf_op jit(solution)/shard_map/ppermute | solution.py:488
  61.5 5.3 %collective-permute-start.14 = (bf16[296,128]{1,0:T(8,128)(2,1)S(1)}, bf16[296,128]{1,0:T(8,128)(2,1)S(1)}, u32[]{:S(2)}, u32[]{:S(2)}) collective-permute-start(bf16[296,128]{1,0:T(8,128)(2,1)S(1)} %get-tuple-element.51), channel_id=1, source_target_pairs={{0,18},{1,19},{2,16},{3,17},{4,22},{5,23},{6,20},{7,21},{8,26},{9,... | collective-permute-start | bytes 227336 | tf_op jit(solution)/shard_map/ppermute | solution.py:488
  66.8 2.5 %collective-permute-start.15 = (bf16[1184,128]{1,0:T(8,128)(2,1)S(1)}, bf16[1184,128]{1,0:T(8,128)(2,1)S(1)}, u32[]{:S(2)}, u32[]{:S(2)}) collective-permute-start(bf16[1184,128]{1,0:T(8,128)(2,1)S(1)} %constant_dynamic-update-slice_fusion.own_ref), channel_id=1, source_target_pairs={{0,1},{1,0},{2,3},{3,2},{4,5},{5,4},{6,7},{7,6},{8,9},{9,8},{10,11... | collective-permute-start | bytes 909320 | tf_op jit(solution)/shard_map/ppermute | solution.py:488

commit v5 on v4

--- a/solution.py
+++ b/solution.py
@@ -142,6 +142,13 @@
     lax.fori_loop(0, frames // group, step, 0)
 
 
+def near_back_kernel(own_ref, kernel_ref, act_ref, near_ref, act_out, wide_ref, sem):
+    copy = pltpu.make_async_copy(act_ref, act_out, sem)
+    copy.start()
+    near_kernel(own_ref, kernel_ref, near_ref, wide_ref)
+    copy.wait()
+
+
 def halo_part(first_ref, second_ref, kernel_ref, upper_ref, lower_ref):
     frames, deep, cols, chans = first_ref.shape
     state_chans = kernel_ref.shape[1] // 3
@@ -203,13 +210,13 @@
 
 def layer_kernel(
     local_ref, carry_ref, reach_ref, own_ref, cot_ref, kernel_ref, gain_ref,
-    state_out, act_out, grad_ref, gain_grad_ref,
-    own_in, cot_in, state_ref, act_ref, sems,
+    state_out, act_ref, grad_ref, gain_grad_ref,
+    own_in, cot_in, state_ref, sems,
 ):
     frames, rows, cols, chans = own_ref.shape
     group = group_of(frames, LAYER_GROUP)
     many = group * rows * cols
-    carry = carry_ref[...].astype(F32)
+    carry = earlier(carry_ref, slice(None))
     steps = frames // group
 
     def start(n, _):
@@ -232,12 +239,11 @@
         own = own_in[pl.ds(base, group)].reshape(many, chans).astype(F32)
         pre = flow + gain_ref[...] * own
         square = pre * pre
-        bend = jnp.tanh(GELU_A * (pre + GELU_B * square * pre))
-        half = 0.5 * (1.0 + bend)
-        slope = half + 0.5 * pre * (1.0 - bend * bend) * (GELU_A * (1.0 + 3.0 * GELU_B * square))
+        half = 0.5 + 0.5 * jnp.tanh(pre * (GELU_A + (GELU_A * GELU_B) * square))
+        act = pre * half
+        slope = half + act * (1.0 - half) * (2.0 * GELU_A + (6.0 * GELU_A * GELU_B) * square)
         grad = cot_in[pl.ds(base, group)].reshape(many, chans).astype(F32) * slope
-        act_ref[pl.ds(base, group)] = (pre * half).astype(BF).reshape(group, rows, cols, chans)
-        piece_copy(act_ref, act_out, sems.at[3], n, group).start()
+        act_ref[pl.ds(base, group)] = act.astype(BF).reshape(group, rows, cols, chans)
         grad_ref[pl.ds(base, group)] = grad.astype(BF).reshape(group, rows, cols, chans)
         return total + jnp.sum((grad * own).reshape(many // 8, 8, chans), axis=0)
 
@@ -246,7 +252,6 @@
 
     def finish(n, _):
         piece_copy(state_ref, state_out, sems.at[2], n, group).wait()
-        piece_copy(act_ref, act_out, sems.at[3], n, group).wait()
         return 0
 
     lax.fori_loop(0, steps, finish, 0)
@@ -307,7 +312,7 @@
     rows = rows_two - 2
     group = group_of(frames, OUTER_GROUP)
     many = rows * cols
-    back = back_ref[...].astype(F32)
+    back = later(back_ref, slice(None))
     alone = group == frames
 
     def step(n, previous):
@@ -328,7 +333,7 @@
         total_ref[...] = found if alone else jnp.where(n == 0, found, total_ref[...] + found)
         return previous
 
-    before = carry_ref[1 : 1 + rows].reshape(many, chans).astype(F32)
+    before = earlier(carry_ref, slice(1, 1 + rows)).reshape(many, chans)
     if alone:
         step(0, before)
     else:
@@ -358,31 +363,41 @@
         kept_ref[count:] = rest
 
 
-def result_kernel(blocks, own_ref, other_ref, in_ref, out_ref, gain_ref, decay_ref):
+def result_kernel(blocks, mine, *refs):
+    half_ref = refs[0]
+    in_out, out_out, gain_out, decay_out, in_ref, out_ref, gain_ref, decay_ref, sems = refs[-9:]
     frames, chans = decay_ref.shape
     size = in_ref.shape[2]
     count = 9 * size
-
-    def put(first, second):
+    first = lax.rem(lax.axis_index("dp"), 2) == (0 if mine else 1)
+
+    def send(wide_ref, wide_out, small_ref, small_out):
+        small = pltpu.make_async_copy(small_ref, small_out, sems.at[3])
+        small.start()
+        copies = []
         for i in range(3):
             for j in range(3):
                 at = (3 * i + j) * size
-                in_ref[i, j] = first[at : at + size].astype(F32)
-                out_ref[i, j] = second[at : at + size].astype(F32)
-        gain_ref[...] = second[count : count + 16].astype(F32)[:1]
+                wide_ref[i, j] = half_ref[at : at + size].astype(F32)
+            copies.append(pltpu.make_async_copy(wide_ref.at[i], wide_out.at[i], sems.at[i]))
+            copies[-1].start()
+        for copy in copies:
+            copy.wait()
+        small.wait()
+
+    @pl.when(first)
+    def _():
         decay = jnp.zeros((frames, chans), F32)
         for n in range(blocks):
-            slot = first[count + n * frames : count + (n + 1) * frames].astype(F32)
+            slot = half_ref[count + n * frames : count + (n + 1) * frames].astype(F32)
             decay = jnp.where(lax.axis_index("tm") == n, slot, decay)
         decay_ref[...] = decay
-
-    @pl.when(lax.rem(lax.axis_index("dp"), 2) == 0)
+        send(in_ref, in_out, decay_ref, decay_out)
+
+    @pl.when(jnp.logical_not(first))
     def _():
-        put(own_ref, other_ref)
-
-    @pl.when(lax.rem(lax.axis_index("dp"), 2) != 0)
-    def _():
-        put(other_ref, own_ref)
+        gain_ref[...] = half_ref[count : count + 16].astype(F32)[:1]
+        send(out_ref, out_out, gain_ref, gain_out)
 
 
 def video_grad_kernel(adjoint_ref, grad_ref, kernel_ref, gain_ref, video_out, out_ref, sems):
@@ -437,38 +452,33 @@
     return first, second
 
 
-def from_earlier(end, totals):
+def carried(value, totals, way):
     count = lax.axis_size("tm")
-    found, between = None, None
-    for k in range(1, count):
-        pairs = [(i, i + k) for i in range(count - k)]
-        piece = lax.ppermute(end, "tm", pairs)
-        if k == 1:
-            found = piece.astype(F32)
-        else:
-            step = lax.ppermute(totals, "tm", [(i, i + k - 1) for i in range(count - k + 1)])
-            between = step if between is None else between + step
-            found = found + jnp.exp(between) * piece.astype(F32)
-    if found is None:
-        return jnp.zeros(end.shape, BF)
+    block = lax.axis_index("tm")
+    if count == 1:
+        return jnp.zeros(value.shape, BF)
+    send = lambda v, k: lax.ppermute(v, "tm", [(i, (i + way * k) % count) for i in range(count)])
+    found = send(value, 1)
+    if count == 2:
+        return found
+    reaches = lambda k: (block >= k) if way == 1 else (block + k < count)
+    found = jnp.where(reaches(1), found.astype(F32), 0.0)
+    between = jnp.zeros_like(totals)
+    for k in range(2, count):
+        between = between + send(totals, k - 1)
+        weight = jnp.exp(jnp.minimum(between, 0.0))
+        found = found + jnp.where(reaches(k), weight * send(value, k).astype(F32), 0.0)
     return found.astype(BF)
 
 
-def from_later(lead, totals):
-    count = lax.axis_size("tm")
-    found, between = None, None
-    for k in range(1, count):
-        pairs = [(i + k, i) for i in range(count - k)]
-        piece = lax.ppermute(lead, "tm", pairs)
-        if k == 1:
-            found = piece.astype(F32)
-        else:
-            step = lax.ppermute(totals, "tm", [(i + k - 1, i) for i in range(count - k + 1)])
-            between = step if between is None else between + step
-            found = found + jnp.exp(between) * piece.astype(F32)
-    if found is None:
-        return jnp.zeros(lead.shape, BF)
-    return found.astype(BF)
+def earlier(carry_ref, rows):
+    carry = carry_ref[rows].astype(F32)
+    return jnp.where(lax.axis_index("tm") > 0, carry, 0.0)
+
+
+def later(back_ref, rows):
+    back = back_ref[rows].astype(F32)
+    return jnp.where(lax.axis_index("tm") < lax.axis_size("tm") - 1, back, 0.0)
 
 
 def tree_sum(sent, kept):
@@ -560,7 +570,7 @@
         flops=each * narrow_rows // 3,
         aliases=((0, 1),),
     )
-    carry = from_earlier(end, totals)
+    carry = carried(end, totals, 1)
     state, act, grad, gain_part = call(
         layer_kernel,
         [
@@ -570,20 +580,23 @@
             shape((1, chans), F32),
         ],
         [local, carry, reach, video, cotangent, flat(out_kernel), gain],
-        "vvvhhvv" + "hhvv",
+        "vvvhhvv" + "hvvv",
         scratch=[
             held(video),
             held(video),
             pltpu.VMEM((frames, rows + 2, cols, state_chans), BF),
-            held(video),
-            pltpu.SemaphoreType.DMA((4, frames // group_of(frames, LAYER_GROUP))),
+            pltpu.SemaphoreType.DMA((3, frames // group_of(frames, LAYER_GROUP))),
         ],
         flops=each * narrow_rows,
     )
     first, second = halo_pair(grad, 2)
-    (near,) = call(
-        near_kernel, [near_shape], [grad, flip(out_kernel)], "vvv",
-        scratch=near_scratch, flops=each * wide_rows,
+    near, act = call(
+        near_back_kernel,
+        [near_shape, shape(act.shape, BF)],
+        [grad, flip(out_kernel), act],
+        "vvv" + "vh",
+        scratch=[*near_scratch, pltpu.SemaphoreType.DMA(())],
+        flops=each * wide_rows,
     )
     (out_part,) = call(
         functools.partial(out_grad_kernel, weight_scale),
@@ -602,7 +615,7 @@
         flops=each * narrow_rows // 3,
         aliases=((0, 0),),
     )
-    back = from_later(lead, totals)
+    back = carried(lead, totals, -1)
     blocks = sizes["tm"]
     full = 9 * chans + blocks * frames
     full += -full % 64 if full % 32 else 0
@@ -634,16 +647,23 @@
         flops=each * narrow_rows,
     )
     own, other = tree_sum(sent, kept)
+    results = [
+        shape((3, 3, chans, state_chans), F32),
+        shape((3, 3, state_chans, chans), F32),
+        shape((1, chans), F32),
+        shape((frames, state_chans), F32),
+    ]
+    scratch = [*[held(r) for r in results], pltpu.SemaphoreType.DMA((4,))]
+    results = call(
+        functools.partial(result_kernel, blocks, True), results, [own], "v" + "hhhh", scratch=scratch
+    )
     in_grad, out_grad, gain_grad, decay_grad = call(
-        functools.partial(result_kernel, blocks),
-        [
-            shape((3, 3, chans, state_chans), F32),
-            shape((3, 3, state_chans, chans), F32),
-            shape((1, chans), F32),
-            shape((frames, state_chans), F32),
-        ],
-        [own, other],
-        "vv" + "vvvv",
+        functools.partial(result_kernel, blocks, False),
+        [shape(r.shape, F32) for r in results],
+        [other, *results],
+        "vhhhh" + "hhhh",
+        scratch=scratch,
+        aliases=((1, 0), (2, 1), (3, 2), (4, 3)),
     )
     return act[None], video_grad[None], in_grad, out_grad, gain_grad[0], decay_grad
 

time: 70.6 us -> 67.8 us (0.960)
  starting transfers between devices: 28.8 us -> 27.1 us
  waiting for transfers between devices: 22.7 us -> 21.5 us
    ppermute x2, starting transfers between devices: 5.01 us -> 3.33 us  [carried(): lax.ppermute(v, 'tm', [(i, (i + way * k) % count) for i in range(count)])]
    ppermute x2, waiting for transfers between devices: 5.02 us -> 3.59 us  [carried(): lax.ppermute(v, 'tm', [(i, (i + way * k) % count) for i in range(count)])]
    pallas_call x10 -> x11, Pallas kernels: 15.1 us -> 15.4 us  [call(): pl.pallas_call(body, out_shape=outs, in_specs=specs[:len(ins)], out_specs...]
  transfers between devices with their start and end apart: 16 -> 16, of which waited for: 12 -> 13; matrix products, arithmetic and copies ran while one was open for 3% -> 3% of each run, Pallas kernels for 9% -> 11%
where the time goes in v5:
time: 67.8 us; the launch traced here: 67.6 us
  starting transfers between devices  27.1 us (40%)
  waiting for transfers between devices  21.5 us (32%)
  Pallas kernels  15.4 us (23%)
  local copies, waits for them, and re-layouts  2.43 us (4%)
  between operations  1.02 us (2%)
    pallas_call x11, Pallas kernels, call(): pl.pallas_call(body, out_shape=outs, in_specs=specs[:len(ins)], out_specs...  15.4 us
    ppermute x10, starting transfers between devices, swap(): return lax.ppermute(value, axes, [(i, i ^ mask) for i in range(devices)])  14.5 us
    ppermute x10, waiting for transfers between devices, swap(): return lax.ppermute(value, axes, [(i, i ^ mask) for i in range(devices)])  13.9 us
    ppermute x2, starting transfers between devices, halo_pair(): first = lax.ppermute(first, 'rows', swap(0))  7.94 us
    ppermute x2, waiting for transfers between devices, halo_pair(): first = lax.ppermute(first, 'rows', swap(0))  3.95 us
    ppermute x2, waiting for transfers between devices, carried(): lax.ppermute(v, 'tm', [(i, (i + way * k) % count) for i in range(count)])  3.59 us
    ppermute x2, starting transfers between devices, carried(): lax.ppermute(v, 'tm', [(i, (i + way * k) % count) for i in range(count)])  3.33 us
    transpose x2, local copies, waits for them, and re-layouts, on_device(): k.transpose(0, 2, 1, 3).reshape(3 * k.shape[2], 3 * k.shape[3])  1.48 us
  transfers between devices with their start and end apart: 16, of which 13 were waited for; matrix products, arithmetic and copies ran while one was open for 3% of the time, Pallas kernels for 11%

profile of v5, /device:TPU:0, one launch (start us, length us, event | category | flops | bytes accessed | tf_op | source)
XLA Modules:
  0.0 67.6 jit_solution(17599103914274830112)
XLA Ops:
  0.6 1.1 %shard_map.110 = (bf16[16,2,32,128]{3,2,1,0:T(8,128)(2,1)S(1)}, bf16[16,2,32,128]{3,2,1,0:T(8,128)(2,1)S(1)}) custom-call(bf16[16,4,32,128]{3,2,1,0:T(8,128)(2,1)} %bitcast.36), custom_call_target="tpu_custom_call" | custom-call | bytes 1048576 | tf_op jit(solution)/shard_map/pallas_call | solution.py:33
  1.8 3.1 %collective-permute-start = (bf16[16,2,32,128]{3,2,1,0:T(8,128)(2,1)S(1)}, bf16[16,2,32,128]{3,2,1,0:T(8,128)(2,1)S(1)}, u32[]{:S(2)}, u32[]{:S(2)}) collective-permute-start(bf16[16,2,32,128]{3,2,1,0:T(8,128)(2,1)S(1)} %get-tuple-element.34), channel_id=1, source_target_pairs={{0,4},{4,0},{8,12},{12,8},{1,5},{5,1},{9,13},{13,9},{2,6},{6,2},{1... | collective-permute-start | bytes 786440 | tf_op jit(solution)/shard_map/ppermute | solution.py:450
  5.6 1.2 %copy.22 = bf16[3,128,3,128]{3,2,1,0:T(4,128)(2,1)S(1)} copy(bf16[3,128,3,128]{3,1,2,0:T(8,128)(2,1)} %bitcast.56) | data formatting | bytes 589824 | tf_op jit(solution)/shard_map/transpose | solution.py:540
  6.9 1.8 %shard_map.109.near_ref = f32[16,6,32,128]{3,2,1,0:T(8,128)S(1)} custom-call(bf16[16,4,32,128]{3,2,1,0:T(8,128)(2,1)S(1)} %bitcast.38, bf16[384,384]{1,0:T(8,128)(2,1)S(1)} %bitcast.43), custom_call_target="tpu_custom_call" | custom-call | flops 905969664 | bytes 2392064 | tf_op jit(solution)/shard_map/pallas_call | solution.py:33
  8.7 2.5 %collective-permute-done.first_ref = bf16[16,2,32,128]{3,2,1,0:T(8,128)(2,1)S(1)} collective-permute-done((bf16[16,2,32,128]{3,2,1,0:T(8,128)(2,1)S(1)}, bf16[16,2,32,128]{3,2,1,0:T(8,128)(2,1)S(1)}, u32[]{:S(2)}, u32[]{:S(2)}) %collective-permute-start) | collective-permute-done | bytes 262176 | tf_op jit(solution)/shard_map/ppermute | solution.py:450
  11.2 1.1 %shard_map.111 = (bf16[16,8,32,128]{3,2,1,0:T(8,128)(2,1)}, f32[16,6,32,128]{3,2,1,0:T(8,128)S(1)}, bf16[6,32,128]{2,1,0:T(8,128)(2,1)S(1)}) custom-call(f32[16,6,32,128]{3,2,1,0:T(8,128)S(1)} %shard_map.109.near_ref, bf16[16,4,32,128]{3,2,1,0:T(8,128)(2,1)S(1)} %bitcast.39, ...), custom_call_target="tpu_custom_call", output_to_operand_aliasing={{1}: (0, {})} | custom-call | flops 201326592 | bytes 5595136 | tf_op jit(solution)/shard_map/pallas_call | solution.py:33
  12.3 1.7 %collective-permute-start.2 = (bf16[6,32,128]{2,1,0:T(8,128)(2,1)S(1)}, bf16[6,32,128]{2,1,0:T(8,128)(2,1)S(1)}, u32[]{:S(2)}, u32[]{:S(2)}) collective-permute-start(bf16[6,32,128]{2,1,0:T(8,128)(2,1)S(1)} %get-tuple-element.37), channel_id=1, source_target_pairs={{0,16},{16,0},{1,17},{17,1},{2,18},{18,2},{3,19},{19,3},{4,20},{20... | collective-permute-start | bytes 147464 | tf_op jit(solution)/shard_map/ppermute | solution.py:460
  14.4 2.0 %collective-permute-done.2.carry_ref = bf16[6,32,128]{2,1,0:T(8,128)(2,1)S(1)} collective-permute-done((bf16[6,32,128]{2,1,0:T(8,128)(2,1)S(1)}, bf16[6,32,128]{2,1,0:T(8,128)(2,1)S(1)}, u32[]{:S(2)}, u32[]{:S(2)}) %collective-permute-start.2) | collective-permute-done | bytes 49184 | tf_op jit(solution)/shard_map/ppermute | solution.py:460
  16.4 2.7 %shard_map.112 = (bf16[16,6,32,128]{3,2,1,0:T(8,128)(2,1)}, bf16[16,4,32,128]{3,2,1,0:T(8,128)(2,1)S(1)}, bf16[16,4,32,128]{3,2,1,0:T(8,128)(2,1)S(1)}, f32[1,128]{1,0:T(1,128)S(1)}) custom-call(f32[16,6,32,128]{3,2,1,0:T(8,128)S(1)} %get-tuple-element.36.local_ref, bf16[6,32,128]{2,1,0:T(8,128)(2,1)S(1)} %collective-permute-done.2.carry_ref, ...), custom_call_target="tpu_custom_call" | custom-call | flops 603979776 | bytes 4809728 | tf_op jit(solution)/shard_map/pallas_call | solution.py:33
  19.2 4.8 %collective-permute-start.3 = (bf16[16,2,32,128]{3,2,1,0:T(8,128)(2,1)S(1)}, bf16[16,2,32,128]{3,2,1,0:T(8,128)(2,1)S(1)}, u32[]{:S(2)}, u32[]{:S(2)}) collective-permute-start(bf16[16,2,32,128]{3,2,1,0:T(8,128)(2,1)S(1)} %get-tuple-element.68), channel_id=1, source_target_pairs={{0,4},{4,0},{8,12},{12,8},{1,5},{5,1},{9,13},{13,9},{2,6},{6,2},{1... | collective-permute-start | bytes 786440 | tf_op jit(solution)/shard_map/ppermute | solution.py:450
  25.0 1.8 %shard_map.113 = (f32[16,6,32,128]{3,2,1,0:T(8,128)S(1)}, bf16[16,4,32,128]{3,2,1,0:T(8,128)(2,1)}) custom-call(bf16[16,4,32,128]{3,2,1,0:T(8,128)(2,1)S(1)} %get-tuple-element.38.own_ref.grad_ref, bf16[384,384]{1,0:T(8,128)(2,1)S(1)} %bitcast.41, bf16[16,4,32,128]{3,2,1,0:T(8,128)(2,1)S(1)} %get-tuple-element.39.act_ref), custom_call_target="tpu_custom_call" | custom-call | flops 905969664 | bytes 3440640 | tf_op jit(solution)/shard_map/pallas_call | solution.py:33
  26.9 1.5 %collective-permute-done.3.first_ref = bf16[16,2,32,128]{3,2,1,0:T(8,128)(2,1)S(1)} collective-permute-done((bf16[16,2,32,128]{3,2,1,0:T(8,128)(2,1)S(1)}, bf16[16,2,32,128]{3,2,1,0:T(8,128)(2,1)S(1)}, u32[]{:S(2)}, u32[]{:S(2)}) %collective-permute-start.3) | collective-permute-done | bytes 262176 | tf_op jit(solution)/shard_map/ppermute | solution.py:450
  28.4 0.9 %shard_map.114 = (f32[16,6,32,128]{3,2,1,0:T(8,128)S(1)}, bf16[6,32,128]{2,1,0:T(8,128)(2,1)S(1)}) custom-call(f32[16,6,32,128]{3,2,1,0:T(8,128)S(1)} %get-tuple-element.41.near_ref, bf16[16,2,32,128]{3,2,1,0:T(8,128)(2,1)S(1)} %collective-permute-done.3.first_ref, ...), custom_call_target="tpu_custom_call", output_to_operand_aliasing={{0}: (0, {})} | custom-call | flops 201326592 | bytes 4022272 | tf_op jit(solution)/shard_map/pallas_call | solution.py:33
  29.3 1.6 %collective-permute-start.5 = (bf16[6,32,128]{2,1,0:T(8,128)(2,1)S(1)}, bf16[6,32,128]{2,1,0:T(8,128)(2,1)S(1)}, u32[]{:S(2)}, u32[]{:S(2)}) collective-permute-start(bf16[6,32,128]{2,1,0:T(8,128)(2,1)S(1)} %get-tuple-element.43), channel_id=1, source_target_pairs={{0,16},{16,0},{1,17},{17,1},{2,18},{18,2},{3,19},{19,3},{4,20},{20... | collective-permute-start | bytes 147464 | tf_op jit(solution)/shard_map/ppermute | solution.py:460
  30.9 1.0 %shard_map.115.other_ref = f32[1152,128]{1,0:T(8,128)S(1)} custom-call(bf16[16,6,32,128]{3,2,1,0:T(8,128)(2,1)S(1)} %copy-done.2, bf16[16,4,32,128]{3,2,1,0:T(8,128)(2,1)S(1)} %get-tuple-element.38.own_ref.grad_ref), custom_call_target="tpu_custom_call" | custom-call | flops 603979776 | bytes 1900544 | tf_op jit(solution)/shard_map/pallas_call | solution.py:33
  31.9 1.6 %collective-permute-done.5.back_ref = bf16[6,32,128]{2,1,0:T(8,128)(2,1)S(1)} collective-permute-done((bf16[6,32,128]{2,1,0:T(8,128)(2,1)S(1)}, bf16[6,32,128]{2,1,0:T(8,128)(2,1)S(1)}, u32[]{:S(2)}, u32[]{:S(2)}) %collective-permute-start.5) | collective-permute-done | bytes 49184 | tf_op jit(solution)/shard_map/ppermute | solution.py:460
  33.5 1.1 %shard_map.116 = (bf16[16,6,32,128]{3,2,1,0:T(8,128)(2,1)S(1)}, bf16[1184,128]{1,0:T(8,128)(2,1)S(1)}, f32[1184,128]{1,0:T(8,128)S(1)}) custom-call(f32[16,6,32,128]{3,2,1,0:T(8,128)S(1)} %get-tuple-element.42.local_ref, bf16[6,32,128]{2,1,0:T(8,128)(2,1)S(1)} %collective-permute-done.5.back_ref, f32[16,1,128]{2,1,0:T(1,128)S(1)} %get-tuple-element.69.reach_ref, ...), custom_call_target="tpu_custom_call" | custom-call | flops 603979776 | bytes 5808640 | tf_op jit(solution)/shard_map/pallas_call | solution.py:33
  34.7 1.5 %collective-permute-done.6 = bf16[1184,128]{1,0:T(8,128)(2,1)S(1)} collective-permute-done((bf16[1184,128]{1,0:T(8,128)(2,1)S(1)}, bf16[1184,128]{1,0:T(8,128)(2,1)S(1)}, u32[]{:S(2)}, u32[]{:S(2)}) %collective-permute-start.6) | collective-permute-done | bytes 303136 | tf_op jit(solution)/shard_map/ppermute | solution.py:498
  36.4 2.5 %collective-permute-start.9 = (bf16[296,128]{1,0:T(8,128)(2,1)S(1)}, bf16[296,128]{1,0:T(8,128)(2,1)S(1)}, u32[]{:S(2)}, u32[]{:S(2)}) collective-permute-start(bf16[296,128]{1,0:T(8,128)(2,1)S(1)} %get-tuple-element.53), channel_id=1, source_target_pairs={{0,18},{1,19},{2,16},{3,17},{4,22},{5,23},{6,20},{7,21},{8,26},{9,... | collective-permute-start | bytes 227336 | tf_op jit(solution)/shard_map/ppermute | solution.py:498
  40.0 1.8 %collective-permute-done.9 = bf16[296,128]{1,0:T(8,128)(2,1)S(1)} collective-permute-done((bf16[296,128]{1,0:T(8,128)(2,1)S(1)}, bf16[296,128]{1,0:T(8,128)(2,1)S(1)}, u32[]{:S(2)}, u32[]{:S(2)}) %collective-permute-start.9) | collective-permute-done | bytes 75808 | tf_op jit(solution)/shard_map/ppermute | solution.py:498
  41.8 1.6 %collective-permute-done.8 = bf16[296,128]{1,0:T(8,128)(2,1)S(1)} collective-permute-done((bf16[296,128]{1,0:T(8,128)(2,1)S(1)}, bf16[296,128]{1,0:T(8,128)(2,1)S(1)}, u32[]{:S(2)}, u32[]{:S(2)}) %collective-permute-start.8) | collective-permute-done | bytes 75808 | tf_op jit(solution)/shard_map/ppermute | solution.py:498
  43.9 4.0 %collective-permute-start.10 = (bf16[296,128]{1,0:T(8,128)(2,1)S(1)}, bf16[296,128]{1,0:T(8,128)(2,1)S(1)}, u32[]{:S(2)}, u32[]{:S(2)}) collective-permute-start(bf16[296,128]{1,0:T(8,128)(2,1)S(1)} %add_convert_fusion.2), channel_id=1, source_target_pairs={{0,4},{1,5},{2,6},{3,7},{4,0},{5,1},{6,2},{7,3},{8,12},{9,13},{10,... | collective-permute-start | bytes 227336 | tf_op jit(solution)/shard_map/ppermute | solution.py:498
  47.9 2.4 %collective-permute-done.10 = bf16[296,128]{1,0:T(8,128)(2,1)S(1)} collective-permute-done((bf16[296,128]{1,0:T(8,128)(2,1)S(1)}, bf16[296,128]{1,0:T(8,128)(2,1)S(1)}, u32[]{:S(2)}, u32[]{:S(2)}) %collective-permute-start.10) | collective-permute-done | bytes 75808 | tf_op jit(solution)/shard_map/ppermute | solution.py:498
  50.3 3.3 %collective-permute-start.11 = (bf16[296,128]{1,0:T(8,128)(2,1)S(1)}, bf16[296,128]{1,0:T(8,128)(2,1)S(1)}, u32[]{:S(2)}, u32[]{:S(2)}) collective-permute-start(bf16[296,128]{1,0:T(8,128)(2,1)S(1)} %add_convert_fusion.1), channel_id=1, source_target_pairs={{0,8},{1,9},{2,10},{3,11},{4,12},{5,13},{6,14},{7,15},{8,0},{9,1},... | collective-permute-start | bytes 227336 | tf_op jit(solution)/shard_map/ppermute | solution.py:498
  53.5 2.4 %collective-permute-done.11 = bf16[296,128]{1,0:T(8,128)(2,1)S(1)} collective-permute-done((bf16[296,128]{1,0:T(8,128)(2,1)S(1)}, bf16[296,128]{1,0:T(8,128)(2,1)S(1)}, u32[]{:S(2)}, u32[]{:S(2)}) %collective-permute-start.11) | collective-permute-done | bytes 75808 | tf_op jit(solution)/shard_map/ppermute | solution.py:498
  56.0 1.2 %collective-permute-start.12 = (bf16[296,128]{1,0:T(8,128)(2,1)S(1)}, bf16[296,128]{1,0:T(8,128)(2,1)S(1)}, u32[]{:S(2)}, u32[]{:S(2)}) collective-permute-start(bf16[296,128]{1,0:T(8,128)(2,1)S(1)} %get-tuple-element.63), channel_id=1, source_target_pairs={{0,2},{1,3},{2,0},{3,1},{4,6},{5,7},{6,4},{7,5},{8,10},{9,11},{10,... | collective-permute-start | bytes 227336 | tf_op jit(solution)/shard_map/ppermute | solution.py:498
  57.1 0.9 %collective-permute-start.13 = (bf16[296,128]{1,0:T(8,128)(2,1)S(1)}, bf16[296,128]{1,0:T(8,128)(2,1)S(1)}, u32[]{:S(2)}, u32[]{:S(2)}) collective-permute-start(bf16[296,128]{1,0:T(8,128)(2,1)S(1)} %get-tuple-element.63), channel_id=1, source_target_pairs={{0,16},{1,17},{2,18},{3,19},{4,20},{5,21},{6,22},{7,23},{8,24},{9,... | collective-permute-start | bytes 227336 | tf_op jit(solution)/shard_map/ppermute | solution.py:498
  58.1 1.4 %collective-permute-start.14 = (bf16[296,128]{1,0:T(8,128)(2,1)S(1)}, bf16[296,128]{1,0:T(8,128)(2,1)S(1)}, u32[]{:S(2)}, u32[]{:S(2)}) collective-permute-start(bf16[296,128]{1,0:T(8,128)(2,1)S(1)} %get-tuple-element.63), channel_id=1, source_target_pairs={{0,18},{1,19},{2,16},{3,17},{4,22},{5,23},{6,20},{7,21},{8,26},{9,... | collective-permute-start | bytes 227336 | tf_op jit(solution)/shard_map/ppermute | solution.py:498
  59.5 0.9 %collective-permute-done.12 = bf16[296,128]{1,0:T(8,128)(2,1)S(1)} collective-permute-done((bf16[296,128]{1,0:T(8,128)(2,1)S(1)}, bf16[296,128]{1,0:T(8,128)(2,1)S(1)}, u32[]{:S(2)}, u32[]{:S(2)}) %collective-permute-start.12) | collective-permute-done | bytes 75808 | tf_op jit(solution)/shard_map/ppermute | solution.py:498
  60.4 1.1 %collective-permute-done.13 = bf16[296,128]{1,0:T(8,128)(2,1)S(1)} collective-permute-done((bf16[296,128]{1,0:T(8,128)(2,1)S(1)}, bf16[296,128]{1,0:T(8,128)(2,1)S(1)}, u32[]{:S(2)}, u32[]{:S(2)}) %collective-permute-start.13) | collective-permute-done | bytes 75808 | tf_op jit(solution)/shard_map/ppermute | solution.py:498
  61.5 1.8 %collective-permute-done.14 = bf16[296,128]{1,0:T(8,128)(2,1)S(1)} collective-permute-done((bf16[296,128]{1,0:T(8,128)(2,1)S(1)}, bf16[296,128]{1,0:T(8,128)(2,1)S(1)}, u32[]{:S(2)}, u32[]{:S(2)}) %collective-permute-start.14) | collective-permute-done | bytes 75808 | tf_op jit(solution)/shard_map/ppermute | solution.py:498
  63.8 2.0 %shard_map.117 = bf16[16,4,32,128]{3,2,1,0:T(8,128)(2,1)} custom-call(bf16[16,6,32,128]{3,2,1,0:T(8,128)(2,1)S(1)} %get-tuple-element.47.adjoint_ref, bf16[16,4,32,128]{3,2,1,0:T(8,128)(2,1)S(1)} %get-tuple-element.38.own_ref.grad_ref, bf16[384,384]{1,0:T(8,128)(2,1)S(1)} %bitcast.45, f32[1,128]{1,0:T(1,128)S(1)} %bitcast.50), custom_call_target="tpu_custom_call" | custom-call | flops 603979776 | bytes 2130432 | tf_op jit(solution)/shard_map/pallas_call | solution.py:33
  (52 shorter events, 6.1 us)
Async XLA Ops:
  0.6 6.2 %copy-start = (bf16[1,16,4,32,128]{4,3,2,1,0:T(8,128)(2,1)S(1)}, bf16[1,16,4,32,128]{4,3,2,1,0:T(8,128)(2,1)}, u32[]{:S(2)}) copy-start(bf16[1,16,4,32,128]{4,3,2,1,0:T(8,128)(2,1)} %param.6) | copy-start | bytes 1572868
  1.8 9.4 %collective-permute-start = (bf16[16,2,32,128]{3,2,1,0:T(8,128)(2,1)S(1)}, bf16[16,2,32,128]{3,2,1,0:T(8,128)(2,1)S(1)}, u32[]{:S(2)}, u32[]{:S(2)}) collective-permute-start(bf16[16,2,32,128]{3,2,1,0:T(8,128)(2,1)S(1)} %get-tuple-element.34), channel_id=1, source_target_pairs={{0,4},{4,0},{8,12},{12,8},{1,5},{5,1},{9,13},{13,9},{2,6},{6,2},{1... | collective-permute-start | bytes 786440 | tf_op jit(solution)/shard_map/ppermute | solution.py:450
  4.9 6.3 %collective-permute-start.1 = (bf16[16,2,32,128]{3,2,1,0:T(8,128)(2,1)S(1)}, bf16[16,2,32,128]{3,2,1,0:T(8,128)(2,1)S(1)}, u32[]{:S(2)}, u32[]{:S(2)}) collective-permute-start(bf16[16,2,32,128]{3,2,1,0:T(8,128)(2,1)S(1)} %get-tuple-element.35), channel_id=1, source_target_pairs={{4,8},{8,4},{5,9},{9,5},{6,10},{10,6},{7,11},{11,7},{20,24},{24,20... | collective-permute-start | bytes 786440 | tf_op jit(solution)/shard_map/ppermute | solution.py:451
  6.8 1.8 %copy-start.7 = (f32[16,128]{1,0:T(8,128)S(1)}, f32[16,128]{1,0:T(8,128)}, u32[]{:S(2)}) copy-start(f32[16,128]{1,0:T(8,128)} %param.11) | copy-start | bytes 24580
  11.2 2.9 %copy-start.4 = (bf16[3,3,128,128]{3,2,1,0:T(8,128)(2,1)S(1)}, bf16[3,3,128,128]{3,2,1,0:T(8,128)(2,1)}, u32[]{:S(2)}) copy-start(bf16[3,3,128,128]{3,2,1,0:T(8,128)(2,1)} %param.9) | copy-start | bytes 884740
  11.2 5.2 %copy-start.3 = (f32[128]{0:T(128)S(1)}, f32[128]{0:T(128)}, u32[]{:S(2)}) copy-start(f32[128]{0:T(128)} %param.10) | copy-start | bytes 1540
  12.3 4.2 %collective-permute-start.2 = (bf16[6,32,128]{2,1,0:T(8,128)(2,1)S(1)}, bf16[6,32,128]{2,1,0:T(8,128)(2,1)S(1)}, u32[]{:S(2)}, u32[]{:S(2)}) collective-permute-start(bf16[6,32,128]{2,1,0:T(8,128)(2,1)S(1)} %get-tuple-element.37), channel_id=1, source_target_pairs={{0,16},{16,0},{1,17},{17,1},{2,18},{18,2},{3,19},{19,3},{4,20},{20... | collective-permute-start | bytes 147464 | tf_op jit(solution)/shard_map/ppermute | solution.py:460
  16.4 8.3 %copy-start.5 = (bf16[3,3,128,128]{3,2,1,0:T(8,128)(2,1)S(1)}, bf16[3,3,128,128]{3,2,1,0:T(8,128)(2,1)}, u32[]{:S(2)}) copy-start(bf16[3,3,128,128]{3,2,1,0:T(8,128)(2,1)} %param.9) | copy-start | bytes 884740
  19.2 9.2 %collective-permute-start.3 = (bf16[16,2,32,128]{3,2,1,0:T(8,128)(2,1)S(1)}, bf16[16,2,32,128]{3,2,1,0:T(8,128)(2,1)S(1)}, u32[]{:S(2)}, u32[]{:S(2)}) collective-permute-start(bf16[16,2,32,128]{3,2,1,0:T(8,128)(2,1)S(1)} %get-tuple-element.68), channel_id=1, source_target_pairs={{0,4},{4,0},{8,12},{12,8},{1,5},{5,1},{9,13},{13,9},{2,6},{6,2},{1... | collective-permute-start | bytes 786440 | tf_op jit(solution)/shard_map/ppermute | solution.py:450
  24.0 4.4 %collective-permute-start.4 = (bf16[16,2,32,128]{3,2,1,0:T(8,128)(2,1)S(1)}, bf16[16,2,32,128]{3,2,1,0:T(8,128)(2,1)S(1)}, u32[]{:S(2)}, u32[]{:S(2)}) collective-permute-start(bf16[16,2,32,128]{3,2,1,0:T(8,128)(2,1)S(1)} %get-tuple-element.67), channel_id=1, source_target_pairs={{4,8},{8,4},{5,9},{9,5},{6,10},{10,6},{7,11},{11,7},{20,24},{24,20... | collective-permute-start | bytes 786440 | tf_op jit(solution)/shard_map/ppermute | solution.py:451
  26.9 4.0 %copy-start.2 = (bf16[16,6,32,128]{3,2,1,0:T(8,128)(2,1)S(1)}, bf16[16,6,32,128]{3,2,1,0:T(8,128)(2,1)}, u32[]{:S(2)}) copy-start(bf16[16,6,32,128]{3,2,1,0:T(8,128)(2,1)} %get-tuple-element.45.state_ref) | copy-start | bytes 2359300
  29.3 4.2 %copy-start.1 = (bf16[16,8,32,128]{3,2,1,0:T(8,128)(2,1)S(1)}, bf16[16,8,32,128]{3,2,1,0:T(8,128)(2,1)}, u32[]{:S(2)}) copy-start(bf16[16,8,32,128]{3,2,1,0:T(8,128)(2,1)} %get-tuple-element.44.wide_ref) | copy-start | bytes 3145732
  29.3 4.2 %collective-permute-start.5 = (bf16[6,32,128]{2,1,0:T(8,128)(2,1)S(1)}, bf16[6,32,128]{2,1,0:T(8,128)(2,1)S(1)}, u32[]{:S(2)}, u32[]{:S(2)}) collective-permute-start(bf16[6,32,128]{2,1,0:T(8,128)(2,1)S(1)} %get-tuple-element.43), channel_id=1, source_target_pairs={{0,16},{16,0},{1,17},{17,1},{2,18},{18,2},{3,19},{19,3},{4,20},{20... | collective-permute-start | bytes 147464 | tf_op jit(solution)/shard_map/ppermute | solution.py:460
  34.6 1.7 %collective-permute-start.6 = (bf16[1184,128]{1,0:T(8,128)(2,1)S(1)}, bf16[1184,128]{1,0:T(8,128)(2,1)S(1)}, u32[]{:S(2)}, u32[]{:S(2)}) collective-permute-start(bf16[1184,128]{1,0:T(8,128)(2,1)S(1)} %get-tuple-element.49), channel_id=1, source_target_pairs={{0,1},{1,0},{2,3},{3,2},{4,5},{5,4},{6,7},{7,6},{8,9},{9,8},{10,11... | collective-permute-start | bytes 909320 | tf_op jit(solution)/shard_map/ppermute | solution.py:498
  36.4 27.1 %copy-start.6 = (bf16[3,3,128,128]{3,2,1,0:T(8,128)(2,1)S(1)}, bf16[3,3,128,128]{3,2,1,0:T(8,128)(2,1)}, u32[]{:S(2)}) copy-start(bf16[3,3,128,128]{3,2,1,0:T(8,128)(2,1)} %param.8) | copy-start | bytes 884740
  36.4 5.4 %collective-permute-start.9 = (bf16[296,128]{1,0:T(8,128)(2,1)S(1)}, bf16[296,128]{1,0:T(8,128)(2,1)S(1)}, u32[]{:S(2)}, u32[]{:S(2)}) collective-permute-start(bf16[296,128]{1,0:T(8,128)(2,1)S(1)} %get-tuple-element.53), channel_id=1, source_target_pairs={{0,18},{1,19},{2,16},{3,17},{4,22},{5,23},{6,20},{7,21},{8,26},{9,... | collective-permute-start | bytes 227336 | tf_op jit(solution)/shard_map/ppermute | solution.py:498
  39.0 4.4 %collective-permute-start.8 = (bf16[296,128]{1,0:T(8,128)(2,1)S(1)}, bf16[296,128]{1,0:T(8,128)(2,1)S(1)}, u32[]{:S(2)}, u32[]{:S(2)}) collective-permute-start(bf16[296,128]{1,0:T(8,128)(2,1)S(1)} %get-tuple-element.52), channel_id=1, source_target_pairs={{0,16},{1,17},{2,18},{3,19},{4,20},{5,21},{6,22},{7,23},{8,24},{9,... | collective-permute-start | bytes 227336 | tf_op jit(solution)/shard_map/ppermute | solution.py:498
  39.5 4.4 %collective-permute-start.7 = (bf16[296,128]{1,0:T(8,128)(2,1)S(1)}, bf16[296,128]{1,0:T(8,128)(2,1)S(1)}, u32[]{:S(2)}, u32[]{:S(2)}) collective-permute-start(bf16[296,128]{1,0:T(8,128)(2,1)S(1)} %get-tuple-element.51), channel_id=1, source_target_pairs={{0,2},{1,3},{2,0},{3,1},{4,6},{5,7},{6,4},{7,5},{8,10},{9,11},{10,... | collective-permute-start | bytes 227336 | tf_op jit(solution)/shard_map/ppermute | solution.py:498
  43.9 6.3 %collective-permute-start.10 = (bf16[296,128]{1,0:T(8,128)(2,1)S(1)}, bf16[296,128]{1,0:T(8,128)(2,1)S(1)}, u32[]{:S(2)}, u32[]{:S(2)}) collective-permute-start(bf16[296,128]{1,0:T(8,128)(2,1)S(1)} %add_convert_fusion.2), channel_id=1, source_target_pairs={{0,4},{1,5},{2,6},{3,7},{4,0},{5,1},{6,2},{7,3},{8,12},{9,13},{10,... | collective-permute-start | bytes 227336 | tf_op jit(solution)/shard_map/ppermute | solution.py:498
  50.3 5.6 %collective-permute-start.11 = (bf16[296,128]{1,0:T(8,128)(2,1)S(1)}, bf16[296,128]{1,0:T(8,128)(2,1)S(1)}, u32[]{:S(2)}, u32[]{:S(2)}) collective-permute-start(bf16[296,128]{1,0:T(8,128)(2,1)S(1)} %add_convert_fusion.1), channel_id=1, source_target_pairs={{0,8},{1,9},{2,10},{3,11},{4,12},{5,13},{6,14},{7,15},{8,0},{9,1},... | collective-permute-start | bytes 227336 | tf_op jit(solution)/shard_map/ppermute | solution.py:498
  56.0 4.4 %collective-permute-start.12 = (bf16[296,128]{1,0:T(8,128)(2,1)S(1)}, bf16[296,128]{1,0:T(8,128)(2,1)S(1)}, u32[]{:S(2)}, u32[]{:S(2)}) collective-permute-start(bf16[296,128]{1,0:T(8,128)(2,1)S(1)} %get-tuple-element.63), channel_id=1, source_target_pairs={{0,2},{1,3},{2,0},{3,1},{4,6},{5,7},{6,4},{7,5},{8,10},{9,11},{10,... | collective-permute-start | bytes 227336 | tf_op jit(solution)/shard_map/ppermute | solution.py:498
  57.1 4.4 %collective-permute-start.13 = (bf16[296,128]{1,0:T(8,128)(2,1)S(1)}, bf16[296,128]{1,0:T(8,128)(2,1)S(1)}, u32[]{:S(2)}, u32[]{:S(2)}) collective-permute-start(bf16[296,128]{1,0:T(8,128)(2,1)S(1)} %get-tuple-element.63), channel_id=1, source_target_pairs={{0,16},{1,17},{2,18},{3,19},{4,20},{5,21},{6,22},{7,23},{8,24},{9,... | collective-permute-start | bytes 227336 | tf_op jit(solution)/shard_map/ppermute | solution.py:498
  58.1 5.3 %collective-permute-start.14 = (bf16[296,128]{1,0:T(8,128)(2,1)S(1)}, bf16[296,128]{1,0:T(8,128)(2,1)S(1)}, u32[]{:S(2)}, u32[]{:S(2)}) collective-permute-start(bf16[296,128]{1,0:T(8,128)(2,1)S(1)} %get-tuple-element.63), channel_id=1, source_target_pairs={{0,18},{1,19},{2,16},{3,17},{4,22},{5,23},{6,20},{7,21},{8,26},{9,... | collective-permute-start | bytes 227336 | tf_op jit(solution)/shard_map/ppermute | solution.py:498
  63.4 3.4 %collective-permute-start.15 = (bf16[1184,128]{1,0:T(8,128)(2,1)S(1)}, bf16[1184,128]{1,0:T(8,128)(2,1)S(1)}, u32[]{:S(2)}, u32[]{:S(2)}) collective-permute-start(bf16[1184,128]{1,0:T(8,128)(2,1)S(1)} %constant_dynamic-update-slice_fusion.refs_0_), channel_id=1, source_target_pairs={{0,1},{1,0},{2,3},{3,2},{4,5},{5,4},{6,7},{7,6},{8,9},{9,8},{10,11... | collective-permute-start | bytes 909320 | tf_op jit(solution)/shard_map/ppermute | solution.py:498

commit v6 on v5

--- a/solution.py
+++ b/solution.py
@@ -14,8 +14,8 @@
 LAYER_GROUP = 8
 LAST_GROUP = 8
 OUTER_GROUP = 16
-NEAR_GROUP = 8
-SCAN_GROUP = 4
+NEAR_GROUP = 16
+SCAN_GROUP = 8
 GELU_A = math.sqrt(2.0 / math.pi)
 GELU_B = 0.044715
 
@@ -513,8 +513,14 @@
     for piece in found:
         total = total + piece.astype(F32)
     total = total.astype(BF)
-    for _, _, mask in far:
-        total = (total.astype(F32) + swap(total, mask).astype(F32)).astype(BF)
+    while far:
+        (_, _, one), *far = far
+        if far:
+            (_, _, two), *far = far
+            swapped = [swap(total, m).astype(F32) for m in (one, two, one + two)]
+            total = ((total.astype(F32) + swapped[0]) + (swapped[1] + swapped[2])).astype(BF)
+        else:
+            total = (total.astype(F32) + swap(total, one).astype(F32)).astype(BF)
     found = [total] + [swap(total, combined(k)) for k in range(1, ways)]
     own = jnp.zeros(sent.shape, BF)
     for k, piece in enumerate(found):

time: 67.8 us -> 66.5 us (0.981)
  starting transfers between devices: 27.1 us -> 25.6 us
    ppermute x10 -> x11, starting transfers between devices: 14.5 us -> 13 us  [swap(): return lax.ppermute(value, axes, [(i, i ^ mask) for i in range(devices)])]
    ppermute x10 -> x11, waiting for transfers between devices: 13.9 us -> 14.1 us  [swap(): return lax.ppermute(value, axes, [(i, i ^ mask) for i in range(devices)])]
  transfers between devices with their start and end apart: 16 -> 17, of which waited for: 13 -> 13; matrix products, arithmetic and copies ran while one was open for 3% -> 3% of each run, Pallas kernels for 11% -> 11%
where the time goes in v6:
time: 66.5 us; the launch traced here: 66.3 us
  starting transfers between devices  25.6 us (38%)
  waiting for transfers between devices  22 us (33%)
  Pallas kernels  15.1 us (23%)
  local copies, waits for them, and re-layouts  2.43 us (4%)
  between operations  1.02 us (2%)
    pallas_call x11, Pallas kernels, call(): pl.pallas_call(body, out_shape=outs, in_specs=specs[:len(ins)], out_specs...  15.1 us
    ppermute x11, waiting for transfers between devices, swap(): return lax.ppermute(value, axes, [(i, i ^ mask) for i in range(devices)])  14.1 us
    ppermute x11, starting transfers between devices, swap(): return lax.ppermute(value, axes, [(i, i ^ mask) for i in range(devices)])  13 us
    ppermute x2, starting transfers between devices, halo_pair(): first = lax.ppermute(first, 'rows', swap(0))  7.94 us
    ppermute x2, waiting for transfers between devices, halo_pair(): first = lax.ppermute(first, 'rows', swap(0))  4.28 us
    ppermute x2, waiting for transfers between devices, carried(): lax.ppermute(v, 'tm', [(i, (i + way * k) % count) for i in range(count)])  3.59 us
    ppermute x2, starting transfers between devices, carried(): lax.ppermute(v, 'tm', [(i, (i + way * k) % count) for i in range(count)])  3.33 us
    transpose x2, local copies, waits for them, and re-layouts, on_device(): k.transpose(0, 2, 1, 3).reshape(3 * k.shape[2], 3 * k.shape[3])  1.48 us
  transfers between devices with their start and end apart: 17, of which 13 were waited for; matrix products, arithmetic and copies ran while one was open for 3% of the time, Pallas kernels for 11%

profile of v6, /device:TPU:0, one launch (start us, length us, event | category | flops | bytes accessed | tf_op | source)
XLA Modules:
  0.0 66.3 jit_solution(6418578561335890813)
XLA Ops:
  0.6 1.1 %shard_map.110 = (bf16[16,2,32,128]{3,2,1,0:T(8,128)(2,1)S(1)}, bf16[16,2,32,128]{3,2,1,0:T(8,128)(2,1)S(1)}) custom-call(bf16[16,4,32,128]{3,2,1,0:T(8,128)(2,1)} %bitcast.36), custom_call_target="tpu_custom_call" | custom-call | bytes 1048576 | tf_op jit(solution)/shard_map/pallas_call | solution.py:33
  1.8 3.1 %collective-permute-start = (bf16[16,2,32,128]{3,2,1,0:T(8,128)(2,1)S(1)}, bf16[16,2,32,128]{3,2,1,0:T(8,128)(2,1)S(1)}, u32[]{:S(2)}, u32[]{:S(2)}) collective-permute-start(bf16[16,2,32,128]{3,2,1,0:T(8,128)(2,1)S(1)} %get-tuple-element.34), channel_id=1, source_target_pairs={{0,4},{4,0},{8,12},{12,8},{1,5},{5,1},{9,13},{13,9},{2,6},{6,2},{1... | collective-permute-start | bytes 786440 | tf_op jit(solution)/shard_map/ppermute | solution.py:450
  5.6 1.2 %copy.22 = bf16[3,128,3,128]{3,2,1,0:T(4,128)(2,1)S(1)} copy(bf16[3,128,3,128]{3,1,2,0:T(8,128)(2,1)} %bitcast.56) | data formatting | bytes 589824 | tf_op jit(solution)/shard_map/transpose | solution.py:546
  6.9 1.6 %shard_map.109.near_ref = f32[16,6,32,128]{3,2,1,0:T(8,128)S(1)} custom-call(bf16[16,4,32,128]{3,2,1,0:T(8,128)(2,1)S(1)} %bitcast.38, bf16[384,384]{1,0:T(8,128)(2,1)S(1)} %bitcast.43), custom_call_target="tpu_custom_call" | custom-call | flops 905969664 | bytes 2392064 | tf_op jit(solution)/shard_map/pallas_call | solution.py:33
  8.6 2.6 %collective-permute-done.first_ref = bf16[16,2,32,128]{3,2,1,0:T(8,128)(2,1)S(1)} collective-permute-done((bf16[16,2,32,128]{3,2,1,0:T(8,128)(2,1)S(1)}, bf16[16,2,32,128]{3,2,1,0:T(8,128)(2,1)S(1)}, u32[]{:S(2)}, u32[]{:S(2)}) %collective-permute-start) | collective-permute-done | bytes 262176 | tf_op jit(solution)/shard_map/ppermute | solution.py:450
  11.2 1.1 %shard_map.111 = (bf16[16,8,32,128]{3,2,1,0:T(8,128)(2,1)}, f32[16,6,32,128]{3,2,1,0:T(8,128)S(1)}, bf16[6,32,128]{2,1,0:T(8,128)(2,1)S(1)}) custom-call(f32[16,6,32,128]{3,2,1,0:T(8,128)S(1)} %shard_map.109.near_ref, bf16[16,4,32,128]{3,2,1,0:T(8,128)(2,1)S(1)} %bitcast.39, ...), custom_call_target="tpu_custom_call", output_to_operand_aliasing={{1}: (0, {})} | custom-call | flops 201326592 | bytes 5595136 | tf_op jit(solution)/shard_map/pallas_call | solution.py:33
  12.3 1.7 %collective-permute-start.2 = (bf16[6,32,128]{2,1,0:T(8,128)(2,1)S(1)}, bf16[6,32,128]{2,1,0:T(8,128)(2,1)S(1)}, u32[]{:S(2)}, u32[]{:S(2)}) collective-permute-start(bf16[6,32,128]{2,1,0:T(8,128)(2,1)S(1)} %get-tuple-element.37), channel_id=1, source_target_pairs={{0,16},{16,0},{1,17},{17,1},{2,18},{18,2},{3,19},{19,3},{4,20},{20... | collective-permute-start | bytes 147464 | tf_op jit(solution)/shard_map/ppermute | solution.py:460
  14.4 2.0 %collective-permute-done.2.carry_ref = bf16[6,32,128]{2,1,0:T(8,128)(2,1)S(1)} collective-permute-done((bf16[6,32,128]{2,1,0:T(8,128)(2,1)S(1)}, bf16[6,32,128]{2,1,0:T(8,128)(2,1)S(1)}, u32[]{:S(2)}, u32[]{:S(2)}) %collective-permute-start.2) | collective-permute-done | bytes 49184 | tf_op jit(solution)/shard_map/ppermute | solution.py:460
  16.4 2.7 %shard_map.112 = (bf16[16,6,32,128]{3,2,1,0:T(8,128)(2,1)}, bf16[16,4,32,128]{3,2,1,0:T(8,128)(2,1)S(1)}, bf16[16,4,32,128]{3,2,1,0:T(8,128)(2,1)S(1)}, f32[1,128]{1,0:T(1,128)S(1)}) custom-call(f32[16,6,32,128]{3,2,1,0:T(8,128)S(1)} %get-tuple-element.36.local_ref, bf16[6,32,128]{2,1,0:T(8,128)(2,1)S(1)} %collective-permute-done.2.carry_ref, ...), custom_call_target="tpu_custom_call" | custom-call | flops 603979776 | bytes 4809728 | tf_op jit(solution)/shard_map/pallas_call | solution.py:33
  19.2 4.8 %collective-permute-start.3 = (bf16[16,2,32,128]{3,2,1,0:T(8,128)(2,1)S(1)}, bf16[16,2,32,128]{3,2,1,0:T(8,128)(2,1)S(1)}, u32[]{:S(2)}, u32[]{:S(2)}) collective-permute-start(bf16[16,2,32,128]{3,2,1,0:T(8,128)(2,1)S(1)} %get-tuple-element.68), channel_id=1, source_target_pairs={{0,4},{4,0},{8,12},{12,8},{1,5},{5,1},{9,13},{13,9},{2,6},{6,2},{1... | collective-permute-start | bytes 786440 | tf_op jit(solution)/shard_map/ppermute | solution.py:450
  25.0 1.7 %shard_map.113 = (f32[16,6,32,128]{3,2,1,0:T(8,128)S(1)}, bf16[16,4,32,128]{3,2,1,0:T(8,128)(2,1)}) custom-call(bf16[16,4,32,128]{3,2,1,0:T(8,128)(2,1)S(1)} %get-tuple-element.38.own_ref.grad_ref, bf16[384,384]{1,0:T(8,128)(2,1)S(1)} %bitcast.41, bf16[16,4,32,128]{3,2,1,0:T(8,128)(2,1)S(1)} %get-tuple-element.39.act_ref), custom_call_target="tpu_custom_call" | custom-call | flops 905969664 | bytes 3440640 | tf_op jit(solution)/shard_map/pallas_call | solution.py:33
  26.7 1.7 %collective-permute-done.3.first_ref = bf16[16,2,32,128]{3,2,1,0:T(8,128)(2,1)S(1)} collective-permute-done((bf16[16,2,32,128]{3,2,1,0:T(8,128)(2,1)S(1)}, bf16[16,2,32,128]{3,2,1,0:T(8,128)(2,1)S(1)}, u32[]{:S(2)}, u32[]{:S(2)}) %collective-permute-start.3) | collective-permute-done | bytes 262176 | tf_op jit(solution)/shard_map/ppermute | solution.py:450
  28.4 0.9 %shard_map.114 = (f32[16,6,32,128]{3,2,1,0:T(8,128)S(1)}, bf16[6,32,128]{2,1,0:T(8,128)(2,1)S(1)}) custom-call(f32[16,6,32,128]{3,2,1,0:T(8,128)S(1)} %get-tuple-element.41.near_ref, bf16[16,2,32,128]{3,2,1,0:T(8,128)(2,1)S(1)} %collective-permute-done.3.first_ref, ...), custom_call_target="tpu_custom_call", output_to_operand_aliasing={{0}: (0, {})} | custom-call | flops 201326592 | bytes 4022272 | tf_op jit(solution)/shard_map/pallas_call | solution.py:33
  29.3 1.6 %collective-permute-start.5 = (bf16[6,32,128]{2,1,0:T(8,128)(2,1)S(1)}, bf16[6,32,128]{2,1,0:T(8,128)(2,1)S(1)}, u32[]{:S(2)}, u32[]{:S(2)}) collective-permute-start(bf16[6,32,128]{2,1,0:T(8,128)(2,1)S(1)} %get-tuple-element.43), channel_id=1, source_target_pairs={{0,16},{16,0},{1,17},{17,1},{2,18},{18,2},{3,19},{19,3},{4,20},{20... | collective-permute-start | bytes 147464 | tf_op jit(solution)/shard_map/ppermute | solution.py:460
  30.9 1.0 %shard_map.115.other_ref = f32[1152,128]{1,0:T(8,128)S(1)} custom-call(bf16[16,6,32,128]{3,2,1,0:T(8,128)(2,1)S(1)} %copy-done.2, bf16[16,4,32,128]{3,2,1,0:T(8,128)(2,1)S(1)} %get-tuple-element.38.own_ref.grad_ref), custom_call_target="tpu_custom_call" | custom-call | flops 603979776 | bytes 1900544 | tf_op jit(solution)/shard_map/pallas_call | solution.py:33
  31.9 1.6 %collective-permute-done.5.back_ref = bf16[6,32,128]{2,1,0:T(8,128)(2,1)S(1)} collective-permute-done((bf16[6,32,128]{2,1,0:T(8,128)(2,1)S(1)}, bf16[6,32,128]{2,1,0:T(8,128)(2,1)S(1)}, u32[]{:S(2)}, u32[]{:S(2)}) %collective-permute-start.5) | collective-permute-done | bytes 49184 | tf_op jit(solution)/shard_map/ppermute | solution.py:460
  33.5 1.1 %shard_map.116 = (bf16[16,6,32,128]{3,2,1,0:T(8,128)(2,1)S(1)}, bf16[1184,128]{1,0:T(8,128)(2,1)S(1)}, f32[1184,128]{1,0:T(8,128)S(1)}) custom-call(f32[16,6,32,128]{3,2,1,0:T(8,128)S(1)} %get-tuple-element.42.local_ref, bf16[6,32,128]{2,1,0:T(8,128)(2,1)S(1)} %collective-permute-done.5.back_ref, f32[16,1,128]{2,1,0:T(1,128)S(1)} %get-tuple-element.69.reach_ref, ...), custom_call_target="tpu_custom_call" | custom-call | flops 603979776 | bytes 5808640 | tf_op jit(solution)/shard_map/pallas_call | solution.py:33
  34.7 1.5 %collective-permute-done.6 = bf16[1184,128]{1,0:T(8,128)(2,1)S(1)} collective-permute-done((bf16[1184,128]{1,0:T(8,128)(2,1)S(1)}, bf16[1184,128]{1,0:T(8,128)(2,1)S(1)}, u32[]{:S(2)}, u32[]{:S(2)}) %collective-permute-start.6) | collective-permute-done | bytes 303136 | tf_op jit(solution)/shard_map/ppermute | solution.py:498
  36.4 2.5 %collective-permute-start.9 = (bf16[296,128]{1,0:T(8,128)(2,1)S(1)}, bf16[296,128]{1,0:T(8,128)(2,1)S(1)}, u32[]{:S(2)}, u32[]{:S(2)}) collective-permute-start(bf16[296,128]{1,0:T(8,128)(2,1)S(1)} %get-tuple-element.53), channel_id=1, source_target_pairs={{0,18},{1,19},{2,16},{3,17},{4,22},{5,23},{6,20},{7,21},{8,26},{9,... | collective-permute-start | bytes 227336 | tf_op jit(solution)/shard_map/ppermute | solution.py:498
  40.0 1.8 %collective-permute-done.9 = bf16[296,128]{1,0:T(8,128)(2,1)S(1)} collective-permute-done((bf16[296,128]{1,0:T(8,128)(2,1)S(1)}, bf16[296,128]{1,0:T(8,128)(2,1)S(1)}, u32[]{:S(2)}, u32[]{:S(2)}) %collective-permute-start.9) | collective-permute-done | bytes 75808 | tf_op jit(solution)/shard_map/ppermute | solution.py:498
  41.8 1.6 %collective-permute-done.8 = bf16[296,128]{1,0:T(8,128)(2,1)S(1)} collective-permute-done((bf16[296,128]{1,0:T(8,128)(2,1)S(1)}, bf16[296,128]{1,0:T(8,128)(2,1)S(1)}, u32[]{:S(2)}, u32[]{:S(2)}) %collective-permute-start.8) | collective-permute-done | bytes 75808 | tf_op jit(solution)/shard_map/ppermute | solution.py:498
  43.9 2.7 %collective-permute-start.12 = (bf16[296,128]{1,0:T(8,128)(2,1)S(1)}, bf16[296,128]{1,0:T(8,128)(2,1)S(1)}, u32[]{:S(2)}, u32[]{:S(2)}) collective-permute-start(bf16[296,128]{1,0:T(8,128)(2,1)S(1)} %add_convert_fusion.1), channel_id=1, source_target_pairs={{0,12},{1,13},{2,14},{3,15},{4,8},{5,9},{6,10},{7,11},{8,4},{9,5},... | collective-permute-start | bytes 227336 | tf_op jit(solution)/shard_map/ppermute | solution.py:498
  46.6 2.8 %collective-permute-start.11 = (bf16[296,128]{1,0:T(8,128)(2,1)S(1)}, bf16[296,128]{1,0:T(8,128)(2,1)S(1)}, u32[]{:S(2)}, u32[]{:S(2)}) collective-permute-start(bf16[296,128]{1,0:T(8,128)(2,1)S(1)} %add_convert_fusion.1), channel_id=1, source_target_pairs={{0,8},{1,9},{2,10},{3,11},{4,12},{5,13},{6,14},{7,15},{8,0},{9,1},... | collective-permute-start | bytes 227336 | tf_op jit(solution)/shard_map/ppermute | solution.py:498
  50.2 4.3 %collective-permute-done.11 = bf16[296,128]{1,0:T(8,128)(2,1)S(1)} collective-permute-done((bf16[296,128]{1,0:T(8,128)(2,1)S(1)}, bf16[296,128]{1,0:T(8,128)(2,1)S(1)}, u32[]{:S(2)}, u32[]{:S(2)}) %collective-permute-start.11) | collective-permute-done | bytes 75808 | tf_op jit(solution)/shard_map/ppermute | solution.py:498
  54.6 1.6 %collective-permute-start.13 = (bf16[296,128]{1,0:T(8,128)(2,1)S(1)}, bf16[296,128]{1,0:T(8,128)(2,1)S(1)}, u32[]{:S(2)}, u32[]{:S(2)}) collective-permute-start(bf16[296,128]{1,0:T(8,128)(2,1)S(1)} %get-tuple-element.63), channel_id=1, source_target_pairs={{0,2},{1,3},{2,0},{3,1},{4,6},{5,7},{6,4},{7,5},{8,10},{9,11},{10,... | collective-permute-start | bytes 227336 | tf_op jit(solution)/shard_map/ppermute | solution.py:498
  56.8 1.4 %collective-permute-start.15 = (bf16[296,128]{1,0:T(8,128)(2,1)S(1)}, bf16[296,128]{1,0:T(8,128)(2,1)S(1)}, u32[]{:S(2)}, u32[]{:S(2)}) collective-permute-start(bf16[296,128]{1,0:T(8,128)(2,1)S(1)} %get-tuple-element.63), channel_id=1, source_target_pairs={{0,18},{1,19},{2,16},{3,17},{4,22},{5,23},{6,20},{7,21},{8,26},{9,... | collective-permute-start | bytes 227336 | tf_op jit(solution)/shard_map/ppermute | solution.py:498
  58.2 1.6 %collective-permute-done.13 = bf16[296,128]{1,0:T(8,128)(2,1)S(1)} collective-permute-done((bf16[296,128]{1,0:T(8,128)(2,1)S(1)}, bf16[296,128]{1,0:T(8,128)(2,1)S(1)}, u32[]{:S(2)}, u32[]{:S(2)}) %collective-permute-start.13) | collective-permute-done | bytes 75808 | tf_op jit(solution)/shard_map/ppermute | solution.py:498
  59.8 0.8 %collective-permute-done.14 = bf16[296,128]{1,0:T(8,128)(2,1)S(1)} collective-permute-done((bf16[296,128]{1,0:T(8,128)(2,1)S(1)}, bf16[296,128]{1,0:T(8,128)(2,1)S(1)}, u32[]{:S(2)}, u32[]{:S(2)}) %collective-permute-start.14) | collective-permute-done | bytes 75808 | tf_op jit(solution)/shard_map/ppermute | solution.py:498
  60.7 1.4 %collective-permute-done.15 = bf16[296,128]{1,0:T(8,128)(2,1)S(1)} collective-permute-done((bf16[296,128]{1,0:T(8,128)(2,1)S(1)}, bf16[296,128]{1,0:T(8,128)(2,1)S(1)}, u32[]{:S(2)}, u32[]{:S(2)}) %collective-permute-start.15) | collective-permute-done | bytes 75808 | tf_op jit(solution)/shard_map/ppermute | solution.py:498
  62.5 2.0 %shard_map.117 = bf16[16,4,32,128]{3,2,1,0:T(8,128)(2,1)} custom-call(bf16[16,6,32,128]{3,2,1,0:T(8,128)(2,1)S(1)} %get-tuple-element.47.adjoint_ref, bf16[16,4,32,128]{3,2,1,0:T(8,128)(2,1)S(1)} %get-tuple-element.38.own_ref.grad_ref, bf16[384,384]{1,0:T(8,128)(2,1)S(1)} %bitcast.45, f32[1,128]{1,0:T(1,128)S(1)} %bitcast.50), custom_call_target="tpu_custom_call" | custom-call | flops 603979776 | bytes 2130432 | tf_op jit(solution)/shard_map/pallas_call | solution.py:33
  64.6 0.9 %shard_map.118 = (f32[3,3,128,128]{3,2,1,0:T(8,128)}, f32[3,3,128,128]{3,2,1,0:T(8,128)}, f32[1,128]{1,0:T(1,128)}, f32[16,128]{1,0:T(8,128)}) custom-call(bf16[1184,128]{1,0:T(8,128)(2,1)S(1)} %constant_dynamic-update-slice_fusion.refs_0_), custom_call_target="tpu_custom_call" | custom-call | bytes 1491456 | tf_op jit(solution)/shard_map/pallas_call | solution.py:33
  65.4 0.9 %shard_map.119 = (f32[3,3,128,128]{3,2,1,0:T(8,128)}, f32[3,3,128,128]{3,2,1,0:T(8,128)}, f32[1,128]{1,0:T(1,128)}, f32[16,128]{1,0:T(8,128)}) custom-call(bf16[1184,128]{1,0:T(8,128)(2,1)S(1)} %collective-permute-done.16.refs_0_, ...), custom_call_target="tpu_custom_call", output_to_operand_aliasing={{0}: (1, {}), {1}: (2, {}), {2}: (3, {}), {3}: (4, {})} | custom-call | bytes 2679808 | tf_op jit(solution)/shard_map/pallas_call | solution.py:33
  (53 shorter events, 5.8 us)
Async XLA Ops:
  0.6 6.2 %copy-start = (bf16[1,16,4,32,128]{4,3,2,1,0:T(8,128)(2,1)S(1)}, bf16[1,16,4,32,128]{4,3,2,1,0:T(8,128)(2,1)}, u32[]{:S(2)}) copy-start(bf16[1,16,4,32,128]{4,3,2,1,0:T(8,128)(2,1)} %param.6) | copy-start | bytes 1572868
  1.8 9.4 %collective-permute-start = (bf16[16,2,32,128]{3,2,1,0:T(8,128)(2,1)S(1)}, bf16[16,2,32,128]{3,2,1,0:T(8,128)(2,1)S(1)}, u32[]{:S(2)}, u32[]{:S(2)}) collective-permute-start(bf16[16,2,32,128]{3,2,1,0:T(8,128)(2,1)S(1)} %get-tuple-element.34), channel_id=1, source_target_pairs={{0,4},{4,0},{8,12},{12,8},{1,5},{5,1},{9,13},{13,9},{2,6},{6,2},{1... | collective-permute-start | bytes 786440 | tf_op jit(solution)/shard_map/ppermute | solution.py:450
  4.9 6.3 %collective-permute-start.1 = (bf16[16,2,32,128]{3,2,1,0:T(8,128)(2,1)S(1)}, bf16[16,2,32,128]{3,2,1,0:T(8,128)(2,1)S(1)}, u32[]{:S(2)}, u32[]{:S(2)}) collective-permute-start(bf16[16,2,32,128]{3,2,1,0:T(8,128)(2,1)S(1)} %get-tuple-element.35), channel_id=1, source_target_pairs={{4,8},{8,4},{5,9},{9,5},{6,10},{10,6},{7,11},{11,7},{20,24},{24,20... | collective-permute-start | bytes 786440 | tf_op jit(solution)/shard_map/ppermute | solution.py:451
  6.8 1.7 %copy-start.7 = (f32[16,128]{1,0:T(8,128)S(1)}, f32[16,128]{1,0:T(8,128)}, u32[]{:S(2)}) copy-start(f32[16,128]{1,0:T(8,128)} %param.11) | copy-start | bytes 24580
  11.2 2.9 %copy-start.4 = (bf16[3,3,128,128]{3,2,1,0:T(8,128)(2,1)S(1)}, bf16[3,3,128,128]{3,2,1,0:T(8,128)(2,1)}, u32[]{:S(2)}) copy-start(bf16[3,3,128,128]{3,2,1,0:T(8,128)(2,1)} %param.9) | copy-start | bytes 884740
  11.2 5.2 %copy-start.3 = (f32[128]{0:T(128)S(1)}, f32[128]{0:T(128)}, u32[]{:S(2)}) copy-start(f32[128]{0:T(128)} %param.10) | copy-start | bytes 1540
  12.3 4.2 %collective-permute-start.2 = (bf16[6,32,128]{2,1,0:T(8,128)(2,1)S(1)}, bf16[6,32,128]{2,1,0:T(8,128)(2,1)S(1)}, u32[]{:S(2)}, u32[]{:S(2)}) collective-permute-start(bf16[6,32,128]{2,1,0:T(8,128)(2,1)S(1)} %get-tuple-element.37), channel_id=1, source_target_pairs={{0,16},{16,0},{1,17},{17,1},{2,18},{18,2},{3,19},{19,3},{4,20},{20... | collective-permute-start | bytes 147464 | tf_op jit(solution)/shard_map/ppermute | solution.py:460
  16.4 8.3 %copy-start.5 = (bf16[3,3,128,128]{3,2,1,0:T(8,128)(2,1)S(1)}, bf16[3,3,128,128]{3,2,1,0:T(8,128)(2,1)}, u32[]{:S(2)}) copy-start(bf16[3,3,128,128]{3,2,1,0:T(8,128)(2,1)} %param.9) | copy-start | bytes 884740
  19.2 9.2 %collective-permute-start.3 = (bf16[16,2,32,128]{3,2,1,0:T(8,128)(2,1)S(1)}, bf16[16,2,32,128]{3,2,1,0:T(8,128)(2,1)S(1)}, u32[]{:S(2)}, u32[]{:S(2)}) collective-permute-start(bf16[16,2,32,128]{3,2,1,0:T(8,128)(2,1)S(1)} %get-tuple-element.68), channel_id=1, source_target_pairs={{0,4},{4,0},{8,12},{12,8},{1,5},{5,1},{9,13},{13,9},{2,6},{6,2},{1... | collective-permute-start | bytes 786440 | tf_op jit(solution)/shard_map/ppermute | solution.py:450
  24.0 4.4 %collective-permute-start.4 = (bf16[16,2,32,128]{3,2,1,0:T(8,128)(2,1)S(1)}, bf16[16,2,32,128]{3,2,1,0:T(8,128)(2,1)S(1)}, u32[]{:S(2)}, u32[]{:S(2)}) collective-permute-start(bf16[16,2,32,128]{3,2,1,0:T(8,128)(2,1)S(1)} %get-tuple-element.67), channel_id=1, source_target_pairs={{4,8},{8,4},{5,9},{9,5},{6,10},{10,6},{7,11},{11,7},{20,24},{24,20... | collective-permute-start | bytes 786440 | tf_op jit(solution)/shard_map/ppermute | solution.py:451
  26.7 4.2 %copy-start.2 = (bf16[16,6,32,128]{3,2,1,0:T(8,128)(2,1)S(1)}, bf16[16,6,32,128]{3,2,1,0:T(8,128)(2,1)}, u32[]{:S(2)}) copy-start(bf16[16,6,32,128]{3,2,1,0:T(8,128)(2,1)} %get-tuple-element.45.state_ref) | copy-start | bytes 2359300
  29.3 4.2 %copy-start.1 = (bf16[16,8,32,128]{3,2,1,0:T(8,128)(2,1)S(1)}, bf16[16,8,32,128]{3,2,1,0:T(8,128)(2,1)}, u32[]{:S(2)}) copy-start(bf16[16,8,32,128]{3,2,1,0:T(8,128)(2,1)} %get-tuple-element.44.wide_ref) | copy-start | bytes 3145732
  29.3 4.2 %collective-permute-start.5 = (bf16[6,32,128]{2,1,0:T(8,128)(2,1)S(1)}, bf16[6,32,128]{2,1,0:T(8,128)(2,1)S(1)}, u32[]{:S(2)}, u32[]{:S(2)}) collective-permute-start(bf16[6,32,128]{2,1,0:T(8,128)(2,1)S(1)} %get-tuple-element.43), channel_id=1, source_target_pairs={{0,16},{16,0},{1,17},{17,1},{2,18},{18,2},{3,19},{19,3},{4,20},{20... | collective-permute-start | bytes 147464 | tf_op jit(solution)/shard_map/ppermute | solution.py:460
  34.6 1.7 %collective-permute-start.6 = (bf16[1184,128]{1,0:T(8,128)(2,1)S(1)}, bf16[1184,128]{1,0:T(8,128)(2,1)S(1)}, u32[]{:S(2)}, u32[]{:S(2)}) collective-permute-start(bf16[1184,128]{1,0:T(8,128)(2,1)S(1)} %get-tuple-element.49), channel_id=1, source_target_pairs={{0,1},{1,0},{2,3},{3,2},{4,5},{5,4},{6,7},{7,6},{8,9},{9,8},{10,11... | collective-permute-start | bytes 909320 | tf_op jit(solution)/shard_map/ppermute | solution.py:498
  36.3 25.8 %copy-start.6 = (bf16[3,3,128,128]{3,2,1,0:T(8,128)(2,1)S(1)}, bf16[3,3,128,128]{3,2,1,0:T(8,128)(2,1)}, u32[]{:S(2)}) copy-start(bf16[3,3,128,128]{3,2,1,0:T(8,128)(2,1)} %param.8) | copy-start | bytes 884740
  36.4 5.4 %collective-permute-start.9 = (bf16[296,128]{1,0:T(8,128)(2,1)S(1)}, bf16[296,128]{1,0:T(8,128)(2,1)S(1)}, u32[]{:S(2)}, u32[]{:S(2)}) collective-permute-start(bf16[296,128]{1,0:T(8,128)(2,1)S(1)} %get-tuple-element.53), channel_id=1, source_target_pairs={{0,18},{1,19},{2,16},{3,17},{4,22},{5,23},{6,20},{7,21},{8,26},{9,... | collective-permute-start | bytes 227336 | tf_op jit(solution)/shard_map/ppermute | solution.py:498
  39.0 4.4 %collective-permute-start.8 = (bf16[296,128]{1,0:T(8,128)(2,1)S(1)}, bf16[296,128]{1,0:T(8,128)(2,1)S(1)}, u32[]{:S(2)}, u32[]{:S(2)}) collective-permute-start(bf16[296,128]{1,0:T(8,128)(2,1)S(1)} %get-tuple-element.52), channel_id=1, source_target_pairs={{0,16},{1,17},{2,18},{3,19},{4,20},{5,21},{6,22},{7,23},{8,24},{9,... | collective-permute-start | bytes 227336 | tf_op jit(solution)/shard_map/ppermute | solution.py:498
  39.5 4.4 %collective-permute-start.7 = (bf16[296,128]{1,0:T(8,128)(2,1)S(1)}, bf16[296,128]{1,0:T(8,128)(2,1)S(1)}, u32[]{:S(2)}, u32[]{:S(2)}) collective-permute-start(bf16[296,128]{1,0:T(8,128)(2,1)S(1)} %get-tuple-element.51), channel_id=1, source_target_pairs={{0,2},{1,3},{2,0},{3,1},{4,6},{5,7},{6,4},{7,5},{8,10},{9,11},{10,... | collective-permute-start | bytes 227336 | tf_op jit(solution)/shard_map/ppermute | solution.py:498
  43.9 6.3 %collective-permute-start.12 = (bf16[296,128]{1,0:T(8,128)(2,1)S(1)}, bf16[296,128]{1,0:T(8,128)(2,1)S(1)}, u32[]{:S(2)}, u32[]{:S(2)}) collective-permute-start(bf16[296,128]{1,0:T(8,128)(2,1)S(1)} %add_convert_fusion.1), channel_id=1, source_target_pairs={{0,12},{1,13},{2,14},{3,15},{4,8},{5,9},{6,10},{7,11},{8,4},{9,5},... | collective-permute-start | bytes 227336 | tf_op jit(solution)/shard_map/ppermute | solution.py:498
  46.6 7.9 %collective-permute-start.11 = (bf16[296,128]{1,0:T(8,128)(2,1)S(1)}, bf16[296,128]{1,0:T(8,128)(2,1)S(1)}, u32[]{:S(2)}, u32[]{:S(2)}) collective-permute-start(bf16[296,128]{1,0:T(8,128)(2,1)S(1)} %add_convert_fusion.1), channel_id=1, source_target_pairs={{0,8},{1,9},{2,10},{3,11},{4,12},{5,13},{6,14},{7,15},{8,0},{9,1},... | collective-permute-start | bytes 227336 | tf_op jit(solution)/shard_map/ppermute | solution.py:498
  49.3 5.2 %collective-permute-start.10 = (bf16[296,128]{1,0:T(8,128)(2,1)S(1)}, bf16[296,128]{1,0:T(8,128)(2,1)S(1)}, u32[]{:S(2)}, u32[]{:S(2)}) collective-permute-start(bf16[296,128]{1,0:T(8,128)(2,1)S(1)} %add_convert_fusion.1), channel_id=1, source_target_pairs={{0,4},{1,5},{2,6},{3,7},{4,0},{5,1},{6,2},{7,3},{8,12},{9,13},{10,... | collective-permute-start | bytes 227336 | tf_op jit(solution)/shard_map/ppermute | solution.py:498
  54.6 5.2 %collective-permute-start.13 = (bf16[296,128]{1,0:T(8,128)(2,1)S(1)}, bf16[296,128]{1,0:T(8,128)(2,1)S(1)}, u32[]{:S(2)}, u32[]{:S(2)}) collective-permute-start(bf16[296,128]{1,0:T(8,128)(2,1)S(1)} %get-tuple-element.63), channel_id=1, source_target_pairs={{0,2},{1,3},{2,0},{3,1},{4,6},{5,7},{6,4},{7,5},{8,10},{9,11},{10,... | collective-permute-start | bytes 227336 | tf_op jit(solution)/shard_map/ppermute | solution.py:498
  56.3 4.4 %collective-permute-start.14 = (bf16[296,128]{1,0:T(8,128)(2,1)S(1)}, bf16[296,128]{1,0:T(8,128)(2,1)S(1)}, u32[]{:S(2)}, u32[]{:S(2)}) collective-permute-start(bf16[296,128]{1,0:T(8,128)(2,1)S(1)} %get-tuple-element.63), channel_id=1, source_target_pairs={{0,16},{1,17},{2,18},{3,19},{4,20},{5,21},{6,22},{7,23},{8,24},{9,... | collective-permute-start | bytes 227336 | tf_op jit(solution)/shard_map/ppermute | solution.py:498
  56.8 5.3 %collective-permute-start.15 = (bf16[296,128]{1,0:T(8,128)(2,1)S(1)}, bf16[296,128]{1,0:T(8,128)(2,1)S(1)}, u32[]{:S(2)}, u32[]{:S(2)}) collective-permute-start(bf16[296,128]{1,0:T(8,128)(2,1)S(1)} %get-tuple-element.63), channel_id=1, source_target_pairs={{0,18},{1,19},{2,16},{3,17},{4,22},{5,23},{6,20},{7,21},{8,26},{9,... | collective-permute-start | bytes 227336 | tf_op jit(solution)/shard_map/ppermute | solution.py:498
  62.1 3.4 %collective-permute-start.16 = (bf16[1184,128]{1,0:T(8,128)(2,1)S(1)}, bf16[1184,128]{1,0:T(8,128)(2,1)S(1)}, u32[]{:S(2)}, u32[]{:S(2)}) collective-permute-start(bf16[1184,128]{1,0:T(8,128)(2,1)S(1)} %constant_dynamic-update-slice_fusion.refs_0_), channel_id=1, source_target_pairs={{0,1},{1,0},{2,3},{3,2},{4,5},{5,4},{6,7},{7,6},{8,9},{9,8},{10,11... | collective-permute-start | bytes 909320 | tf_op jit(solution)/shard_map/ppermute | solution.py:498
